TPU v7x, 512 devices: a whole 4x8x8 slice. The times are simulated.
512 devices in a mesh: dp: 64 (over x, y, core), tensor: 4 (over z_hi), replica: 2 (over z_lo).
Axes of the slice: x: 4, y: 8, z: 8 (z_hi: 4, z_lo: 2; z = z_hi * 2 + z_lo), core: 2. Of those that a mesh axis runs over, the one named last changes fastest.
Arguments:
- features: bfloat16 [128, 1536, 1024], P(('dp', 'replica'), 'tensor'), may hold values from -600 to 600
- cotangents: bfloat16 [128, 1536, 2, 1024], P(('dp', 'replica'), None, None, 'tensor'), may hold values from -150 to 150
- moment_one: float32 [2, 1024, 1024], P(None, ('dp', 'replica'), 'tensor'), may hold values from -6 to 6
- moment_two: float32 [2, 1024, 1024], P(None, ('dp', 'replica'), 'tensor'), may hold values from 0.01 to 4
- master: float32 [2, 1024, 1024], P(None, ('dp', 'replica'), 'tensor'), may hold values from -6 to 6
- average: float32 [128, 4, 4, 1024], P(('dp', 'replica'), 'tensor'), may hold values from -6 to 6
Outputs:
- weights: bfloat16 [2, 1024, 1024], P(None, None, 'tensor')
- new_first: float32 [2, 1024, 1024], P(None, ('dp', 'replica'), 'tensor')
- new_second: float32 [2, 1024, 1024], P(None, ('dp', 'replica'), 'tensor')
- new_master: float32 [2, 1024, 1024], P(None, ('dp', 'replica'), 'tensor')
- new_average: float32 [128, 4, 4, 1024], P(('dp', 'replica'), 'tensor')
All inputs are finite; a program needn't handle non-finite values.
Results may differ from a plain program's by a relative error of at most 0.0055.
Values may be sent and summed in bfloat16 or wider, within the bound.
No kernel may reach another device: no remote copies, remote signals or barrier semaphores. Data moves between devices by JAX's collectives and lax.ppermute only.
A program may use at most 64 MiB of HBM per device.

v0:
```python
import jax
import jax.numpy as jnp
from jax import lax
from jax.sharding import PartitionSpec as P

STEP = 100


beta_one = 0.9
beta_two = 0.95
learn_rate = 0.05
decay_rate = 0.1
adam_eps = 1e-08
average_keep = 0.9


def shards(features, cotangents, moment_one, moment_two, master, average):
    col_width = cotangents.shape[3]
    tokens_all = lax.all_gather(features, "tensor", axis=1, tiled=True)[0]
    dim_model = tokens_all.shape[1]
    outgrad = cotangents[0].reshape(cotangents.shape[1], 2 * col_width)
    groups = lax.axis_size("dp") * lax.axis_size("replica")
    product = lax.dot_general(
        tokens_all, outgrad, (((0,), (0,)), ((), ())), preferred_element_type=jnp.float32
    )
    grad_piece = lax.psum_scatter(
        product.reshape(dim_model // groups * lax.axis_size(("dp", "replica")), 2, col_width),
        ("dp", "replica"),
        scatter_dimension=0,
        tiled=True,
    )
    gradient = jnp.transpose(grad_piece, (1, 0, 2))
    square_total = lax.psum(jnp.sum(gradient * gradient), ("dp", "tensor", "replica"))
    count_all = 2.0 * dim_model * dim_model
    clip_factor = 1.0 / jnp.sqrt(square_total / count_all + 1e-06)
    scaled = clip_factor * gradient
    new_first = beta_one * moment_one + (1.0 - beta_one) * scaled
    new_second = beta_two * moment_two + (1.0 - beta_two) * (scaled * scaled)
    fix_one = 1.0 - beta_one**STEP
    fix_two = 1.0 - beta_two**STEP
    direction = new_first / fix_one / (jnp.sqrt(new_second / fix_two) + adam_eps)
    new_master = master - learn_rate * (direction + decay_rate * master)
    weights = lax.all_gather(new_master.astype(jnp.bfloat16), ("dp", "replica"), axis=1, tiled=True)
    flat_rows = new_master.reshape(2 * new_master.shape[1], col_width)
    row_flat = lax.all_to_all(flat_rows, "tensor", split_axis=0, concat_axis=1, tiled=True)
    new_average = average_keep * average + (1.0 - average_keep) * row_flat.reshape(average.shape)
    return (weights, new_first, new_second, new_master, new_average)


def solution(mesh):
    placed = (
        P(("dp", "replica"), "tensor", None),
        P(("dp", "replica"), None, None, "tensor"),
        P(None, ("dp", "replica"), "tensor"),
        P(None, ("dp", "replica"), "tensor"),
        P(None, ("dp", "replica"), "tensor"),
        P(("dp", "replica"), "tensor", None, None),
    )
    return jax.shard_map(
        shards,
        mesh=mesh,
        in_specs=placed,
        out_specs=(
            P(None, None, "tensor"),
            P(None, ("dp", "replica"), "tensor"),
            P(None, ("dp", "replica"), "tensor"),
            P(None, ("dp", "replica"), "tensor"),
            P(("dp", "replica"), "tensor", None, None),
        ),
        check_vma=False,
    )
```

profile of v0, /device:TPU:1, one launch (start us, length us, event | category | flops | bytes accessed | tf_op | source)
XLA Modules:
  0.0 1036.2 jit_solution(7877374615193380906)
XLA Ops:
  7.2 0.0 copy-start
  7.2 0.0 all-gather.3.cloned.1.call-start
  7.2 2.4 copy.11
  9.6 0.0 all-gather.3.cloned.1.call-update
  9.6 0.0 reduce-scatter.2.cloned.1.call-start
  9.7 0.0 copy-done
  9.7 0.3 copy.14
  10.0 0.7 copy.12
  10.8 77.6 %all-gather.3.cloned.1.call-done = bf16[1,1536,1024]{1,2,0:T(8,128)(2,1)} async-done(((bf16[1,384,1024]{1,2,0:T(8,128)(2,1)}), bf16[1,1536,1024]{1,2,0:T(8,128)(2,1)}) %all-gather.3.cloned.1.call-update) | async-done | bytes 3145744 | tf_op jit(solution)/shard_map/all_gather | solution.py:19
  88.3 5.1 fusion
  93.4 0.0 copy-start.2
  93.4 0.0 copy-start.3
  93.4 0.0 copy-start.4
  93.4 0.0 copy-start.5
  93.4 0.0 reduce-scatter.2.cloned.1.call-update
  93.4 0.0 all-gather.5.cloned.1.call-start
  93.5 563.7 %reduce-scatter.2.cloned.1.call-done = f32[8,2,256]{2,0,1:T(8,128)} async-done(((f32[1024,2,256]{2,0,1:T(8,128)}), f32[8,2,256]{2,0,1:T(8,128)}) %reduce-scatter.2.cloned.1.call-update) | async-done | bytes 16400 | tf_op jit(solution)/shard_map/reduce_scatter | solution.py:26
  657.1 1.3 multiply_reduce_fusion
  658.5 98.3 %psum.7 = f32[]{:T(128)} all-reduce(f32[]{:T(128)} %multiply_reduce_fusion), channel_id=1, replica_groups=mesh['dp'=64,'tensor'=4,'replica'=2] {'dp','tensor','replica'}, use_global_device_ids=true, to_apply=%region_2.0 | all-reduce | flops 1 | bytes 8 | tf_op jit(solution)/shard_map/psum | solution.py:33
  757.5 0.0 copy-done.2
  757.5 0.0 copy-done.3
  757.5 0.0 copy-done.4
  757.5 1.3 fusion.2
  758.8 0.0 copy-start.1
  758.8 0.0 all-gather.5.cloned.1.call-update
  758.9 10.9 %all_to_all.13 = f32[4,4,256]{2,1,0:T(4,128)S(1)} all-to-all(f32[4,4,256]{2,1,0:T(4,128)S(1)} %all_to_all.10), channel_id=1, replica_groups=mesh['dp'=64,'tensor'=4,'replica'=2] {'tensor'}, dimensions={0} | all-to-all | bytes 32768 | tf_op jit(solution)/shard_map/all_to_all | solution.py:45
  769.8 0.0 copy-done.5
  769.8 0.6 multiply_add_fusion
  770.4 257.0 %all-gather.5.cloned.1.call-done = bf16[2,1024,256]{2,1,0:T(8,128)(2,1)} async-done(((bf16[2,8,256]{2,1,0:T(8,128)(2,1)}), bf16[2,1024,256]{2,1,0:T(8,128)(2,1)}) %all-gather.5.cloned.1.call-update) | async-done | bytes 1048592 | tf_op jit(solution)/shard_map/all_gather | solution.py:43
  1027.4 2.3 copy.16
  1029.7 0.0 copy-done.1
  (2 shorter events, 0.0 us)
Async XLA Ops:
  7.2 2.5 copy-start
  7.2 81.1 %all-gather.3.cloned.1.call-start = ((), (), s32[]{:S(2)}) async-start(), calls=%async_computation.2 | async-start | bytes 3932160 | tf_op jit(solution)/shard_map/all_gather | solution.py:19
  9.6 647.5 %reduce-scatter.2.cloned.1.call-start = ((), (), s32[]{:S(2)}) async-start(), calls=%async_computation.3 | async-start | bytes 2113536 | tf_op jit(solution)/shard_map/reduce_scatter | solution.py:26
  93.4 664.1 %copy-start.2 = (f32[2,8,256]{2,1,0:T(8,128)S(1)}, f32[2,8,256]{2,1,0:T(8,128)}, u32[]{:S(2)}) copy-start(f32[2,8,256]{2,1,0:T(8,128)} %param.10) | copy-start | bytes 49156
  93.4 664.1 %copy-start.3 = (f32[2,8,256]{2,1,0:T(8,128)S(1)}, f32[2,8,256]{2,1,0:T(8,128)}, u32[]{:S(2)}) copy-start(f32[2,8,256]{2,1,0:T(8,128)} %param.8) | copy-start | bytes 49156
  93.4 664.1 %copy-start.4 = (f32[2,8,256]{2,1,0:T(8,128)S(1)}, f32[2,8,256]{2,1,0:T(8,128)}, u32[]{:S(2)}) copy-start(f32[2,8,256]{2,1,0:T(8,128)} %param.9) | copy-start | bytes 49156
  93.4 676.4 %copy-start.5 = (f32[1,1,4,1024]{3,2,1,0:T(4,128)S(1)}, f32[1,1,4,1024]{3,2,1,0:T(4,128)}, u32[]{:S(2)}) copy-start(f32[1,1,4,1024]{3,2,1,0:T(4,128)} %param.11) | copy-start | bytes 49156
  93.4 934.0 %all-gather.5.cloned.1.call-start = ((), (), s32[]{:S(2)}) async-start(), calls=%async_computation.4 | async-start | bytes 1056768 | tf_op jit(solution)/shard_map/all_gather | solution.py:43
  758.8 270.8 %copy-start.1 = (f32[2,8,256]{2,1,0:T(8,128)}, f32[2,8,256]{2,1,0:T(8,128)S(1)}, u32[]{:S(2)}) copy-start(f32[2,8,256]{2,1,0:T(8,128)S(1)} %get-tuple-element.17) | copy-start | bytes 49156
Sparse Core Ops, SparseCore 0:
  10.7 77.5 all-gather.2
  93.5 563.5 reduce-scatter.1
  759.0 268.3 all-gather.4
where the time goes:
time: 1040 us
  waiting for transfers between devices  898 us (86%)
  blocking collectives  109 us (10%)
  between operations  14.5 us (1%)
    reduce_scatter x1, waiting for transfers between devices, shards(): lax.psum_scatter(product.reshape(dim_model // groups * lax.axis_size(('dp...  564 us
    all_gather x1, waiting for transfers between devices, shards(): lax.all_gather(new_master.astype(jnp.bfloat16), ('dp', 'replica'), axis=1...  257 us
    psum x1, blocking collectives, shards(): lax.psum(jnp.sum(gradient * gradient), ('dp', 'tensor', 'replica'))  98.3 us
    all_gather x1, waiting for transfers between devices, shards(): tokens_all = lax.all_gather(features, 'tensor', axis=1, tiled=True)[0]  77.6 us
  transfers between devices with their start and end apart: 3, of which 3 were waited for; matrix products, arithmetic and copies ran while one was open for 0% of the time, Pallas kernels for 0%

commit v1 on v0

v1 whole, which is shorter than its diff:
```python
import jax
import jax.numpy as jnp
from jax import lax
from jax.sharding import Mesh, PartitionSpec as P

STEP = 100


beta_one = 0.9
beta_two = 0.95
learn_rate = 0.05
decay_rate = 0.1
adam_eps = 1e-08
average_keep = 0.9

XYR = ("x", "y", "replica")
SWAP = ((0, 1), (1, 0))


def shards(features, cotangents, moment_one, moment_two, master, average):
    f32, bf16 = jnp.float32, jnp.bfloat16
    col_width = cotangents.shape[3]
    rows = moment_one.shape[1]
    nx, ny, nr = (lax.axis_size(name) for name in XYR)
    peers = nx * ny * nr
    core = lax.axis_index("core")

    tokens_all = lax.all_gather(features, "tensor", axis=1, tiled=True)[0]
    dim_model = tokens_all.shape[1]
    outgrad = cotangents[0].reshape(cotangents.shape[1], 2 * col_width)
    product = lax.dot_general(
        tokens_all, outgrad, (((0,), (0,)), ((), ())), preferred_element_type=f32
    )
    pieces = product.reshape(nx * ny, 2, nr, rows, 2 * col_width)
    keep = lax.dynamic_index_in_dim(pieces, core, axis=1, keepdims=False)
    give = lax.dynamic_index_in_dim(pieces, 1 - core, axis=1, keepdims=False)
    got = lax.ppermute(give.astype(bf16), "core", SWAP)
    half = (keep + got.astype(f32)).astype(bf16).reshape(peers, rows, 2 * col_width)
    terms = lax.all_to_all(half, XYR, split_axis=0, concat_axis=0, tiled=True)
    grad_piece = jnp.sum(terms.astype(f32), axis=0).reshape(rows, 2, col_width)
    gradient = jnp.transpose(grad_piece, (1, 0, 2))

    square_total = jnp.sum(gradient * gradient)
    for names in ("core", "x", "y", ("tensor", "replica")):
        square_total = lax.psum(square_total, names)
    count_all = 2.0 * dim_model * dim_model
    clip_factor = 1.0 / jnp.sqrt(square_total / count_all + 1e-06)
    scaled = clip_factor * gradient
    new_first = beta_one * moment_one + (1.0 - beta_one) * scaled
    new_second = beta_two * moment_two + (1.0 - beta_two) * (scaled * scaled)
    fix_one = 1.0 - beta_one**STEP
    fix_two = 1.0 - beta_two**STEP
    direction = new_first / fix_one / (jnp.sqrt(new_second / fix_two) + adam_eps)
    new_master = master - learn_rate * (direction + decay_rate * master)

    mine = new_master.astype(bf16)
    spread = jnp.broadcast_to(mine[None], (peers,) + mine.shape)
    column = lax.all_to_all(spread, XYR, split_axis=0, concat_axis=0, tiled=True)
    other = lax.ppermute(column, "core", SWAP)
    even = jnp.where(core == 0, column, other)
    odd = jnp.where(core == 0, other, column)
    both = jnp.stack([even, odd]).reshape(2, nx * ny, nr, 2, rows, col_width)
    weights = jnp.transpose(both, (3, 1, 0, 2, 4, 5)).reshape(2, dim_model, col_width)

    flat_rows = new_master.reshape(2 * rows, col_width)
    row_flat = lax.all_to_all(flat_rows, "tensor", split_axis=0, concat_axis=1, tiled=True)
    new_average = average_keep * average + (1.0 - average_keep) * row_flat.reshape(average.shape)
    return (weights, new_first, new_second, new_master, new_average)


def solution(mesh):
    shape = dict(zip(mesh.axis_names, mesh.devices.shape))
    nx, ny = 4, shape["dp"] // 8
    fine = Mesh(
        mesh.devices.reshape(nx, ny, 2, shape["tensor"], shape["replica"]),
        ("x", "y", "core", "tensor", "replica"),
    )
    groups = ("x", "y", "core", "replica")
    state = P(None, groups, "tensor")
    placed = (
        P(groups, "tensor", None),
        P(groups, None, None, "tensor"),
        state,
        state,
        state,
        P(groups, "tensor", None, None),
    )
    return jax.shard_map(
        shards,
        mesh=fine,
        in_specs=placed,
        out_specs=(P(None, None, "tensor"), state, state, state, P(groups, "tensor", None, None)),
        check_vma=False,
    )
```

time: 1040 us -> 220 us (0.21)
  waiting for transfers between devices: 898 us -> 84.9 us
  blocking collectives: 109 us -> 81.8 us
  starting transfers between devices: 0.12 us -> 20.9 us
    reduce_scatter x1 -> x0, waiting for transfers between devices: 564 us -> none  [shards(): lax.psum_scatter(product.reshape(dim_model // groups * lax.axis_size(('dp...]
    all_gather x1 -> x0, waiting for transfers between devices: 257 us -> none  [shards(): lax.all_gather(new_master.astype(jnp.bfloat16), ('dp', 'replica'), axis=1...]
    psum x1 -> x4, blocking collectives: 98.3 us -> 38.4 us  [shards(): square_total = lax.psum(square_total, names)]
    all_to_all x1 -> x2, blocking collectives: 10.9 us -> 43.4 us  [the longest x1 25.9 us: shards(): terms = lax.all_to_all(half, XYR, split_axis=0, concat_axis=0, tiled=True)]
    ppermute x0 -> x2, starting transfers between devices: none -> 15.9 us  [the longest x1 13.1 us: shards(): other = lax.ppermute(column, 'core', SWAP)]
  transfers between devices with their start and end apart: 3 -> 4, of which waited for: 3 -> 3; matrix products, arithmetic and copies ran while one was open for 0% -> 2% of each run, Pallas kernels for 0% -> 0%
where the time goes in v1:
time: 220 us; the launch traced here: 219 us
  waiting for transfers between devices  84.9 us (39%)
  blocking collectives  81.8 us (37%)
  starting transfers between devices  20.9 us (10%)
  between operations  14.9 us (7%)
  local copies, waits for them, and re-layouts  10.1 us (5%)
  other arithmetic  3.53 us (2%)
  matrix products  3.19 us (1%)
    all_gather x1, waiting for transfers between devices, shards(): tokens_all = lax.all_gather(features, 'tensor', axis=1, tiled=True)[0]  76.1 us
    psum x4, blocking collectives, shards(): square_total = lax.psum(square_total, names)  38.4 us
    all_to_all x1, blocking collectives, shards(): terms = lax.all_to_all(half, XYR, split_axis=0, concat_axis=0, tiled=True)  25.9 us
    all_to_all x1, blocking collectives, shards(): lax.all_to_all(spread, XYR, split_axis=0, concat_axis=0, tiled=True)  17.5 us
    ppermute x1, starting transfers between devices, shards(): other = lax.ppermute(column, 'core', SWAP)  13.1 us
    all_to_all x1, waiting for transfers between devices, shards(): lax.all_to_all(flat_rows, 'tensor', split_axis=0, concat_axis=1, tiled=True)  6.63 us
    all_to_all x1, starting transfers between devices, shards(): lax.all_to_all(flat_rows, 'tensor', split_axis=0, concat_axis=1, tiled=True)  4.95 us
  transfers between devices with their start and end apart: 4, of which 3 were waited for; matrix products, arithmetic and copies ran while one was open for 2% of the time, Pallas kernels for 0%

profile of v1, /device:TPU:1, one launch (start us, length us, event | category | flops | bytes accessed | tf_op | source)
XLA Modules:
  0.0 219.2 jit_solution(5503771907246698766)
XLA Ops:
  7.2 0.0 all-gather.2.cloned.1.call-start
  7.2 0.7 all-gather.2.cloned.1.call-update
  7.9 3.7 %reshape.57 = bf16[1536,512,1,1,1]{1,0,2,3,4:T(8,128)(2,1)} reshape(bf16[1,1536,2,256]{3,2,1,0:T(2,128)(2,1)} %param.7) | data formatting | bytes 3145728 | tf_op jit(solution)/shard_map/reshape;squeeze | solution.py:30
  11.6 76.1 %all-gather.2.cloned.1.call-done = bf16[1,1536,1024]{2,1,0:T(8,128)(2,1)} async-done(((bf16[1,384,1024]{2,1,0:T(8,128)(2,1)}), bf16[1,1536,1024]{2,1,0:T(8,128)(2,1)}) %all-gather.2.cloned.1.call-update) | async-done | bytes 3145744 | tf_op jit(solution)/shard_map/all_gather | solution.py:28
  87.7 3.2 %copy.15 = bf16[1024,1536]{1,0:T(8,128)(2,1)S(1)} copy(bf16[1024,1536]{0,1:T(8,128)(2,1)} %bitcast.29) | data formatting | bytes 6291456 | tf_op jit(solution)/shard_map/dot_general | solution.py:31
  90.9 3.2 %fusion = f32[32,2,2,8,512]{4,3,2,1,0:T(8,128)S(1)} fusion(bf16[32,2,2,8,1536]{4,3,2,1,0:T(8,128)(2,1)S(1)} %bitcast.30, bf16[1536,512,1,1,1]{1,0,2,3,4:T(8,128)(2,1)} %reshape.57), kind=kOutput, calls=%fused_computation | convolution fusion | flops 1610612736 | bytes 6815744 | tf_op jit(solution)/shard_map/dot_general | solution.py:31
  94.1 0.0 copy-start
  94.1 1.3 copy-done
  95.4 0.1 fusion.3
  95.5 0.0 copy-start.2
  95.5 0.0 copy-start.3
  95.5 0.0 copy-start.4
  95.6 2.8 %collective-permute-start = (bf16[32,2,8,512]{3,2,1,0:T(8,128)(2,1)S(1)}, bf16[32,2,8,512]{3,2,1,0:T(8,128)(2,1)S(1)}, u32[]{:S(2)}, u32[]{:S(2)}) collective-permute-start(bf16[32,2,8,512]{3,2,1,0:T(8,128)(2,1)S(1)} %fusion.3), channel_id=1, source_target_pairs={{0,8},{8,0},{1,9},{9,1},{2,10},{10,2},{3,11},{11,3},{4,12},{12,4},... | collective-permute-start | bytes 1572872 | tf_op jit(solution)/shard_map/ppermute | solution.py:37
  98.3 1.5 collective-permute-done
  99.8 1.4 fusion.2
  101.2 0.0 copy-start.5
  101.3 25.9 %all_to_all.23 = bf16[64,8,512]{2,1,0:T(8,128)(2,1)S(1)} all-to-all(bf16[64,8,512]{2,1,0:T(8,128)(2,1)S(1)} %bitcast.31), channel_id=1, replica_groups=mesh['x'=4,'y'=8,'core'=2,'tensor'=4,'replica'=2] {'x','y','replica'}, dimensions={0} | all-to-all | bytes 1048576 | tf_op jit(solution)/shard_map/all_to_all | solution.py:39
  127.2 0.1 convert_reduce_fusion
  127.3 0.6 multiply_reduce_fusion
  127.9 5.6 %psum.28 = f32[]{:T(128)} all-reduce(f32[]{:T(128)} %multiply_reduce_fusion), channel_id=1, replica_groups=mesh['x'=4,'y'=8,'core'=2,'tensor'=4,'replica'=2] {'core'}, use_global_device_ids=true, to_apply=%region_2.3 | all-reduce | flops 1 | bytes 8 | tf_op jit(solution)/shard_map/psum | solution.py:45
  133.4 7.8 %psum.29 = f32[]{:T(128)} all-reduce(f32[]{:T(128)} %psum.28), channel_id=1, replica_groups=mesh['x'=4,'y'=8,'core'=2,'tensor'=4,'replica'=2] {'x'}, use_global_device_ids=true, to_apply=%region_3.4 | all-reduce | flops 1 | bytes 8 | tf_op jit(solution)/shard_map/psum | solution.py:45
  141.3 12.5 %psum.30 = f32[]{:T(128)} all-reduce(f32[]{:T(128)} %psum.29), channel_id=1, replica_groups=mesh['x'=4,'y'=8,'core'=2,'tensor'=4,'replica'=2] {'y'}, use_global_device_ids=true, to_apply=%region_4.5 | all-reduce | flops 1 | bytes 8 | tf_op jit(solution)/shard_map/psum | solution.py:45
  153.8 12.5 %psum.31 = f32[]{:T(128)} all-reduce(f32[]{:T(128)} %psum.30), channel_id=1, replica_groups=mesh['x'=4,'y'=8,'core'=2,'tensor'=4,'replica'=2] {'tensor','replica'}, use_global_device_ids=true, to_apply=%region_5.6 | all-reduce | flops 1 | bytes 8 | tf_op jit(solution)/shard_map/psum | solution.py:45
  167.0 0.0 copy-done.2
  167.0 0.0 copy-done.3
  167.0 0.0 copy-done.4
  167.0 0.6 fusion.4
  167.6 0.0 copy-start.1
  167.7 17.5 %all_to_all.24 = bf16[64,2,8,256]{3,2,1,0:T(8,128)(2,1)S(1)} all-to-all(bf16[64,2,8,256]{3,2,1,0:T(8,128)(2,1)S(1)} %broadcast_in_dim.2), channel_id=1, replica_groups=mesh['x'=4,'y'=8,'core'=2,'tensor'=4,'replica'=2] {'x','y','replica'}, dimensions={0} | all-to-all | bytes 1048576 | tf_op jit(solution)/shard_map/all_to_all | solution.py:58
  185.2 13.1 %collective-permute-start.1 = (bf16[64,2,8,256]{3,2,1,0:T(8,128)(2,1)S(1)}, bf16[64,2,8,256]{3,2,1,0:T(8,128)(2,1)S(1)}, u32[]{:S(2)}, u32[]{:S(2)}) collective-permute-start(bf16[64,2,8,256]{3,2,1,0:T(8,128)(2,1)S(1)} %all_to_all.24), channel_id=1, source_target_pairs={{0,8},{8,0},{1,9},{9,1},{2,10},{10,2},{3,11},{11,3},{4,12},{12,4},... | collective-permute-start | bytes 1572872 | tf_op jit(solution)/shard_map/ppermute | solution.py:59
  198.3 0.6 all_to_all.18
  198.9 5.0 %all-to-all-start.2 = ((f32[4,4,256]{2,1,0:T(4,128)}), f32[4,4,256]{2,1,0:T(4,128)S(1)}, u32[]{:S(2)}, u32[]{:S(2)}) async-start(f32[4,4,256]{2,1,0:T(4,128)} %all_to_all.18), calls=%async_computation.2 | async-start | bytes 32768 | tf_op jit(solution)/shard_map/all_to_all | solution.py:66
  203.9 6.6 %all-to-all-done.2 = f32[4,4,256]{2,1,0:T(4,128)S(1)} async-done(((f32[4,4,256]{2,1,0:T(4,128)}), f32[4,4,256]{2,1,0:T(4,128)S(1)}, u32[]{:S(2)}, u32[]{:S(2)}) %all-to-all-start.2) | async-done | bytes 16416 | tf_op jit(solution)/shard_map/all_to_all | solution.py:66
  210.5 0.0 copy-done.5
  210.5 0.6 multiply_add_fusion
  211.1 0.0 collective-permute-done.1
  211.1 0.1 broadcast_select_fusion.1
  211.2 0.1 maximum_bitcast_fusion
  211.3 0.0 copy-done.1
  211.3 1.1 copy.16
  (3 shorter events, 0.0 us)
Async XLA Ops:
  7.2 80.5 %all-gather.2.cloned.1.call-start = ((), (), s32[]{:S(2)}) async-start(), calls=%async_computation.3 | async-start | bytes 3932160 | tf_op jit(solution)/shard_map/all_gather | solution.py:28
  94.1 1.4 copy-start
  95.5 71.5 %copy-start.2 = (f32[2,8,256]{2,1,0:T(8,128)S(1)}, f32[2,8,256]{2,1,0:T(8,128)}, u32[]{:S(2)}) copy-start(f32[2,8,256]{2,1,0:T(8,128)} %param.10) | copy-start | bytes 49156
  95.5 71.5 %copy-start.3 = (f32[2,8,256]{2,1,0:T(8,128)S(1)}, f32[2,8,256]{2,1,0:T(8,128)}, u32[]{:S(2)}) copy-start(f32[2,8,256]{2,1,0:T(8,128)} %param.8) | copy-start | bytes 49156
  95.5 71.5 %copy-start.4 = (f32[2,8,256]{2,1,0:T(8,128)S(1)}, f32[2,8,256]{2,1,0:T(8,128)}, u32[]{:S(2)}) copy-start(f32[2,8,256]{2,1,0:T(8,128)} %param.9) | copy-start | bytes 49156
  95.6 4.3 %collective-permute-start = (bf16[32,2,8,512]{3,2,1,0:T(8,128)(2,1)S(1)}, bf16[32,2,8,512]{3,2,1,0:T(8,128)(2,1)S(1)}, u32[]{:S(2)}, u32[]{:S(2)}) collective-permute-start(bf16[32,2,8,512]{3,2,1,0:T(8,128)(2,1)S(1)} %fusion.3), channel_id=1, source_target_pairs={{0,8},{8,0},{1,9},{9,1},{2,10},{10,2},{3,11},{11,3},{4,12},{12,4},... | collective-permute-start | bytes 1572872 | tf_op jit(solution)/shard_map/ppermute | solution.py:37
  101.2 109.2 %copy-start.5 = (f32[1,1,4,1024]{3,2,1,0:T(4,128)S(1)}, f32[1,1,4,1024]{3,2,1,0:T(4,128)}, u32[]{:S(2)}) copy-start(f32[1,1,4,1024]{3,2,1,0:T(4,128)} %param.11) | copy-start | bytes 49156
  167.6 43.7 %copy-start.1 = (f32[2,8,256]{2,1,0:T(8,128)}, f32[2,8,256]{2,1,0:T(8,128)S(1)}, u32[]{:S(2)}) copy-start(f32[2,8,256]{2,1,0:T(8,128)S(1)} %get-tuple-element.6) | copy-start | bytes 49156
  185.2 25.9 %collective-permute-start.1 = (bf16[64,2,8,256]{3,2,1,0:T(8,128)(2,1)S(1)}, bf16[64,2,8,256]{3,2,1,0:T(8,128)(2,1)S(1)}, u32[]{:S(2)}, u32[]{:S(2)}) collective-permute-start(bf16[64,2,8,256]{3,2,1,0:T(8,128)(2,1)S(1)} %all_to_all.24), channel_id=1, source_target_pairs={{0,8},{8,0},{1,9},{9,1},{2,10},{10,2},{3,11},{11,3},{4,12},{12,4},... | collective-permute-start | bytes 1572872 | tf_op jit(solution)/shard_map/ppermute | solution.py:59
  198.9 11.6 %all-to-all-start.2 = ((f32[4,4,256]{2,1,0:T(4,128)}), f32[4,4,256]{2,1,0:T(4,128)S(1)}, u32[]{:S(2)}, u32[]{:S(2)}) async-start(f32[4,4,256]{2,1,0:T(4,128)} %all_to_all.18), calls=%async_computation.2 | async-start | bytes 32768 | tf_op jit(solution)/shard_map/all_to_all | solution.py:66
Sparse Core Ops, SparseCore 0:
  10.1 77.5 all-gather.1

commit v2 on v1

v2 whole, which is shorter than its diff:
```python
import jax
import jax.numpy as jnp
from jax import lax
from jax.experimental import pallas as pl
from jax.experimental.pallas import tpu as pltpu
from jax.sharding import Mesh, PartitionSpec as P

STEP = 100


beta_one = 0.9
beta_two = 0.95
learn_rate = 0.05
decay_rate = 0.1
adam_eps = 1e-08
average_keep = 0.9

XYR = ("x", "y", "replica")
SWAP = ((0, 1), (1, 0))


def round_trip(count, step):
    return [(i, (i + step) % count) for i in range(count)]


def along_tokens(block, against):
    return lax.dot_general(
        block, against, (((0,), (0,)), ((), ())), preferred_element_type=jnp.float32
    )


def near_kernel(where, own, low_first, high_second, low_second, high_first, outgrad, _, total):
    count, part = own.shape[0], low_first.shape[0]
    shards_all = outgrad.shape[0] // count

    def against(step, half, size):
        start = lax.rem(where[0] + step, shards_all) * count + half * part
        return outgrad[pl.ds(pl.multiple_of(start, part), size), :]

    total[...] = (
        along_tokens(own[...], against(0, 0, count))
        + along_tokens(low_first[...], against(shards_all - 1, 0, part))
        + along_tokens(low_second[...], against(shards_all - 1, 1, part))
        + along_tokens(high_first[...], against(1, 0, part))
        + along_tokens(high_second[...], against(1, 1, part))
    )


def far_kernel(where, total, far_first, far_second, outgrad, keep, give):
    part = far_first.shape[0]
    start = lax.rem(where[0] + 2, outgrad.shape[0] // (2 * part)) * (2 * part)
    against = outgrad[pl.ds(pl.multiple_of(start, part), 2 * part), :]
    value = (
        total[...]
        + along_tokens(far_first[...], against[:part])
        + along_tokens(far_second[...], against[part:])
    )
    lines, width = keep.shape[1], keep.shape[2]
    value = value.reshape(keep.shape[0], 2, lines, width)
    even, odd = value[:, 0], value[:, 1]
    first_core = where[1] == 0
    keep[...] = jnp.where(first_core, even, odd)
    give[...] = jnp.where(first_core, odd, even).astype(give.dtype)


def shards(features, cotangents, moment_one, moment_two, master, average):
    f32, bf16 = jnp.float32, jnp.bfloat16
    col_width = cotangents.shape[3]
    rows = moment_one.shape[1]
    nx, ny, nr = (lax.axis_size(name) for name in XYR)
    nt = lax.axis_size("tensor")
    peers = nx * ny * nr
    core = lax.axis_index("core")
    place = lax.axis_index("tensor")
    where = jnp.stack([place, core]).astype(jnp.int32)

    tokens = features[0]
    count, dim_model = tokens.shape
    part = count // 2
    first, second = tokens[:part], tokens[part:]
    up, down = round_trip(nt, 1), round_trip(nt, nt - 1)
    low_first = lax.ppermute(first, "tensor", up)
    high_second = lax.ppermute(second, "tensor", down)
    low_second = lax.ppermute(second, "tensor", up)
    high_first = lax.ppermute(first, "tensor", down)
    far_first = lax.ppermute(low_first, "tensor", up)
    far_second = lax.ppermute(high_second, "tensor", down)
    outgrad = cotangents[0].reshape(cotangents.shape[1], 2 * col_width)

    held_rows = 2 * rows // nt
    state = jnp.stack([moment_one, moment_two, master])
    state = state.reshape(3, nt, held_rows, col_width).transpose(1, 0, 2, 3)
    state = lax.all_to_all(state, "tensor", 0, 0, tiled=True)

    tile = dim_model // nx
    width = 2 * col_width
    lines = nr * rows
    whole = pl.BlockSpec(outgrad.shape, lambda i, w: (0, 0))
    piece = pl.BlockSpec((part, tile), lambda i, w: (0, i))
    block = pl.BlockSpec((tile, width), lambda i, w: (i, 0))
    split = pl.BlockSpec((ny, lines, width), lambda i, w: (i, 0, 0))
    total = pl.pallas_call(
        near_kernel,
        out_shape=jax.ShapeDtypeStruct((dim_model, width), f32),
        grid_spec=pltpu.PrefetchScalarGridSpec(
            num_scalar_prefetch=1,
            grid=(nx,),
            in_specs=[
                pl.BlockSpec((count, tile), lambda i, w: (0, i)),
                piece,
                piece,
                piece,
                piece,
                whole,
                pl.BlockSpec(memory_space=pl.ANY),
            ],
            out_specs=block,
        ),
        cost_estimate=pl.CostEstimate(
            flops=6 * count * dim_model * width, bytes_accessed=8 * 2**20, transcendentals=0
        ),
    )(where, tokens, low_first, high_second, low_second, high_first, outgrad, state)
    keep, give = pl.pallas_call(
        far_kernel,
        out_shape=(
            jax.ShapeDtypeStruct((nx * ny, lines, width), f32),
            jax.ShapeDtypeStruct((nx * ny, lines, width), bf16),
        ),
        grid_spec=pltpu.PrefetchScalarGridSpec(
            num_scalar_prefetch=1,
            grid=(nx,),
            in_specs=[block, piece, piece, whole],
            out_specs=(split, split),
        ),
        cost_estimate=pl.CostEstimate(
            flops=2 * count * dim_model * width, bytes_accessed=6 * 2**20, transcendentals=0
        ),
    )(where, total, far_first, far_second, outgrad)

    got = lax.ppermute(give, "core", SWAP)
    half = (keep + got.astype(f32)).astype(bf16).reshape(peers, rows, width)
    terms = lax.all_to_all(half, XYR, split_axis=0, concat_axis=0, tiled=True)
    grad_piece = jnp.sum(terms.astype(f32), axis=0).reshape(rows, 2, col_width)
    gradient = jnp.transpose(grad_piece, (1, 0, 2))

    flat = gradient.reshape(nt, held_rows, col_width)
    squares = jnp.sum(flat * flat, axis=(0, 1))
    mixed = jnp.concatenate([flat, jnp.broadcast_to(squares, flat.shape)], axis=1)
    mixed = lax.all_to_all(mixed, "tensor", 0, 0, tiled=True)
    row_grad = mixed[:, :held_rows]
    squares = jnp.sum(mixed[:, held_rows], axis=0)
    others = ("x", "y", "core", "replica")
    spread = jnp.broadcast_to(squares, (lax.axis_size(others), col_width))
    squares = jnp.sum(lax.all_to_all(spread, others, 0, 0, tiled=True))
    count_all = 2.0 * dim_model * dim_model
    clip_factor = 1.0 / jnp.sqrt(squares / count_all + 1e-06)

    fix_one = 1.0 - beta_one**STEP
    fix_two = 1.0 - beta_two**STEP

    def update(grad, one, two, held):
        scaled = clip_factor * grad
        new_one = beta_one * one + (1.0 - beta_one) * scaled
        new_two = beta_two * two + (1.0 - beta_two) * (scaled * scaled)
        direction = new_one / fix_one / (jnp.sqrt(new_two / fix_two) + adam_eps)
        return new_one, new_two, held - learn_rate * (direction + decay_rate * held)

    new_first, new_second, new_master = update(gradient, moment_one, moment_two, master)

    mine = new_master.astype(bf16)
    spread = jnp.broadcast_to(mine[None], (peers,) + mine.shape)
    column = lax.all_to_all(spread, XYR, split_axis=0, concat_axis=0, tiled=True)
    other = lax.ppermute(column, "core", SWAP)
    even = jnp.where(core == 0, column, other)
    odd = jnp.where(core == 0, other, column)
    both = jnp.stack([even, odd]).reshape(2, nx * ny, nr, 2, rows, col_width)
    weights = jnp.transpose(both, (3, 1, 0, 2, 4, 5)).reshape(2, dim_model, col_width)

    row_master = update(row_grad, state[:, 0], state[:, 1], state[:, 2])[2]
    row_master = jnp.transpose(row_master, (1, 0, 2)).reshape(average.shape)
    new_average = average_keep * average + (1.0 - average_keep) * row_master
    return (weights, new_first, new_second, new_master, new_average)


def solution(mesh):
    shape = dict(zip(mesh.axis_names, mesh.devices.shape))
    nx, ny = 4, shape["dp"] // 8
    fine = Mesh(
        mesh.devices.reshape(nx, ny, 2, shape["tensor"], shape["replica"]),
        ("x", "y", "core", "tensor", "replica"),
    )
    groups = ("x", "y", "core", "replica")
    state = P(None, groups, "tensor")
    placed = (
        P(groups, "tensor", None),
        P(groups, None, None, "tensor"),
        state,
        state,
        state,
        P(groups, "tensor", None, None),
    )
    return jax.shard_map(
        shards,
        mesh=fine,
        in_specs=placed,
        out_specs=(P(None, None, "tensor"), state, state, state, P(groups, "tensor", None, None)),
        check_vma=False,
    )
```

time: 220 us -> 182 us (0.83)
  waiting for transfers between devices: 84.9 us -> 35.2 us
  starting transfers between devices: 20.9 us -> 41.4 us
  between operations: 14.9 us -> 1.58 us
  Pallas kernels: 0 us -> 12.1 us
  local copies, waits for them, and re-layouts: 10.1 us -> 6.49 us
  matrix products: 3.19 us -> 0 us
  blocking collectives: 81.8 us -> 79.3 us
    all_gather x1 -> x0, waiting for transfers between devices: 76.1 us -> none  [shards(): tokens_all = lax.all_gather(features, 'tensor', axis=1, tiled=True)[0]]
    psum x4 -> x0, blocking collectives: 38.4 us -> none  [shards(): square_total = lax.psum(square_total, names)]
    all_to_all x0 -> x2, blocking collectives: none -> 33.2 us  [the longest x1 21.4 us: shards(): squares = jnp.sum(lax.all_to_all(spread, others, 0, 0, tiled=True))]
    ppermute x1 -> x7, starting transfers between devices: 2.75 us -> 31.8 us  [the longest x1 11.5 us: shards(): high_second = lax.ppermute(second, 'tensor', down)]
    all_to_all x1, waiting for transfers between devices: 6.63 us -> 24.8 us  [shards(): state = lax.all_to_all(state, 'tensor', 0, 0, tiled=True)]
    pallas_call x0 -> x2, Pallas kernels: none -> 12.1 us  [the longest x1 6.46 us: shards(): pl.pallas_call(near_kernel, out_shape=jax.ShapeDtypeStruct((dim_model, wi...]
    ppermute x1, starting transfers between devices: 13.1 us -> 4.75 us  [shards(): other = lax.ppermute(column, 'core', SWAP)]
    ppermute x1 -> x7, waiting for transfers between devices: 1.51 us -> 9.58 us  [the longest x1 7.84 us: shards(): high_second = lax.ppermute(second, 'tensor', down)]
  transfers between devices with their start and end apart: 4 -> 9, of which waited for: 3 -> 4; matrix products, arithmetic and copies ran while one was open for 2% -> 2% of each run, Pallas kernels for 0% -> 4%
where the time goes in v2:
time: 182 us; the launch traced here: 181 us
  blocking collectives  79.3 us (44%)
  starting transfers between devices  41.4 us (23%)
  waiting for transfers between devices  35.2 us (19%)
  Pallas kernels  12.1 us (7%)
  local copies, waits for them, and re-layouts  6.49 us (4%)
  other arithmetic  5.11 us (3%)
    all_to_all x1, blocking collectives, shards(): terms = lax.all_to_all(half, XYR, split_axis=0, concat_axis=0, tiled=True)  26 us
    all_to_all x1, waiting for transfers between devices, shards(): state = lax.all_to_all(state, 'tensor', 0, 0, tiled=True)  24.8 us
    all_to_all x1, blocking collectives, shards(): squares = jnp.sum(lax.all_to_all(spread, others, 0, 0, tiled=True))  21.4 us
    all_to_all x1, blocking collectives, shards(): lax.all_to_all(spread, XYR, split_axis=0, concat_axis=0, tiled=True)  20 us
    all_to_all x1, blocking collectives, shards(): mixed = lax.all_to_all(mixed, 'tensor', 0, 0, tiled=True)  11.8 us
    ppermute x1, starting transfers between devices, shards(): high_second = lax.ppermute(second, 'tensor', down)  11.5 us
    ppermute x1, waiting for transfers between devices, shards(): high_second = lax.ppermute(second, 'tensor', down)  7.84 us
    pallas_call x1, Pallas kernels, shards(): pl.pallas_call(near_kernel, out_shape=jax.ShapeDtypeStruct((dim_model, wi...  6.46 us
  transfers between devices with their start and end apart: 9, of which 4 were waited for; matrix products, arithmetic and copies ran while one was open for 2% of the time, Pallas kernels for 4%

profile of v2, /device:TPU:1, one launch (start us, length us, event | category | flops | bytes accessed | tf_op | source)
XLA Modules:
  0.0 181.2 jit_solution(4786720424500177896)
XLA Ops:
  0.6 0.0 copy-start.9
  0.6 0.0 copy-start.8
  0.7 0.0 copy-start.7
  0.7 0.0 copy-start
  0.7 2.2 %slice_bitcast_fusion = (bf16[192,1024]{1,0:T(8,128)(2,1)}, bf16[192,1024]{1,0:T(8,128)(2,1)}) fusion(bf16[1,384,1024]{2,1,0:T(8,128)(2,1)} %param.6), kind=kLoop, calls=%fused_computation.5 | loop fusion | bytes 1572864 | tf_op jit(solution)/shard_map/slice | solution.py:80
  2.8 11.5 %collective-permute-start.1 = (bf16[192,1024]{1,0:T(8,128)(2,1)}, bf16[192,1024]{1,0:T(8,128)(2,1)S(1)}, u32[]{:S(2)}, u32[]{:S(2)}) collective-permute-start(bf16[192,1024]{1,0:T(8,128)(2,1)} %get-tuple-element.15), channel_id=1, source_target_pairs={{0,6},{2,0},{4,2},{6,4},{1,7},{3,1},{5,3},{7,5},{8,14},{10,8},{12,... | collective-permute-start | bytes 1179656 | tf_op jit(solution)/shard_map/ppermute | solution.py:83
  14.3 1.9 %collective-permute-start = (bf16[192,1024]{1,0:T(8,128)(2,1)}, bf16[192,1024]{1,0:T(8,128)(2,1)S(1)}, u32[]{:S(2)}, u32[]{:S(2)}) collective-permute-start(bf16[192,1024]{1,0:T(8,128)(2,1)} %get-tuple-element.16), channel_id=1, source_target_pairs={{0,2},{2,4},{4,6},{6,0},{1,3},{3,5},{5,7},{7,1},{8,10},{10,12},{12... | collective-permute-start | bytes 1179656 | tf_op jit(solution)/shard_map/ppermute | solution.py:82
  16.3 2.2 %collective-permute-start.2 = (bf16[192,1024]{1,0:T(8,128)(2,1)}, bf16[192,1024]{1,0:T(8,128)(2,1)S(1)}, u32[]{:S(2)}, u32[]{:S(2)}) collective-permute-start(bf16[192,1024]{1,0:T(8,128)(2,1)} %get-tuple-element.15), channel_id=1, source_target_pairs={{0,2},{2,4},{4,6},{6,0},{1,3},{3,5},{5,7},{7,1},{8,10},{10,12},{12... | collective-permute-start | bytes 1179656 | tf_op jit(solution)/shard_map/ppermute | solution.py:84
  18.4 5.2 %collective-permute-start.3 = (bf16[192,1024]{1,0:T(8,128)(2,1)}, bf16[192,1024]{1,0:T(8,128)(2,1)}, u32[]{:S(2)}, u32[]{:S(2)}) collective-permute-start(bf16[192,1024]{1,0:T(8,128)(2,1)} %get-tuple-element.16), channel_id=1, source_target_pairs={{0,6},{2,0},{4,2},{6,4},{1,7},{3,1},{5,3},{7,5},{8,14},{10,8},{12,... | collective-permute-start | bytes 1179656 | tf_op jit(solution)/shard_map/ppermute | solution.py:85
  23.7 7.8 %collective-permute-done.1.high_second = bf16[192,1024]{1,0:T(8,128)(2,1)S(1)} collective-permute-done((bf16[192,1024]{1,0:T(8,128)(2,1)}, bf16[192,1024]{1,0:T(8,128)(2,1)S(1)}, u32[]{:S(2)}, u32[]{:S(2)}) %collective-permute-start.1) | collective-permute-done | bytes 393248 | tf_op jit(solution)/shard_map/ppermute | solution.py:83
  31.5 0.0 copy-start.3
  31.5 6.2 %collective-permute-start.5 = (bf16[192,1024]{1,0:T(8,128)(2,1)S(1)}, bf16[192,1024]{1,0:T(8,128)(2,1)S(1)}, u32[]{:S(2)}, u32[]{:S(2)}) collective-permute-start(bf16[192,1024]{1,0:T(8,128)(2,1)S(1)} %collective-permute-done.1.high_second), channel_id=1, source_target_pairs={{0,6},{2,0},{4,2},{6,4},{1,7},{3,1},{5,3},{7,5},{8,14},{10,8},{12,... | collective-permute-start | bytes 1179656 | tf_op jit(solution)/shard_map/ppermute | solution.py:87
  37.8 0.0 collective-permute-done.low_first
  37.8 0.0 copy-start.4
  37.8 1.9 %collective-permute-start.4 = (bf16[192,1024]{1,0:T(8,128)(2,1)S(1)}, bf16[192,1024]{1,0:T(8,128)(2,1)}, u32[]{:S(2)}, u32[]{:S(2)}) collective-permute-start(bf16[192,1024]{1,0:T(8,128)(2,1)S(1)} %collective-permute-done.low_first), channel_id=1, source_target_pairs={{0,2},{2,4},{4,6},{6,0},{1,3},{3,5},{5,7},{7,1},{8,10},{10,12},{12... | collective-permute-start | bytes 1179656 | tf_op jit(solution)/shard_map/ppermute | solution.py:86
  39.7 0.0 copy-done.9
  39.7 0.0 copy-done.8
  39.8 0.0 copy-done.7
  39.8 0.6 maximum_bitcast_fusion.1
  40.4 4.8 %all-to-all-start = ((f32[4,3,4,256]{3,2,1,0:T(4,128)}), f32[4,3,4,256]{3,2,1,0:T(4,128)S(1)}, u32[]{:S(2)}, u32[]{:S(2)}) async-start(f32[4,3,4,256]{3,2,1,0:T(4,128)} %maximum_bitcast_fusion.1), calls=%async_computation | async-start | bytes 98304 | tf_op jit(solution)/shard_map/all_to_all | solution.py:93
  45.3 0.0 copy-done
  45.3 1.5 copy.26
  46.8 0.0 copy-done.3
  46.8 0.0 copy-done.4
  46.8 0.6 pad_add_fusion.where
  47.4 24.8 %all-to-all-done._ = f32[4,3,4,256]{3,2,1,0:T(4,128)S(1)} async-done(((f32[4,3,4,256]{3,2,1,0:T(4,128)}), f32[4,3,4,256]{3,2,1,0:T(4,128)S(1)}, u32[]{:S(2)}, u32[]{:S(2)}) %all-to-all-start) | async-done | bytes 49184 | tf_op jit(solution)/shard_map/all_to_all | solution.py:93
  72.2 0.0 copy-start.1
  72.2 0.0 collective-permute-done.2.low_second
  72.2 0.0 copy-start.6
  72.2 0.0 collective-permute-done.3.high_first
  72.2 0.6 copy-done.1
  72.8 0.1 copy-done.6
  73.0 6.5 %shard_map.101.total = f32[1024,512]{1,0:T(8,128)} custom-call(s32[2]{0:T(128)} %pad_add_fusion.where, bf16[384,1024]{1,0:T(8,128)(2,1)} %bitcast.70, bf16[192,1024]{1,0:T(8,128)(2,1)} %copy-done.4, bf16[192,1024]{1,0:T(8,128)(2,1)} %copy-done.3, bf16[192,1024]{1,0:T(8,128)(2,1)} %copy-done.6, bf16[192,1024]{1,0:T(8,128)(2,1)} %collective-permute-done.3.high_first, ...), custom_call_target="tpu_custom_call" | custom-call | flops 1207959552 | bytes 8388608 | tf_op jit(solution)/shard_map/pallas_call | solution.py:102
  79.4 0.0 collective-permute-done.5.far_second
  79.4 0.0 copy-start.5
  79.4 0.0 collective-permute-done.4.far_first
  79.4 0.8 copy-done.5
  80.2 5.6 %shard_map.102 = (f32[32,16,512]{2,1,0:T(8,128)}, bf16[32,16,512]{2,1,0:T(8,128)(2,1)}) custom-call(s32[2]{0:T(128)} %pad_add_fusion.where, f32[1024,512]{1,0:T(8,128)} %shard_map.101.total, bf16[192,1024]{1,0:T(8,128)(2,1)} %collective-permute-done.4.far_first, bf16[192,1024]{1,0:T(8,128)(2,1)} %copy-done.5, bf16[1536,512]{1,0:T(8,128)(2,1)} %bitcast.69), custom_call_target="tpu_custom_call" | custom-call | flops 402653184 | bytes 6291456 | tf_op jit(solution)/shard_map/pallas_call | solution.py:123
  85.8 2.8 %collective-permute-start.6 = (bf16[32,16,512]{2,1,0:T(8,128)(2,1)}, bf16[32,16,512]{2,1,0:T(8,128)(2,1)S(1)}, u32[]{:S(2)}, u32[]{:S(2)}) collective-permute-start(bf16[32,16,512]{2,1,0:T(8,128)(2,1)} %get-tuple-element.8), channel_id=1, source_target_pairs={{0,8},{8,0},{1,9},{9,1},{2,10},{10,2},{3,11},{11,3},{4,12},{12,4},... | collective-permute-start | bytes 1572872 | tf_op jit(solution)/shard_map/ppermute | solution.py:140
  88.7 1.7 collective-permute-done.6
  90.4 1.4 add_convert_fusion
  91.8 26.0 %all_to_all.26 = bf16[64,8,512]{2,1,0:T(8,128)(2,1)S(1)} all-to-all(bf16[64,8,512]{2,1,0:T(8,128)(2,1)S(1)} %bitcast.73), channel_id=1, replica_groups=mesh['x'=4,'y'=8,'core'=2,'tensor'=4,'replica'=2] {'x','y','replica'}, dimensions={0} | all-to-all | bytes 1048576 | tf_op jit(solution)/shard_map/all_to_all | solution.py:142
  117.8 0.0 copy-start.2
  117.9 0.0 copy-start.10
  117.9 0.1 convert_reduce_fusion
  118.0 11.8 %all_to_all.27 = f32[4,8,256]{2,1,0:T(8,128)S(1)} all-to-all(f32[4,8,256]{2,1,0:T(8,128)S(1)} %pad_maximum_fusion), channel_id=1, replica_groups=mesh['x'=4,'y'=8,'core'=2,'tensor'=4,'replica'=2] {'tensor'}, dimensions={0} | all-to-all | bytes 65536 | tf_op jit(solution)/shard_map/all_to_all | solution.py:149
  129.8 0.1 broadcast_in_dim.13
  129.9 21.4 %all_to_all.28 = f32[128,1,256]{2,1,0:T(1,128)S(1)} all-to-all(f32[128,1,256]{2,1,0:T(1,128)S(1)} %broadcast_in_dim.13), channel_id=1, replica_groups=mesh['x'=4,'y'=8,'core'=2,'tensor'=4,'replica'=2] {'x','y','core','repli..., dimensions={0} | all-to-all | bytes 262144 | tf_op jit(solution)/shard_map/all_to_all | solution.py:154
  151.3 0.9 reduce_sum.39
  152.9 0.6 fusion.10
  153.6 20.0 %all_to_all.29 = bf16[64,2,8,256]{3,2,1,0:T(8,128)(2,1)S(1)} all-to-all(bf16[64,2,8,256]{3,2,1,0:T(8,128)(2,1)S(1)} %broadcast_in_dim.14), channel_id=1, replica_groups=mesh['x'=4,'y'=8,'core'=2,'tensor'=4,'replica'=2] {'x','y','replica'}, dimensions={0} | all-to-all | bytes 1048576 | tf_op jit(solution)/shard_map/all_to_all | solution.py:172
  173.6 4.7 %collective-permute-start.7 = (bf16[64,2,8,256]{3,2,1,0:T(8,128)(2,1)S(1)}, bf16[64,2,8,256]{3,2,1,0:T(8,128)(2,1)S(1)}, u32[]{:S(2)}, u32[]{:S(2)}) collective-permute-start(bf16[64,2,8,256]{3,2,1,0:T(8,128)(2,1)S(1)} %all_to_all.29), channel_id=1, source_target_pairs={{0,8},{8,0},{1,9},{9,1},{2,10},{10,2},{3,11},{11,3},{4,12},{12,4},... | collective-permute-start | bytes 1572872 | tf_op jit(solution)/shard_map/ppermute | solution.py:173
  178.4 0.0 copy-done.2
  178.4 0.0 copy-done.10
  178.4 0.6 multiply_add_fusion
  179.0 0.8 collective-permute-done.7
  179.9 0.1 broadcast_select_fusion.1
  179.9 0.1 maximum_bitcast_fusion
  180.1 1.1 copy.20
  (10 shorter events, 0.2 us)
Async XLA Ops:
  0.6 39.1 %copy-start.9 = (f32[2,8,256]{2,1,0:T(8,128)S(1)}, f32[2,8,256]{2,1,0:T(8,128)}, u32[]{:S(2)}) copy-start(f32[2,8,256]{2,1,0:T(8,128)} %param.8) | copy-start | bytes 49156
  0.6 39.1 %copy-start.8 = (f32[2,8,256]{2,1,0:T(8,128)S(1)}, f32[2,8,256]{2,1,0:T(8,128)}, u32[]{:S(2)}) copy-start(f32[2,8,256]{2,1,0:T(8,128)} %param.9) | copy-start | bytes 49156
  0.7 39.1 %copy-start.7 = (f32[2,8,256]{2,1,0:T(8,128)S(1)}, f32[2,8,256]{2,1,0:T(8,128)}, u32[]{:S(2)}) copy-start(f32[2,8,256]{2,1,0:T(8,128)} %param.10) | copy-start | bytes 49156
  0.7 44.6 %copy-start = (bf16[1,1536,2,256]{3,2,1,0:T(2,128)(2,1)S(1)}, bf16[1,1536,2,256]{3,2,1,0:T(2,128)(2,1)}, u32[]{:S(2)}) copy-start(bf16[1,1536,2,256]{3,2,1,0:T(2,128)(2,1)} %param.7) | copy-start | bytes 4718596
  2.8 28.7 %collective-permute-start.1 = (bf16[192,1024]{1,0:T(8,128)(2,1)}, bf16[192,1024]{1,0:T(8,128)(2,1)S(1)}, u32[]{:S(2)}, u32[]{:S(2)}) collective-permute-start(bf16[192,1024]{1,0:T(8,128)(2,1)} %get-tuple-element.15), channel_id=1, source_target_pairs={{0,6},{2,0},{4,2},{6,4},{1,7},{3,1},{5,3},{7,5},{8,14},{10,8},{12,... | collective-permute-start | bytes 1179656 | tf_op jit(solution)/shard_map/ppermute | solution.py:83
  14.3 23.4 %collective-permute-start = (bf16[192,1024]{1,0:T(8,128)(2,1)}, bf16[192,1024]{1,0:T(8,128)(2,1)S(1)}, u32[]{:S(2)}, u32[]{:S(2)}) collective-permute-start(bf16[192,1024]{1,0:T(8,128)(2,1)} %get-tuple-element.16), channel_id=1, source_target_pairs={{0,2},{2,4},{4,6},{6,0},{1,3},{3,5},{5,7},{7,1},{8,10},{10,12},{12... | collective-permute-start | bytes 1179656 | tf_op jit(solution)/shard_map/ppermute | solution.py:82
  16.3 55.9 %collective-permute-start.2 = (bf16[192,1024]{1,0:T(8,128)(2,1)}, bf16[192,1024]{1,0:T(8,128)(2,1)S(1)}, u32[]{:S(2)}, u32[]{:S(2)}) collective-permute-start(bf16[192,1024]{1,0:T(8,128)(2,1)} %get-tuple-element.15), channel_id=1, source_target_pairs={{0,2},{2,4},{4,6},{6,0},{1,3},{3,5},{5,7},{7,1},{8,10},{10,12},{12... | collective-permute-start | bytes 1179656 | tf_op jit(solution)/shard_map/ppermute | solution.py:84
  18.4 53.8 %collective-permute-start.3 = (bf16[192,1024]{1,0:T(8,128)(2,1)}, bf16[192,1024]{1,0:T(8,128)(2,1)}, u32[]{:S(2)}, u32[]{:S(2)}) collective-permute-start(bf16[192,1024]{1,0:T(8,128)(2,1)} %get-tuple-element.16), channel_id=1, source_target_pairs={{0,6},{2,0},{4,2},{6,4},{1,7},{3,1},{5,3},{7,5},{8,14},{10,8},{12,... | collective-permute-start | bytes 1179656 | tf_op jit(solution)/shard_map/ppermute | solution.py:85
  31.5 15.3 %copy-start.3 = (bf16[192,1024]{1,0:T(8,128)(2,1)}, bf16[192,1024]{1,0:T(8,128)(2,1)S(1)}, u32[]{:S(2)}) copy-start(bf16[192,1024]{1,0:T(8,128)(2,1)S(1)} %collective-permute-done.1.high_second) | copy-start | bytes 1179652
  31.5 47.9 %collective-permute-start.5 = (bf16[192,1024]{1,0:T(8,128)(2,1)S(1)}, bf16[192,1024]{1,0:T(8,128)(2,1)S(1)}, u32[]{:S(2)}, u32[]{:S(2)}) collective-permute-start(bf16[192,1024]{1,0:T(8,128)(2,1)S(1)} %collective-permute-done.1.high_second), channel_id=1, source_target_pairs={{0,6},{2,0},{4,2},{6,4},{1,7},{3,1},{5,3},{7,5},{8,14},{10,8},{12,... | collective-permute-start | bytes 1179656 | tf_op jit(solution)/shard_map/ppermute | solution.py:87
  37.8 9.0 %copy-start.4 = (bf16[192,1024]{1,0:T(8,128)(2,1)}, bf16[192,1024]{1,0:T(8,128)(2,1)S(1)}, u32[]{:S(2)}) copy-start(bf16[192,1024]{1,0:T(8,128)(2,1)S(1)} %collective-permute-done.low_first) | copy-start | bytes 1179652
  37.8 41.7 %collective-permute-start.4 = (bf16[192,1024]{1,0:T(8,128)(2,1)S(1)}, bf16[192,1024]{1,0:T(8,128)(2,1)}, u32[]{:S(2)}, u32[]{:S(2)}) collective-permute-start(bf16[192,1024]{1,0:T(8,128)(2,1)S(1)} %collective-permute-done.low_first), channel_id=1, source_target_pairs={{0,2},{2,4},{4,6},{6,0},{1,3},{3,5},{5,7},{7,1},{8,10},{10,12},{12... | collective-permute-start | bytes 1179656 | tf_op jit(solution)/shard_map/ppermute | solution.py:86
  40.4 31.8 %all-to-all-start = ((f32[4,3,4,256]{3,2,1,0:T(4,128)}), f32[4,3,4,256]{3,2,1,0:T(4,128)S(1)}, u32[]{:S(2)}, u32[]{:S(2)}) async-start(f32[4,3,4,256]{3,2,1,0:T(4,128)} %maximum_bitcast_fusion.1), calls=%async_computation | async-start | bytes 98304 | tf_op jit(solution)/shard_map/all_to_all | solution.py:93
  72.2 0.6 copy-start.1
  72.2 0.8 copy-start.6
  79.4 0.8 copy-start.5
  85.8 4.6 %collective-permute-start.6 = (bf16[32,16,512]{2,1,0:T(8,128)(2,1)}, bf16[32,16,512]{2,1,0:T(8,128)(2,1)S(1)}, u32[]{:S(2)}, u32[]{:S(2)}) collective-permute-start(bf16[32,16,512]{2,1,0:T(8,128)(2,1)} %get-tuple-element.8), channel_id=1, source_target_pairs={{0,8},{8,0},{1,9},{9,1},{2,10},{10,2},{3,11},{11,3},{4,12},{12,4},... | collective-permute-start | bytes 1572872 | tf_op jit(solution)/shard_map/ppermute | solution.py:140
  117.8 60.5 %copy-start.2 = (f32[4,3,4,256]{3,2,1,0:T(4,128)S(1)}, f32[4,3,4,256]{3,2,1,0:T(4,128)}, u32[]{:S(2)}) copy-start(f32[4,3,4,256]{3,2,1,0:T(4,128)} %copy-done.1) | copy-start | bytes 147460
  117.9 60.6 %copy-start.10 = (f32[1,1,4,1024]{3,2,1,0:T(4,128)S(1)}, f32[1,1,4,1024]{3,2,1,0:T(4,128)}, u32[]{:S(2)}) copy-start(f32[1,1,4,1024]{3,2,1,0:T(4,128)} %param.11) | copy-start | bytes 49156
  173.6 6.3 %collective-permute-start.7 = (bf16[64,2,8,256]{3,2,1,0:T(8,128)(2,1)S(1)}, bf16[64,2,8,256]{3,2,1,0:T(8,128)(2,1)S(1)}, u32[]{:S(2)}, u32[]{:S(2)}) collective-permute-start(bf16[64,2,8,256]{3,2,1,0:T(8,128)(2,1)S(1)} %all_to_all.29), channel_id=1, source_target_pairs={{0,8},{8,0},{1,9},{9,1},{2,10},{10,2},{3,11},{11,3},{4,12},{12,4},... | collective-permute-start | bytes 1572872 | tf_op jit(solution)/shard_map/ppermute | solution.py:173

commit v3 on v2

v3 whole, which is shorter than its diff:
```python
import jax
import jax.numpy as jnp
from jax import lax
from jax.experimental import pallas as pl
from jax.experimental.pallas import tpu as pltpu
from jax.sharding import Mesh, PartitionSpec as P

STEP = 100


beta_one = 0.9
beta_two = 0.95
learn_rate = 0.05
decay_rate = 0.1
adam_eps = 1e-08
average_keep = 0.9

XYR = ("x", "y", "replica")
SWAP = ((0, 1), (1, 0))


def round_trip(count, step):
    return [(i, (i + step) % count) for i in range(count)]


def along_tokens(block, against):
    return lax.dot_general(
        block, against, (((0,), (0,)), ((), ())), preferred_element_type=jnp.float32
    )


def near_kernel(where, own, low, high, outgrad, total):
    count = own.shape[0]
    shards_all = outgrad.shape[0] // count
    tile = 256

    def against(step):
        start = lax.rem(where[0] + step, shards_all) * count
        return outgrad[pl.ds(pl.multiple_of(start, count), count), :]

    for left in range(0, own.shape[1], tile):
        part = slice(left, left + tile)
        total[part, :] = (
            along_tokens(own[:, part], against(0))
            + along_tokens(low[:, part], against(shards_all - 1))
            + along_tokens(high[:, part], against(1))
        )


def far_kernel(where, total, far_first, far_second, outgrad, keep, give):
    part = far_first.shape[0]
    start = lax.rem(where[0] + 2, outgrad.shape[0] // (2 * part)) * (2 * part)
    against = outgrad[pl.ds(pl.multiple_of(start, 2 * part), 2 * part), :]
    first_core = where[1] == 0
    lines, width = keep.shape[1], keep.shape[2]
    tile = 256
    for left in range(0, total.shape[0], tile):
        cut = slice(left, left + tile)
        value = (
            total[cut, :]
            + along_tokens(far_first[:, cut], against[:part])
            + along_tokens(far_second[:, cut], against[part:])
        )
        value = value.reshape(tile // (2 * lines), 2, lines, width)
        even, odd = value[:, 0], value[:, 1]
        out = slice(left // (2 * lines), (left + tile) // (2 * lines))
        keep[out] = jnp.where(first_core, even, odd)
        give[out] = jnp.where(first_core, odd, even).astype(give.dtype)


def shards(features, cotangents, moment_one, moment_two, master, average):
    f32, bf16 = jnp.float32, jnp.bfloat16
    col_width = cotangents.shape[3]
    rows = moment_one.shape[1]
    nx, ny, nr = (lax.axis_size(name) for name in XYR)
    nt = lax.axis_size("tensor")
    peers = nx * ny * nr
    core = lax.axis_index("core")
    place = lax.axis_index("tensor")
    where = jnp.stack([place, core]).astype(jnp.int32)

    tokens = features[0]
    count, dim_model = tokens.shape
    part = count // 2
    up, down = round_trip(nt, 1), round_trip(nt, nt - 1)
    low = lax.ppermute(tokens, "tensor", up)
    high = lax.ppermute(tokens, "tensor", down)
    far_first = lax.ppermute(low[:part], "tensor", up)
    far_second = lax.ppermute(high[part:], "tensor", down)
    outgrad = cotangents[0].reshape(cotangents.shape[1], 2 * col_width)

    width = 2 * col_width
    lines = nr * rows
    scalars = pl.BlockSpec(memory_space=pltpu.SMEM)
    local = pl.BlockSpec(memory_space=pltpu.VMEM)
    params = pltpu.CompilerParams(vmem_limit_bytes=24 * 2**20)
    total = pl.pallas_call(
        near_kernel,
        out_shape=jax.ShapeDtypeStruct((dim_model, width), f32),
        in_specs=[scalars] + [local] * 4,
        out_specs=local,
        compiler_params=params,
        cost_estimate=pl.CostEstimate(
            flops=6 * count * dim_model * width, bytes_accessed=6 * 2**20, transcendentals=0
        ),
    )(where, tokens, low, high, outgrad)
    keep, give = pl.pallas_call(
        far_kernel,
        out_shape=(
            jax.ShapeDtypeStruct((nx * ny, lines, width), f32),
            jax.ShapeDtypeStruct((nx * ny, lines, width), bf16),
        ),
        in_specs=[scalars] + [local] * 4,
        out_specs=(local, local),
        compiler_params=params,
        cost_estimate=pl.CostEstimate(
            flops=2 * count * dim_model * width, bytes_accessed=6 * 2**20, transcendentals=0
        ),
    )(where, total, far_first, far_second, outgrad)

    got = lax.ppermute(give, "core", SWAP)
    half = (keep + got.astype(f32)).astype(bf16).reshape(peers, rows, width)
    terms = lax.all_to_all(half, XYR, split_axis=0, concat_axis=0, tiled=True)
    grad_piece = jnp.sum(terms.astype(f32), axis=0).reshape(rows, 2, col_width)
    gradient = jnp.transpose(grad_piece, (1, 0, 2))

    held_rows = 2 * rows // nt
    by_rows = lambda block: block.reshape(nt, held_rows, col_width)
    flat = by_rows(gradient)
    squares = jnp.broadcast_to(jnp.sum(flat * flat, axis=(0, 1)), flat.shape)
    mixed = [flat, by_rows(moment_one), by_rows(moment_two), by_rows(master), squares]
    mixed = lax.all_to_all(jnp.concatenate(mixed, axis=1), "tensor", 0, 0, tiled=True)
    row_grad, row_one, row_two, row_held, squares = jnp.split(mixed, 5, axis=1)
    squares = jnp.sum(squares[:, 0], axis=0)
    others = ("x", "y", "core", "replica")
    spread = jnp.broadcast_to(squares, (lax.axis_size(others), col_width))
    squares = jnp.sum(lax.all_to_all(spread, others, 0, 0, tiled=True))
    count_all = 2.0 * dim_model * dim_model
    clip_factor = 1.0 / jnp.sqrt(squares / count_all + 1e-06)

    fix_one = 1.0 - beta_one**STEP
    fix_two = 1.0 - beta_two**STEP

    def update(grad, one, two, held):
        scaled = clip_factor * grad
        new_one = beta_one * one + (1.0 - beta_one) * scaled
        new_two = beta_two * two + (1.0 - beta_two) * (scaled * scaled)
        direction = new_one / fix_one / (jnp.sqrt(new_two / fix_two) + adam_eps)
        return new_one, new_two, held - learn_rate * (direction + decay_rate * held)

    new_first, new_second, new_master = update(gradient, moment_one, moment_two, master)

    mine = new_master.astype(bf16)
    spread = jnp.broadcast_to(mine[None], (peers,) + mine.shape)
    column = lax.all_to_all(spread, XYR, split_axis=0, concat_axis=0, tiled=True)
    other = lax.ppermute(column, "core", SWAP)
    even = jnp.where(core == 0, column, other)
    odd = jnp.where(core == 0, other, column)
    both = jnp.stack([even, odd]).reshape(2, nx * ny, nr, 2, rows, col_width)
    weights = jnp.transpose(both, (3, 1, 0, 2, 4, 5)).reshape(2, dim_model, col_width)

    row_master = update(row_grad, row_one, row_two, row_held)[2]
    row_master = jnp.transpose(row_master, (1, 0, 2)).reshape(average.shape)
    new_average = average_keep * average + (1.0 - average_keep) * row_master
    return (weights, new_first, new_second, new_master, new_average)


def solution(mesh):
    shape = dict(zip(mesh.axis_names, mesh.devices.shape))
    nx, ny = 4, shape["dp"] // 8
    fine = Mesh(
        mesh.devices.reshape(nx, ny, 2, shape["tensor"], shape["replica"]),
        ("x", "y", "core", "tensor", "replica"),
    )
    groups = ("x", "y", "core", "replica")
    state = P(None, groups, "tensor")
    placed = (
        P(groups, "tensor", None),
        P(groups, None, None, "tensor"),
        state,
        state,
        state,
        P(groups, "tensor", None, None),
    )
    return jax.shard_map(
        shards,
        mesh=fine,
        in_specs=placed,
        out_specs=(P(None, None, "tensor"), state, state, state, P(groups, "tensor", None, None)),
        check_vma=False,
    )
```

time: 182 us -> 169 us (0.929)
  blocking collectives: 79.3 us -> 52.5 us
  starting transfers between devices: 41.4 us -> 62.4 us
  Pallas kernels: 12.1 us -> 3.65 us
  waiting for transfers between devices: 35.2 us -> 41.4 us
  local copies, waits for them, and re-layouts: 6.49 us -> 3.21 us
    all_to_all x2 -> x1, blocking collectives: 37.8 us -> 10.9 us  [shards(): lax.all_to_all(jnp.concatenate(mixed, axis=1), 'tensor', 0, 0, tiled=True)]
    ppermute x6 -> x4, waiting for transfers between devices: 7.85 us -> 23.2 us  [the longest x1 15.2 us: shards(): low = lax.ppermute(tokens, 'tensor', up)]
    all_to_all x1, starting transfers between devices: 4.83 us -> 17 us  [shards(): terms = lax.all_to_all(half, XYR, split_axis=0, concat_axis=0, tiled=True)]
    all_to_all x1, waiting for transfers between devices: 24.8 us -> 15.9 us  [shards(): terms = lax.all_to_all(half, XYR, split_axis=0, concat_axis=0, tiled=True)]
    ppermute x6 -> x4, starting transfers between devices: 29 us -> 36.5 us  [the longest x1 18.3 us: shards(): far_first = lax.ppermute(low[:part], 'tensor', up)]
    pallas_call x1, Pallas kernels: 5.65 us -> 1.31 us  [shards(): pl.pallas_call(far_kernel, out_shape=(jax.ShapeDtypeStruct((nx * ny, line...]
    pallas_call x1, Pallas kernels: 6.46 us -> 2.34 us  [shards(): pl.pallas_call(near_kernel, out_shape=jax.ShapeDtypeStruct((dim_model, wi...]
    slice x1 -> x2, local copies, waits for them, and re-layouts: 2.18 us -> 0.05 us  [the longest x1 0.03 us: shards(): far_second = lax.ppermute(high[part:], 'tensor', down)]
  transfers between devices with their start and end apart: 9 -> 7, of which waited for: 4 -> 6; matrix products, arithmetic and copies ran while one was open for 2% -> 2% of each run, Pallas kernels for 4% -> 1%
where the time goes in v3:
time: 169 us; the launch traced here: 168 us
  starting transfers between devices  62.4 us (37%)
  blocking collectives  52.5 us (31%)
  waiting for transfers between devices  41.4 us (24%)
  Pallas kernels  3.65 us (2%)
  other arithmetic  3.53 us (2%)
  local copies, waits for them, and re-layouts  3.21 us (2%)
    all_to_all x1, blocking collectives, shards(): squares = jnp.sum(lax.all_to_all(spread, others, 0, 0, tiled=True))  21.6 us
    all_to_all x1, blocking collectives, shards(): lax.all_to_all(spread, XYR, split_axis=0, concat_axis=0, tiled=True)  20 us
    ppermute x1, starting transfers between devices, shards(): far_first = lax.ppermute(low[:part], 'tensor', up)  18.3 us
    all_to_all x1, starting transfers between devices, shards(): terms = lax.all_to_all(half, XYR, split_axis=0, concat_axis=0, tiled=True)  17 us
    all_to_all x1, waiting for transfers between devices, shards(): terms = lax.all_to_all(half, XYR, split_axis=0, concat_axis=0, tiled=True)  15.9 us
    ppermute x1, waiting for transfers between devices, shards(): low = lax.ppermute(tokens, 'tensor', up)  15.2 us
    all_to_all x1, blocking collectives, shards(): lax.all_to_all(jnp.concatenate(mixed, axis=1), 'tensor', 0, 0, tiled=True)  10.9 us
    ppermute x1, starting transfers between devices, shards(): high = lax.ppermute(tokens, 'tensor', down)  6.77 us
  transfers between devices with their start and end apart: 7, of which 6 were waited for; matrix products, arithmetic and copies ran while one was open for 2% of the time, Pallas kernels for 1%

profile of v3, /device:TPU:1, one launch (start us, length us, event | category | flops | bytes accessed | tf_op | source)
XLA Modules:
  0.0 168.2 jit_solution(11116773161123933627)
XLA Ops:
  0.6 6.6 %collective-permute-start = (bf16[384,1024]{1,0:T(8,128)(2,1)}, bf16[384,1024]{1,0:T(8,128)(2,1)S(1)}, u32[]{:S(2)}, u32[]{:S(2)}) collective-permute-start(bf16[384,1024]{1,0:T(8,128)(2,1)} %bitcast.20), channel_id=1, source_target_pairs={{0,2},{2,4},{4,6},{6,0},{1,3},{3,5},{5,7},{7,1},{8,10},{10,12},{12... | collective-permute-start | bytes 2359304 | tf_op jit(solution)/shard_map/ppermute | solution.py:86
  7.3 6.8 %collective-permute-start.1 = (bf16[384,1024]{1,0:T(8,128)(2,1)}, bf16[384,1024]{1,0:T(8,128)(2,1)S(1)}, u32[]{:S(2)}, u32[]{:S(2)}) collective-permute-start(bf16[384,1024]{1,0:T(8,128)(2,1)} %bitcast.21), channel_id=1, source_target_pairs={{0,6},{2,0},{4,2},{6,4},{1,7},{3,1},{5,3},{7,5},{8,14},{10,8},{12,... | collective-permute-start | bytes 2359304 | tf_op jit(solution)/shard_map/ppermute | solution.py:87
  14.1 15.2 %collective-permute-done.low = bf16[384,1024]{1,0:T(8,128)(2,1)S(1)} collective-permute-done((bf16[384,1024]{1,0:T(8,128)(2,1)}, bf16[384,1024]{1,0:T(8,128)(2,1)S(1)}, u32[]{:S(2)}, u32[]{:S(2)}) %collective-permute-start) | collective-permute-done | bytes 786464 | tf_op jit(solution)/shard_map/ppermute | solution.py:86
  29.3 18.3 %collective-permute-start.2 = (bf16[192,1024]{1,0:T(8,128)(2,1)S(1)}, bf16[192,1024]{1,0:T(8,128)(2,1)S(1)}, u32[]{:S(2)}, u32[]{:S(2)}) collective-permute-start(bf16[192,1024]{1,0:T(8,128)(2,1)S(1)} %slice.13), channel_id=1, source_target_pairs={{0,2},{2,4},{4,6},{6,0},{1,3},{3,5},{5,7},{7,1},{8,10},{10,12},{12... | collective-permute-start | bytes 1179656 | tf_op jit(solution)/shard_map/ppermute | solution.py:88
  47.6 0.0 collective-permute-done.1.high
  47.7 4.7 %collective-permute-start.3 = (bf16[192,1024]{1,0:T(8,128)(2,1)S(1)}, bf16[192,1024]{1,0:T(8,128)(2,1)S(1)}, u32[]{:S(2)}, u32[]{:S(2)}) collective-permute-start(bf16[192,1024]{1,0:T(8,128)(2,1)S(1)} %slice.14), channel_id=1, source_target_pairs={{0,6},{2,0},{4,2},{6,4},{1,7},{3,1},{5,3},{7,5},{8,14},{10,8},{12,... | collective-permute-start | bytes 1179656 | tf_op jit(solution)/shard_map/ppermute | solution.py:89
  52.4 0.0 copy-start
  52.4 1.8 %copy.20 = bf16[192,8,2,256]{3,1,2,0:T(8,128)(2,1)S(1)} copy(bf16[192,8,2,256]{3,2,1,0:T(2,128)(2,1)} %bitcast.25) | data formatting | bytes 3145728
  54.2 0.1 pad_add_fusion.where
  54.3 0.0 copy-done
  54.3 2.3 %shard_map.101.total = f32[1024,512]{1,0:T(8,128)S(1)} custom-call(s32[2]{0:T(128)S(1)} %pad_add_fusion.where, bf16[384,1024]{1,0:T(8,128)(2,1)S(1)} %bitcast.22, bf16[384,1024]{1,0:T(8,128)(2,1)S(1)} %collective-permute-done.low, bf16[384,1024]{1,0:T(8,128)(2,1)S(1)} %collective-permute-done.1.high, bf16[1536,512]{1,0:T(8,128)(2,1)S(1)} %bitcast.18), custom_call_target="tpu_custom_call" | custom-call | flops 1207959552 | bytes 6291456 | tf_op jit(solution)/shard_map/pallas_call | solution.py:97
  56.7 6.4 %collective-permute-done.2.far_first = bf16[192,1024]{1,0:T(8,128)(2,1)S(1)} collective-permute-done((bf16[192,1024]{1,0:T(8,128)(2,1)S(1)}, bf16[192,1024]{1,0:T(8,128)(2,1)S(1)}, u32[]{:S(2)}, u32[]{:S(2)}) %collective-permute-start.2) | collective-permute-done | bytes 393248 | tf_op jit(solution)/shard_map/ppermute | solution.py:88
  63.0 1.6 collective-permute-done.3.far_second
  64.6 1.3 shard_map.102
  65.9 4.3 %collective-permute-start.4 = (bf16[32,16,512]{2,1,0:T(8,128)(2,1)S(1)}, bf16[32,16,512]{2,1,0:T(8,128)(2,1)S(1)}, u32[]{:S(2)}, u32[]{:S(2)}) collective-permute-start(bf16[32,16,512]{2,1,0:T(8,128)(2,1)S(1)} %get-tuple-element.8), channel_id=1, source_target_pairs={{0,8},{8,0},{1,9},{9,1},{2,10},{10,2},{3,11},{11,3},{4,12},{12,4},... | collective-permute-start | bytes 1572872 | tf_op jit(solution)/shard_map/ppermute | solution.py:121
  70.2 1.5 collective-permute-done.4
  71.7 0.0 copy-start.2
  71.7 0.0 copy-start.3
  71.7 0.0 copy-start.1
  71.7 1.0 add_convert_fusion
  72.7 17.0 %all-to-all-start = ((bf16[64,8,512]{2,1,0:T(8,128)(2,1)}), bf16[64,8,512]{2,1,0:T(8,128)(2,1)S(1)}, u32[]{:S(2)}, u32[]{:S(2)}) async-start(bf16[64,8,512]{2,1,0:T(8,128)(2,1)} %bitcast.3), calls=%async_computation | async-start | bytes 1048576 | tf_op jit(solution)/shard_map/all_to_all | solution.py:123
  89.7 0.0 copy-done.2
  89.7 0.0 copy-done.3
  89.7 0.0 copy-done.1
  89.8 0.0 copy-start.4
  89.8 15.9 %all-to-all-done = bf16[64,8,512]{2,1,0:T(8,128)(2,1)S(1)} async-done(((bf16[64,8,512]{2,1,0:T(8,128)(2,1)}), bf16[64,8,512]{2,1,0:T(8,128)(2,1)S(1)}, u32[]{:S(2)}, u32[]{:S(2)}) %all-to-all-start) | async-done | bytes 524320 | tf_op jit(solution)/shard_map/all_to_all | solution.py:123
  105.6 0.1 convert_reduce_fusion
  105.8 0.1 concatenate.4
  105.9 10.9 %all_to_all.21 = f32[4,20,256]{2,1,0:T(8,128)S(1)} all-to-all(f32[4,20,256]{2,1,0:T(8,128)S(1)} %concatenate.4), channel_id=1, replica_groups=mesh['x'=4,'y'=8,'core'=2,'tensor'=4,'replica'=2] {'tensor'}, dimensions={0} | all-to-all | bytes 163840 | tf_op jit(solution)/shard_map/all_to_all | solution.py:132
  116.8 0.1 broadcast_in_dim.13
  116.9 21.6 %all_to_all.22 = f32[128,1,256]{2,1,0:T(1,128)S(1)} all-to-all(f32[128,1,256]{2,1,0:T(1,128)S(1)} %broadcast_in_dim.13), channel_id=1, replica_groups=mesh['x'=4,'y'=8,'core'=2,'tensor'=4,'replica'=2] {'x','y','core','repli..., dimensions={0} | all-to-all | bytes 262144 | tf_op jit(solution)/shard_map/all_to_all | solution.py:137
  138.4 0.9 reduce_sum.39
  140.0 0.6 fusion.7
  140.7 20.0 %all_to_all.23 = bf16[64,2,8,256]{3,2,1,0:T(8,128)(2,1)S(1)} all-to-all(bf16[64,2,8,256]{3,2,1,0:T(8,128)(2,1)S(1)} %broadcast_in_dim.14), channel_id=1, replica_groups=mesh['x'=4,'y'=8,'core'=2,'tensor'=4,'replica'=2] {'x','y','replica'}, dimensions={0} | all-to-all | bytes 1048576 | tf_op jit(solution)/shard_map/all_to_all | solution.py:155
  160.7 4.7 %collective-permute-start.5 = (bf16[64,2,8,256]{3,2,1,0:T(8,128)(2,1)S(1)}, bf16[64,2,8,256]{3,2,1,0:T(8,128)(2,1)S(1)}, u32[]{:S(2)}, u32[]{:S(2)}) collective-permute-start(bf16[64,2,8,256]{3,2,1,0:T(8,128)(2,1)S(1)} %all_to_all.23), channel_id=1, source_target_pairs={{0,8},{8,0},{1,9},{9,1},{2,10},{10,2},{3,11},{11,3},{4,12},{12,4},... | collective-permute-start | bytes 1572872 | tf_op jit(solution)/shard_map/ppermute | solution.py:156
  165.5 0.0 copy-done.4
  165.5 0.6 multiply_add_fusion
  166.1 0.8 collective-permute-done.5
  167.0 0.1 broadcast_select_fusion.1
  167.0 0.1 maximum_bitcast_fusion
  167.1 1.1 copy.18
  (11 shorter events, 0.2 us)
Async XLA Ops:
  0.6 28.6 %collective-permute-start = (bf16[384,1024]{1,0:T(8,128)(2,1)}, bf16[384,1024]{1,0:T(8,128)(2,1)S(1)}, u32[]{:S(2)}, u32[]{:S(2)}) collective-permute-start(bf16[384,1024]{1,0:T(8,128)(2,1)} %bitcast.20), channel_id=1, source_target_pairs={{0,2},{2,4},{4,6},{6,0},{1,3},{3,5},{5,7},{7,1},{8,10},{10,12},{12... | collective-permute-start | bytes 2359304 | tf_op jit(solution)/shard_map/ppermute | solution.py:86
  7.3 40.4 %collective-permute-start.1 = (bf16[384,1024]{1,0:T(8,128)(2,1)}, bf16[384,1024]{1,0:T(8,128)(2,1)S(1)}, u32[]{:S(2)}, u32[]{:S(2)}) collective-permute-start(bf16[384,1024]{1,0:T(8,128)(2,1)} %bitcast.21), channel_id=1, source_target_pairs={{0,6},{2,0},{4,2},{6,4},{1,7},{3,1},{5,3},{7,5},{8,14},{10,8},{12,... | collective-permute-start | bytes 2359304 | tf_op jit(solution)/shard_map/ppermute | solution.py:87
  29.3 33.7 %collective-permute-start.2 = (bf16[192,1024]{1,0:T(8,128)(2,1)S(1)}, bf16[192,1024]{1,0:T(8,128)(2,1)S(1)}, u32[]{:S(2)}, u32[]{:S(2)}) collective-permute-start(bf16[192,1024]{1,0:T(8,128)(2,1)S(1)} %slice.13), channel_id=1, source_target_pairs={{0,2},{2,4},{4,6},{6,0},{1,3},{3,5},{5,7},{7,1},{8,10},{10,12},{12... | collective-permute-start | bytes 1179656 | tf_op jit(solution)/shard_map/ppermute | solution.py:88
  47.7 16.9 %collective-permute-start.3 = (bf16[192,1024]{1,0:T(8,128)(2,1)S(1)}, bf16[192,1024]{1,0:T(8,128)(2,1)S(1)}, u32[]{:S(2)}, u32[]{:S(2)}) collective-permute-start(bf16[192,1024]{1,0:T(8,128)(2,1)S(1)} %slice.14), channel_id=1, source_target_pairs={{0,6},{2,0},{4,2},{6,4},{1,7},{3,1},{5,3},{7,5},{8,14},{10,8},{12,... | collective-permute-start | bytes 1179656 | tf_op jit(solution)/shard_map/ppermute | solution.py:89
  52.4 1.9 %copy-start = (bf16[1,384,1024]{2,1,0:T(8,128)(2,1)S(1)}, bf16[1,384,1024]{2,1,0:T(8,128)(2,1)}, u32[]{:S(2)}) copy-start(bf16[1,384,1024]{2,1,0:T(8,128)(2,1)} %param.6) | copy-start | bytes 2359300
  65.9 5.8 %collective-permute-start.4 = (bf16[32,16,512]{2,1,0:T(8,128)(2,1)S(1)}, bf16[32,16,512]{2,1,0:T(8,128)(2,1)S(1)}, u32[]{:S(2)}, u32[]{:S(2)}) collective-permute-start(bf16[32,16,512]{2,1,0:T(8,128)(2,1)S(1)} %get-tuple-element.8), channel_id=1, source_target_pairs={{0,8},{8,0},{1,9},{9,1},{2,10},{10,2},{3,11},{11,3},{4,12},{12,4},... | collective-permute-start | bytes 1572872 | tf_op jit(solution)/shard_map/ppermute | solution.py:121
  71.7 18.0 %copy-start.2 = (f32[2,8,256]{2,1,0:T(8,128)S(1)}, f32[2,8,256]{2,1,0:T(8,128)}, u32[]{:S(2)}) copy-start(f32[2,8,256]{2,1,0:T(8,128)} %param.8) | copy-start | bytes 49156
  71.7 18.0 %copy-start.3 = (f32[2,8,256]{2,1,0:T(8,128)S(1)}, f32[2,8,256]{2,1,0:T(8,128)}, u32[]{:S(2)}) copy-start(f32[2,8,256]{2,1,0:T(8,128)} %param.9) | copy-start | bytes 49156
  71.7 18.0 %copy-start.1 = (f32[2,8,256]{2,1,0:T(8,128)S(1)}, f32[2,8,256]{2,1,0:T(8,128)}, u32[]{:S(2)}) copy-start(f32[2,8,256]{2,1,0:T(8,128)} %param.10) | copy-start | bytes 49156
  72.7 32.9 %all-to-all-start = ((bf16[64,8,512]{2,1,0:T(8,128)(2,1)}), bf16[64,8,512]{2,1,0:T(8,128)(2,1)S(1)}, u32[]{:S(2)}, u32[]{:S(2)}) async-start(bf16[64,8,512]{2,1,0:T(8,128)(2,1)} %bitcast.3), calls=%async_computation | async-start | bytes 1048576 | tf_op jit(solution)/shard_map/all_to_all | solution.py:123
  89.8 75.7 %copy-start.4 = (f32[1,1,4,1024]{3,2,1,0:T(4,128)S(1)}, f32[1,1,4,1024]{3,2,1,0:T(4,128)}, u32[]{:S(2)}) copy-start(f32[1,1,4,1024]{3,2,1,0:T(4,128)} %param.11) | copy-start | bytes 49156
  160.7 6.3 %collective-permute-start.5 = (bf16[64,2,8,256]{3,2,1,0:T(8,128)(2,1)S(1)}, bf16[64,2,8,256]{3,2,1,0:T(8,128)(2,1)S(1)}, u32[]{:S(2)}, u32[]{:S(2)}) collective-permute-start(bf16[64,2,8,256]{3,2,1,0:T(8,128)(2,1)S(1)} %all_to_all.23), channel_id=1, source_target_pairs={{0,8},{8,0},{1,9},{9,1},{2,10},{10,2},{3,11},{11,3},{4,12},{12,4},... | collective-permute-start | bytes 1572872 | tf_op jit(solution)/shard_map/ppermute | solution.py:156

commit v4 on v3

--- a/solution.py
+++ b/solution.py
@@ -16,7 +16,14 @@
 average_keep = 0.9
 
 XYR = ("x", "y", "replica")
+PLANE = ("x", "y")
 SWAP = ((0, 1), (1, 0))
+
+
+def gather_plane(block):
+    peers = lax.axis_size(PLANE)
+    spread = jnp.broadcast_to(block[None], (peers,) + block.shape)
+    return lax.all_to_all(spread, PLANE, 0, 0, tiled=True)
 
 
 def round_trip(count, step):
@@ -27,6 +34,19 @@
     return lax.dot_general(
         block, against, (((0,), (0,)), ((), ())), preferred_element_type=jnp.float32
     )
+
+
+def state_kernel(one, two, held, wide):
+    bf16 = jnp.bfloat16
+    peers, _, _, width = wide.shape
+    col_width = width // 2
+    for half in range(2):
+        master = held[half]
+        high = master.astype(bf16)
+        low = (master - high.astype(jnp.float32)).astype(bf16)
+        for k, block in enumerate((one[half].astype(bf16), two[half].astype(bf16), high, low)):
+            columns = slice(half * col_width, (half + 1) * col_width)
+            wide[:, k, :, columns] = jnp.broadcast_to(block[None], (peers,) + block.shape)
 
 
 def near_kernel(where, own, low, high, outgrad, total):
@@ -47,7 +67,7 @@
         )
 
 
-def far_kernel(where, total, far_first, far_second, outgrad, keep, give):
+def far_kernel(where, total, far_first, far_second, outgrad, _, keep, give):
     part = far_first.shape[0]
     start = lax.rem(where[0] + 2, outgrad.shape[0] // (2 * part)) * (2 * part)
     against = outgrad[pl.ds(pl.multiple_of(start, 2 * part), 2 * part), :]
@@ -76,24 +96,35 @@
     nt = lax.axis_size("tensor")
     peers = nx * ny * nr
     core = lax.axis_index("core")
+    twin = lax.axis_index("replica")
     place = lax.axis_index("tensor")
     where = jnp.stack([place, core]).astype(jnp.int32)
 
     tokens = features[0]
     count, dim_model = tokens.shape
     part = count // 2
+    width = 2 * col_width
     up, down = round_trip(nt, 1), round_trip(nt, nt - 1)
     low = lax.ppermute(tokens, "tensor", up)
     high = lax.ppermute(tokens, "tensor", down)
+
+    local = pl.BlockSpec(memory_space=pltpu.VMEM)
+    anywhere = pl.BlockSpec(memory_space=pl.ANY)
+    state = pl.pallas_call(
+        state_kernel,
+        out_shape=jax.ShapeDtypeStruct((nx * ny, 4, rows, width), bf16),
+        in_specs=[local] * 3,
+        out_specs=local,
+    )(moment_one, moment_two, master)
+    state = lax.all_to_all(state, PLANE, 0, 0, tiled=True)
+
     far_first = lax.ppermute(low[:part], "tensor", up)
     far_second = lax.ppermute(high[part:], "tensor", down)
     outgrad = cotangents[0].reshape(cotangents.shape[1], 2 * col_width)
 
-    width = 2 * col_width
     lines = nr * rows
     scalars = pl.BlockSpec(memory_space=pltpu.SMEM)
-    local = pl.BlockSpec(memory_space=pltpu.VMEM)
-    params = pltpu.CompilerParams(vmem_limit_bytes=24 * 2**20)
+    params = pltpu.CompilerParams(vmem_limit_bytes=4 * 2**20)
     total = pl.pallas_call(
         near_kernel,
         out_shape=jax.ShapeDtypeStruct((dim_model, width), f32),
@@ -110,31 +141,25 @@
             jax.ShapeDtypeStruct((nx * ny, lines, width), f32),
             jax.ShapeDtypeStruct((nx * ny, lines, width), bf16),
         ),
-        in_specs=[scalars] + [local] * 4,
+        in_specs=[scalars] + [local] * 4 + [anywhere],
         out_specs=(local, local),
         compiler_params=params,
         cost_estimate=pl.CostEstimate(
             flops=2 * count * dim_model * width, bytes_accessed=6 * 2**20, transcendentals=0
         ),
-    )(where, total, far_first, far_second, outgrad)
+    )(where, total, far_first, far_second, outgrad, state)
 
     got = lax.ppermute(give, "core", SWAP)
     half = (keep + got.astype(f32)).astype(bf16).reshape(peers, rows, width)
     terms = lax.all_to_all(half, XYR, split_axis=0, concat_axis=0, tiled=True)
-    grad_piece = jnp.sum(terms.astype(f32), axis=0).reshape(rows, 2, col_width)
-    gradient = jnp.transpose(grad_piece, (1, 0, 2))
-
-    held_rows = 2 * rows // nt
-    by_rows = lambda block: block.reshape(nt, held_rows, col_width)
-    flat = by_rows(gradient)
-    squares = jnp.broadcast_to(jnp.sum(flat * flat, axis=(0, 1)), flat.shape)
-    mixed = [flat, by_rows(moment_one), by_rows(moment_two), by_rows(master), squares]
-    mixed = lax.all_to_all(jnp.concatenate(mixed, axis=1), "tensor", 0, 0, tiled=True)
-    row_grad, row_one, row_two, row_held, squares = jnp.split(mixed, 5, axis=1)
-    squares = jnp.sum(squares[:, 0], axis=0)
-    others = ("x", "y", "core", "replica")
-    spread = jnp.broadcast_to(squares, (lax.axis_size(others), col_width))
-    squares = jnp.sum(lax.all_to_all(spread, others, 0, 0, tiled=True))
+    grad_lines = jnp.sum(terms.astype(f32), axis=0)
+    gradient = jnp.transpose(grad_lines.reshape(rows, 2, col_width), (1, 0, 2))
+
+    shared = gather_plane(grad_lines.astype(bf16)).astype(f32)
+    squares = jnp.sum(shared * shared, axis=(0, 1)).reshape(2, col_width).sum(axis=0)
+    others = ("core", "tensor", "replica")
+    squares = jnp.broadcast_to(squares, (lax.axis_size(others), col_width))
+    squares = jnp.sum(lax.all_to_all(squares, others, 0, 0, tiled=True))
     count_all = 2.0 * dim_model * dim_model
     clip_factor = 1.0 / jnp.sqrt(squares / count_all + 1e-06)
 
@@ -148,20 +173,20 @@
         direction = new_one / fix_one / (jnp.sqrt(new_two / fix_two) + adam_eps)
         return new_one, new_two, held - learn_rate * (direction + decay_rate * held)
 
+    wide = state.astype(f32)
+    mine = update(shared, wide[:, 0], wide[:, 1], wide[:, 2] + wide[:, 3])[2].astype(bf16)
+    other = lax.ppermute(mine, "replica", SWAP)
+    mine, other = jnp.where(twin == 0, mine, other), jnp.where(twin == 0, other, mine)
+    mine = jnp.stack([mine, other], axis=1)
+    other = lax.ppermute(mine, "core", SWAP)
+    mine, other = jnp.where(core == 0, mine, other), jnp.where(core == 0, other, mine)
+    both = jnp.stack([mine, other], axis=1).reshape(nx * ny, 2, nr, rows, 2, col_width)
+    weights = jnp.transpose(both, (4, 0, 1, 2, 3, 5)).reshape(2, dim_model, col_width)
+
     new_first, new_second, new_master = update(gradient, moment_one, moment_two, master)
-
-    mine = new_master.astype(bf16)
-    spread = jnp.broadcast_to(mine[None], (peers,) + mine.shape)
-    column = lax.all_to_all(spread, XYR, split_axis=0, concat_axis=0, tiled=True)
-    other = lax.ppermute(column, "core", SWAP)
-    even = jnp.where(core == 0, column, other)
-    odd = jnp.where(core == 0, other, column)
-    both = jnp.stack([even, odd]).reshape(2, nx * ny, nr, 2, rows, col_width)
-    weights = jnp.transpose(both, (3, 1, 0, 2, 4, 5)).reshape(2, dim_model, col_width)
-
-    row_master = update(row_grad, row_one, row_two, row_held)[2]
-    row_master = jnp.transpose(row_master, (1, 0, 2)).reshape(average.shape)
-    new_average = average_keep * average + (1.0 - average_keep) * row_master
+    flat_rows = new_master.reshape(2 * rows, col_width)
+    row_flat = lax.all_to_all(flat_rows, "tensor", split_axis=0, concat_axis=1, tiled=True)
+    new_average = average_keep * average + (1.0 - average_keep) * row_flat.reshape(average.shape)
     return (weights, new_first, new_second, new_master, new_average)
 
 

time: 169 us -> 180 us (1.065)
  waiting for transfers between devices: 41.4 us -> 61.8 us
  blocking collectives: 52.5 us -> 41.1 us
  starting transfers between devices: 62.4 us -> 54.8 us
  local copies, waits for them, and re-layouts: 3.21 us -> 10.7 us
  Pallas kernels: 3.65 us -> 6.15 us
    ppermute x1, waiting for transfers between devices: 0.01 us -> 31 us  [shards(): high = lax.ppermute(tokens, 'tensor', down)]
    ppermute x1, starting transfers between devices: 18.3 us -> 1.91 us  [shards(): far_first = lax.ppermute(low[:part], 'tensor', up)]
    ppermute x1, waiting for transfers between devices: 15.2 us -> 0.01 us  [shards(): low = lax.ppermute(tokens, 'tensor', up)]
    all_to_all x3 -> x2, blocking collectives: 52.5 us -> 41.1 us  [the longest x1 25.6 us: shards(): terms = lax.all_to_all(half, XYR, split_axis=0, concat_axis=0, tiled=True)]
    ppermute x1 -> x2, waiting for transfers between devices: 0.83 us -> 6.45 us  [the longest x1 6.45 us: shards(): other = lax.ppermute(mine, 'replica', SWAP)]
    unnamed x11 -> x23, local copies, waits for them, and re-layouts: 1.83 us -> 6.81 us
    ppermute x1, starting transfers between devices: 6.64 us -> 1.92 us  [shards(): low = lax.ppermute(tokens, 'tensor', up)]
    ppermute x1, starting transfers between devices: 6.77 us -> 10.7 us  [shards(): high = lax.ppermute(tokens, 'tensor', down)]
  transfers between devices with their start and end apart: 7 -> 10, of which waited for: 6 -> 7; matrix products, arithmetic and copies ran while one was open for 2% -> 3% of each run, Pallas kernels for 1% -> 1%
where the time goes in v4:
time: 180 us
  waiting for transfers between devices  61.8 us (34%)
  starting transfers between devices  54.8 us (30%)
  blocking collectives  41.1 us (23%)
  local copies, waits for them, and re-layouts  10.7 us (6%)
  Pallas kernels  6.15 us (3%)
  other arithmetic  3.34 us (2%)
    ppermute x1, waiting for transfers between devices, shards(): high = lax.ppermute(tokens, 'tensor', down)  31 us
    all_to_all x1, blocking collectives, shards(): terms = lax.all_to_all(half, XYR, split_axis=0, concat_axis=0, tiled=True)  25.6 us
    all_to_all x1, blocking collectives, gather_plane(): return lax.all_to_all(spread, PLANE, 0, 0, tiled=True)  15.5 us
    ppermute x1, starting transfers between devices, shards(): high = lax.ppermute(tokens, 'tensor', down)  10.7 us
    all_to_all x1, starting transfers between devices, shards(): state = lax.all_to_all(state, PLANE, 0, 0, tiled=True)  10.5 us
    ppermute x1, starting transfers between devices, shards(): got = lax.ppermute(give, 'core', SWAP)  7.16 us
    all_to_all x1, starting transfers between devices, shards(): squares = jnp.sum(lax.all_to_all(squares, others, 0, 0, tiled=True))  7 us
    unnamed x23, local copies, waits for them, and re-layouts  6.81 us
  transfers between devices with their start and end apart: 10, of which 7 were waited for; matrix products, arithmetic and copies ran while one was open for 3% of the time, Pallas kernels for 1%

profile of v4, /device:TPU:1, one launch (start us, length us, event | category | flops | bytes accessed | tf_op | source)
XLA Modules:
  0.0 179.6 jit_solution(14940746126861196221)
XLA Ops:
  0.6 0.0 copy-start.4
  0.6 1.9 %shard_map.101 = bf16[32,4,8,512]{3,2,1,0:T(8,128)(2,1)} custom-call(f32[2,8,256]{2,1,0:T(8,128)} %one.1, f32[2,8,256]{2,1,0:T(8,128)} %two.1, f32[2,8,256]{2,1,0:T(8,128)} %held.1), custom_call_target="tpu_custom_call" | custom-call | tf_op jit(solution)/shard_map/pallas_call | solution.py:113
  2.6 10.5 %all-to-all-start = ((bf16[32,4,8,512]{3,2,1,0:T(8,128)(2,1)}), bf16[32,4,8,512]{3,2,1,0:T(8,128)(2,1)S(1)}, u32[]{:S(2)}, u32[]{:S(2)}) async-start(bf16[32,4,8,512]{3,2,1,0:T(8,128)(2,1)} %shard_map.101), calls=%async_computation | async-start | bytes 2097152 | tf_op jit(solution)/shard_map/all_to_all | solution.py:119
  13.1 0.0 copy-done.4
  13.1 10.7 %collective-permute-start.1 = (bf16[384,1024]{1,0:T(8,128)(2,1)S(1)}, bf16[384,1024]{1,0:T(8,128)(2,1)S(1)}, u32[]{:S(2)}, u32[]{:S(2)}) collective-permute-start(bf16[384,1024]{1,0:T(8,128)(2,1)S(1)} %bitcast.73), channel_id=1, source_target_pairs={{0,6},{2,0},{4,2},{6,4},{1,7},{3,1},{5,3},{7,5},{8,14},{10,8},{12,... | collective-permute-start | bytes 2359304 | tf_op jit(solution)/shard_map/ppermute | solution.py:109
  23.7 1.9 %collective-permute-start = (bf16[384,1024]{1,0:T(8,128)(2,1)S(1)}, bf16[384,1024]{1,0:T(8,128)(2,1)S(1)}, u32[]{:S(2)}, u32[]{:S(2)}) collective-permute-start(bf16[384,1024]{1,0:T(8,128)(2,1)S(1)} %bitcast.74), channel_id=1, source_target_pairs={{0,2},{2,4},{4,6},{6,0},{1,3},{3,5},{5,7},{7,1},{8,10},{10,12},{12... | collective-permute-start | bytes 2359304 | tf_op jit(solution)/shard_map/ppermute | solution.py:108
  25.7 31.0 %collective-permute-done.1.high = bf16[384,1024]{1,0:T(8,128)(2,1)S(1)} collective-permute-done((bf16[384,1024]{1,0:T(8,128)(2,1)S(1)}, bf16[384,1024]{1,0:T(8,128)(2,1)S(1)}, u32[]{:S(2)}, u32[]{:S(2)}) %collective-permute-start.1) | collective-permute-done | bytes 786464 | tf_op jit(solution)/shard_map/ppermute | solution.py:109
  56.7 0.8 slice.28
  57.5 6.3 %collective-permute-start.3 = (bf16[192,1024]{1,0:T(8,128)(2,1)}, bf16[192,1024]{1,0:T(8,128)(2,1)}, u32[]{:S(2)}, u32[]{:S(2)}) collective-permute-start(bf16[192,1024]{1,0:T(8,128)(2,1)} %slice.28), channel_id=1, source_target_pairs={{0,6},{2,0},{4,2},{6,4},{1,7},{3,1},{5,3},{7,5},{8,14},{10,8},{12,... | collective-permute-start | bytes 1179656 | tf_op jit(solution)/shard_map/ppermute | solution.py:122
  63.8 0.0 collective-permute-done.low
  63.9 0.8 slice.27
  64.6 0.0 copy-start.2
  64.6 0.9 copy-done.2
  65.5 1.9 %collective-permute-start.2 = (bf16[192,1024]{1,0:T(8,128)(2,1)}, bf16[192,1024]{1,0:T(8,128)(2,1)}, u32[]{:S(2)}, u32[]{:S(2)}) collective-permute-start(bf16[192,1024]{1,0:T(8,128)(2,1)} %slice.27), channel_id=1, source_target_pairs={{0,2},{2,4},{4,6},{6,0},{1,3},{3,5},{5,7},{7,1},{8,10},{10,12},{12... | collective-permute-start | bytes 1179656 | tf_op jit(solution)/shard_map/ppermute | solution.py:121
  67.4 0.0 copy-start.3
  67.4 1.8 %copy.33 = bf16[192,8,2,256]{3,1,2,0:T(8,128)(2,1)S(1)} copy(bf16[192,8,2,256]{3,2,1,0:T(2,128)(2,1)} %bitcast.79) | data formatting | bytes 3145728
  69.3 0.1 pad_add_fusion.where
  69.3 0.0 copy-done.3
  69.3 0.0 copy-start.5
  69.3 1.1 copy-done.5
  70.5 2.4 %shard_map.102.total = f32[1024,512]{1,0:T(8,128)S(1)} custom-call(s32[2]{0:T(128)S(1)} %pad_add_fusion.where, bf16[384,1024]{1,0:T(8,128)(2,1)S(1)} %bitcast.75, bf16[384,1024]{1,0:T(8,128)(2,1)S(1)} %copy-done.3, bf16[384,1024]{1,0:T(8,128)(2,1)S(1)} %collective-permute-done.1.high, bf16[1536,512]{1,0:T(8,128)(2,1)S(1)} %bitcast.71), custom_call_target="tpu_custom_call" | custom-call | flops 1207959552 | bytes 6291456 | tf_op jit(solution)/shard_map/pallas_call | solution.py:128
  72.8 0.0 copy-start
  72.8 1.3 copy-done
  74.2 3.7 %collective-permute-done.3.far_second = bf16[192,1024]{1,0:T(8,128)(2,1)} collective-permute-done((bf16[192,1024]{1,0:T(8,128)(2,1)}, bf16[192,1024]{1,0:T(8,128)(2,1)}, u32[]{:S(2)}, u32[]{:S(2)}) %collective-permute-start.3) | collective-permute-done | bytes 393248 | tf_op jit(solution)/shard_map/ppermute | solution.py:122
  77.9 5.8 %collective-permute-done.2.far_first = bf16[192,1024]{1,0:T(8,128)(2,1)} collective-permute-done((bf16[192,1024]{1,0:T(8,128)(2,1)}, bf16[192,1024]{1,0:T(8,128)(2,1)}, u32[]{:S(2)}, u32[]{:S(2)}) %collective-permute-start.2) | collective-permute-done | bytes 393248 | tf_op jit(solution)/shard_map/ppermute | solution.py:121
  83.7 0.0 all-to-all-done._
  83.7 0.0 copy-start.1
  83.7 1.6 copy-done.1
  85.3 1.9 %shard_map.103 = (f32[32,16,512]{2,1,0:T(8,128)S(1)}, bf16[32,16,512]{2,1,0:T(8,128)(2,1)S(1)}) custom-call(s32[2]{0:T(128)S(1)} %pad_add_fusion.where, f32[1024,512]{1,0:T(8,128)S(1)} %copy-done.1, bf16[192,1024]{1,0:T(8,128)(2,1)} %collective-permute-done.2.far_first, bf16[192,1024]{1,0:T(8,128)(2,1)} %collective-permute-done.3.far_second, ...), custom_call_target="tpu_custom_call" | custom-call | flops 402653184 | bytes 6291456 | tf_op jit(solution)/shard_map/pallas_call | solution.py:138
  87.2 7.2 %collective-permute-start.4 = (bf16[32,16,512]{2,1,0:T(8,128)(2,1)S(1)}, bf16[32,16,512]{2,1,0:T(8,128)(2,1)S(1)}, u32[]{:S(2)}, u32[]{:S(2)}) collective-permute-start(bf16[32,16,512]{2,1,0:T(8,128)(2,1)S(1)} %get-tuple-element.8), channel_id=1, source_target_pairs={{0,8},{8,0},{1,9},{9,1},{2,10},{10,2},{3,11},{11,3},{4,12},{12,4},... | collective-permute-start | bytes 1572872 | tf_op jit(solution)/shard_map/ppermute | solution.py:152
  94.4 1.5 collective-permute-done.4
  95.9 0.2 add_convert_fusion
  96.1 25.6 %all_to_all.34 = bf16[64,8,512]{2,1,0:T(8,128)(2,1)S(1)} all-to-all(bf16[64,8,512]{2,1,0:T(8,128)(2,1)S(1)} %bitcast.78), channel_id=1, replica_groups=mesh['x'=4,'y'=8,'core'=2,'tensor'=4,'replica'=2] {'x','y','replica'}, dimensions={0} | all-to-all | bytes 1048576 | tf_op jit(solution)/shard_map/all_to_all | solution.py:154
  121.7 0.1 convert_reduce_fusion
  121.8 15.5 %all_to_all.35 = bf16[32,8,512]{2,1,0:T(8,128)(2,1)S(1)} all-to-all(bf16[32,8,512]{2,1,0:T(8,128)(2,1)S(1)} %broadcast_in_dim.4), channel_id=1, replica_groups=mesh['x'=4,'y'=8,'core'=2,'tensor'=4,'replica'=2] {'x','y'}, dimensions={0} | all-to-all | bytes 524288 | tf_op jit(solution)/shard_map/all_to_all | solution.py:26
  137.3 0.1 fusion.13
  137.4 0.6 broadcast_in_dim.10
  138.1 7.0 %all-to-all-start.3 = ((f32[16,1,256]{2,1,0:T(1,128)}), f32[16,1,256]{2,1,0:T(1,128)S(1)}, u32[]{:S(2)}, u32[]{:S(2)}) async-start(f32[16,1,256]{2,1,0:T(1,128)} %broadcast_in_dim.10), calls=%async_computation.3 | async-start | bytes 32768 | tf_op jit(solution)/shard_map/all_to_all | solution.py:162
  145.1 0.3 convert_element_type.25
  145.3 6.7 %all-to-all-done.3 = f32[16,1,256]{2,1,0:T(1,128)S(1)} async-done(((f32[16,1,256]{2,1,0:T(1,128)}), f32[16,1,256]{2,1,0:T(1,128)S(1)}, u32[]{:S(2)}, u32[]{:S(2)}) %all-to-all-start.3) | async-done | bytes 16416 | tf_op jit(solution)/shard_map/all_to_all | solution.py:162
  152.0 0.6 reduce_sum.39
  153.4 0.0 copy-start.6
  153.4 0.0 copy-start.7
  153.4 0.0 copy-start.8
  153.4 0.0 copy-start.10
  153.4 0.5 fusion.19
  153.9 2.5 %collective-permute-start.5 = (bf16[32,8,512]{2,1,0:T(8,128)(2,1)S(1)}, bf16[32,8,512]{2,1,0:T(8,128)(2,1)S(1)}, u32[]{:S(2)}, u32[]{:S(2)}) collective-permute-start(bf16[32,8,512]{2,1,0:T(8,128)(2,1)S(1)} %fusion.19), channel_id=1, source_target_pairs={{0,1},{1,0},{2,3},{3,2},{4,5},{5,4},{6,7},{7,6},{8,9},{9,8},{10,11... | collective-permute-start | bytes 786440 | tf_op jit(solution)/shard_map/ppermute | solution.py:178
  156.5 6.5 %collective-permute-done.5 = bf16[32,8,512]{2,1,0:T(8,128)(2,1)S(1)} collective-permute-done((bf16[32,8,512]{2,1,0:T(8,128)(2,1)S(1)}, bf16[32,8,512]{2,1,0:T(8,128)(2,1)S(1)}, u32[]{:S(2)}, u32[]{:S(2)}) %collective-permute-start.5) | collective-permute-done | bytes 262176 | tf_op jit(solution)/shard_map/ppermute | solution.py:178
  162.9 0.1 pad_maximum_fusion
  163.0 3.5 %collective-permute-start.6 = (bf16[32,2,8,512]{3,2,0,1:T(8,128)(2,1)S(1)}, bf16[32,2,8,512]{3,2,0,1:T(8,128)(2,1)S(1)}, u32[]{:S(2)}, u32[]{:S(2)}) collective-permute-start(bf16[32,2,8,512]{3,2,0,1:T(8,128)(2,1)S(1)} %pad_maximum_fusion), channel_id=1, source_target_pairs={{0,8},{8,0},{1,9},{9,1},{2,10},{10,2},{3,11},{11,3},{4,12},{12,4},... | collective-permute-start | bytes 1572872 | tf_op jit(solution)/shard_map/ppermute | solution.py:181
  166.5 0.0 copy-done.6
  166.5 0.0 copy-done.7
  166.5 0.0 copy-done.8
  166.5 0.6 multiply_subtract_fusion
  167.2 0.6 all_to_all.27
  167.8 3.3 %all-to-all-start.4 = ((f32[4,4,256]{2,1,0:T(4,128)}), f32[4,4,256]{2,1,0:T(4,128)S(1)}, u32[]{:S(2)}, u32[]{:S(2)}) async-start(f32[4,4,256]{2,1,0:T(4,128)} %all_to_all.27), calls=%async_computation.4 | async-start | bytes 32768 | tf_op jit(solution)/shard_map/all_to_all | solution.py:188
  171.0 6.6 %all-to-all-done.4 = f32[4,4,256]{2,1,0:T(4,128)S(1)} async-done(((f32[4,4,256]{2,1,0:T(4,128)}), f32[4,4,256]{2,1,0:T(4,128)S(1)}, u32[]{:S(2)}, u32[]{:S(2)}) %all-to-all-start.4) | async-done | bytes 16416 | tf_op jit(solution)/shard_map/all_to_all | solution.py:188
  177.6 0.0 copy-done.10
  177.6 0.6 multiply_add_fusion
  178.3 0.0 collective-permute-done.6
  178.3 0.1 broadcast_select_fusion.1
  178.3 0.1 maximum_bitcast_fusion
  178.4 0.0 copy-done.9
  178.5 1.1 copy.28
  (8 shorter events, 0.1 us)
Async XLA Ops:
  0.6 12.4 %copy-start.4 = (bf16[1,384,1024]{2,1,0:T(8,128)(2,1)S(1)}, bf16[1,384,1024]{2,1,0:T(8,128)(2,1)}, u32[]{:S(2)}) copy-start(bf16[1,384,1024]{2,1,0:T(8,128)(2,1)} %param.6) | copy-start | bytes 2359300
  2.6 81.2 %all-to-all-start = ((bf16[32,4,8,512]{3,2,1,0:T(8,128)(2,1)}), bf16[32,4,8,512]{3,2,1,0:T(8,128)(2,1)S(1)}, u32[]{:S(2)}, u32[]{:S(2)}) async-start(bf16[32,4,8,512]{3,2,1,0:T(8,128)(2,1)} %shard_map.101), calls=%async_computation | async-start | bytes 2097152 | tf_op jit(solution)/shard_map/all_to_all | solution.py:119
  13.1 43.6 %collective-permute-start.1 = (bf16[384,1024]{1,0:T(8,128)(2,1)S(1)}, bf16[384,1024]{1,0:T(8,128)(2,1)S(1)}, u32[]{:S(2)}, u32[]{:S(2)}) collective-permute-start(bf16[384,1024]{1,0:T(8,128)(2,1)S(1)} %bitcast.73), channel_id=1, source_target_pairs={{0,6},{2,0},{4,2},{6,4},{1,7},{3,1},{5,3},{7,5},{8,14},{10,8},{12,... | collective-permute-start | bytes 2359304 | tf_op jit(solution)/shard_map/ppermute | solution.py:109
  23.7 40.1 %collective-permute-start = (bf16[384,1024]{1,0:T(8,128)(2,1)S(1)}, bf16[384,1024]{1,0:T(8,128)(2,1)S(1)}, u32[]{:S(2)}, u32[]{:S(2)}) collective-permute-start(bf16[384,1024]{1,0:T(8,128)(2,1)S(1)} %bitcast.74), channel_id=1, source_target_pairs={{0,2},{2,4},{4,6},{6,0},{1,3},{3,5},{5,7},{7,1},{8,10},{10,12},{12... | collective-permute-start | bytes 2359304 | tf_op jit(solution)/shard_map/ppermute | solution.py:108
  57.5 20.4 %collective-permute-start.3 = (bf16[192,1024]{1,0:T(8,128)(2,1)}, bf16[192,1024]{1,0:T(8,128)(2,1)}, u32[]{:S(2)}, u32[]{:S(2)}) collective-permute-start(bf16[192,1024]{1,0:T(8,128)(2,1)} %slice.28), channel_id=1, source_target_pairs={{0,6},{2,0},{4,2},{6,4},{1,7},{3,1},{5,3},{7,5},{8,14},{10,8},{12,... | collective-permute-start | bytes 1179656 | tf_op jit(solution)/shard_map/ppermute | solution.py:122
  64.6 0.9 copy-start.2
  65.5 18.2 %collective-permute-start.2 = (bf16[192,1024]{1,0:T(8,128)(2,1)}, bf16[192,1024]{1,0:T(8,128)(2,1)}, u32[]{:S(2)}, u32[]{:S(2)}) collective-permute-start(bf16[192,1024]{1,0:T(8,128)(2,1)} %slice.27), channel_id=1, source_target_pairs={{0,2},{2,4},{4,6},{6,0},{1,3},{3,5},{5,7},{7,1},{8,10},{10,12},{12... | collective-permute-start | bytes 1179656 | tf_op jit(solution)/shard_map/ppermute | solution.py:121
  67.4 1.9 %copy-start.3 = (bf16[384,1024]{1,0:T(8,128)(2,1)S(1)}, bf16[384,1024]{1,0:T(8,128)(2,1)}, u32[]{:S(2)}) copy-start(bf16[384,1024]{1,0:T(8,128)(2,1)} %copy-done.2) | copy-start | bytes 2359300
  69.3 1.1 copy-start.5
  72.8 1.3 copy-start
  83.7 1.6 copy-start.1
  87.2 8.7 %collective-permute-start.4 = (bf16[32,16,512]{2,1,0:T(8,128)(2,1)S(1)}, bf16[32,16,512]{2,1,0:T(8,128)(2,1)S(1)}, u32[]{:S(2)}, u32[]{:S(2)}) collective-permute-start(bf16[32,16,512]{2,1,0:T(8,128)(2,1)S(1)} %get-tuple-element.8), channel_id=1, source_target_pairs={{0,8},{8,0},{1,9},{9,1},{2,10},{10,2},{3,11},{11,3},{4,12},{12,4},... | collective-permute-start | bytes 1572872 | tf_op jit(solution)/shard_map/ppermute | solution.py:152
  138.1 14.0 %all-to-all-start.3 = ((f32[16,1,256]{2,1,0:T(1,128)}), f32[16,1,256]{2,1,0:T(1,128)S(1)}, u32[]{:S(2)}, u32[]{:S(2)}) async-start(f32[16,1,256]{2,1,0:T(1,128)} %broadcast_in_dim.10), calls=%async_computation.3 | async-start | bytes 32768 | tf_op jit(solution)/shard_map/all_to_all | solution.py:162
  153.4 13.2 %copy-start.6 = (f32[2,8,256]{2,1,0:T(8,128)S(1)}, f32[2,8,256]{2,1,0:T(8,128)}, u32[]{:S(2)}) copy-start(f32[2,8,256]{2,1,0:T(8,128)} %one.1) | copy-start | bytes 49156
  153.4 13.2 %copy-start.7 = (f32[2,8,256]{2,1,0:T(8,128)S(1)}, f32[2,8,256]{2,1,0:T(8,128)}, u32[]{:S(2)}) copy-start(f32[2,8,256]{2,1,0:T(8,128)} %two.1) | copy-start | bytes 49156
  153.4 13.2 %copy-start.8 = (f32[2,8,256]{2,1,0:T(8,128)S(1)}, f32[2,8,256]{2,1,0:T(8,128)}, u32[]{:S(2)}) copy-start(f32[2,8,256]{2,1,0:T(8,128)} %held.1) | copy-start | bytes 49156
  153.4 24.2 %copy-start.10 = (f32[1,1,4,1024]{3,2,1,0:T(4,128)S(1)}, f32[1,1,4,1024]{3,2,1,0:T(4,128)}, u32[]{:S(2)}) copy-start(f32[1,1,4,1024]{3,2,1,0:T(4,128)} %param.11) | copy-start | bytes 49156
  153.9 9.0 %collective-permute-start.5 = (bf16[32,8,512]{2,1,0:T(8,128)(2,1)S(1)}, bf16[32,8,512]{2,1,0:T(8,128)(2,1)S(1)}, u32[]{:S(2)}, u32[]{:S(2)}) collective-permute-start(bf16[32,8,512]{2,1,0:T(8,128)(2,1)S(1)} %fusion.19), channel_id=1, source_target_pairs={{0,1},{1,0},{2,3},{3,2},{4,5},{5,4},{6,7},{7,6},{8,9},{9,8},{10,11... | collective-permute-start | bytes 786440 | tf_op jit(solution)/shard_map/ppermute | solution.py:178
  163.0 15.3 %collective-permute-start.6 = (bf16[32,2,8,512]{3,2,0,1:T(8,128)(2,1)S(1)}, bf16[32,2,8,512]{3,2,0,1:T(8,128)(2,1)S(1)}, u32[]{:S(2)}, u32[]{:S(2)}) collective-permute-start(bf16[32,2,8,512]{3,2,0,1:T(8,128)(2,1)S(1)} %pad_maximum_fusion), channel_id=1, source_target_pairs={{0,8},{8,0},{1,9},{9,1},{2,10},{10,2},{3,11},{11,3},{4,12},{12,4},... | collective-permute-start | bytes 1572872 | tf_op jit(solution)/shard_map/ppermute | solution.py:181
  167.2 11.3 %copy-start.9 = (f32[2,8,256]{2,1,0:T(8,128)}, f32[2,8,256]{2,1,0:T(8,128)S(1)}, u32[]{:S(2)}) copy-start(f32[2,8,256]{2,1,0:T(8,128)S(1)} %get-tuple-element.9) | copy-start | bytes 49156
  167.8 9.9 %all-to-all-start.4 = ((f32[4,4,256]{2,1,0:T(4,128)}), f32[4,4,256]{2,1,0:T(4,128)S(1)}, u32[]{:S(2)}, u32[]{:S(2)}) async-start(f32[4,4,256]{2,1,0:T(4,128)} %all_to_all.27), calls=%async_computation.4 | async-start | bytes 32768 | tf_op jit(solution)/shard_map/all_to_all | solution.py:188

commit v5 on v3

--- a/solution.py
+++ b/solution.py
@@ -29,8 +29,8 @@
     )
 
 
-def near_kernel(where, own, low, high, outgrad, total):
-    count = own.shape[0]
+def near_kernel(where, own, low_first, low_second, high_first, high_second, outgrad, total):
+    count, part = own.shape[0], low_first.shape[0]
     shards_all = outgrad.shape[0] // count
     tile = 256
 
@@ -39,11 +39,14 @@
         return outgrad[pl.ds(pl.multiple_of(start, count), count), :]
 
     for left in range(0, own.shape[1], tile):
-        part = slice(left, left + tile)
-        total[part, :] = (
-            along_tokens(own[:, part], against(0))
-            + along_tokens(low[:, part], against(shards_all - 1))
-            + along_tokens(high[:, part], against(1))
+        cut = slice(left, left + tile)
+        below, above = against(shards_all - 1), against(1)
+        total[cut, :] = (
+            along_tokens(own[:, cut], against(0))
+            + along_tokens(low_first[:, cut], below[:part])
+            + along_tokens(low_second[:, cut], below[part:])
+            + along_tokens(high_first[:, cut], above[:part])
+            + along_tokens(high_second[:, cut], above[part:])
         )
 
 
@@ -68,6 +71,73 @@
         give[out] = jnp.where(first_core, odd, even).astype(give.dtype)
 
 
+def own_kernel(
+    where, lines, sums, one, two, held, new_one, new_two, new_held, spread, *lent
+):
+    halves, rows, width = one.shape
+    peers = spread.shape[0]
+    count_all = 2.0 * (width * len(lent)) ** 2
+    total = jnp.sum(sums[...], axis=(0, 1), keepdims=True)[0]
+    total = jnp.sum(total, axis=1, keepdims=True)
+    clip_factor = 1.0 / jnp.sqrt(total / count_all + 1e-06)
+    fix_one = 1.0 - beta_one**STEP
+    fix_two = 1.0 - beta_two**STEP
+    blocks = []
+    for half in range(halves):
+        scaled = clip_factor * lines[:, half * width : (half + 1) * width]
+        first = beta_one * one[half] + (1.0 - beta_one) * scaled
+        second = beta_two * two[half] + (1.0 - beta_two) * (scaled * scaled)
+        direction = first / fix_one / (jnp.sqrt(second / fix_two) + adam_eps)
+        master = held[half] - learn_rate * (direction + decay_rate * held[half])
+        new_one[half] = first
+        new_two[half] = second
+        new_held[half] = master
+        copy = master.astype(spread.dtype)
+        spread[:, half] = jnp.broadcast_to(copy[None], (peers, rows, width))
+        count = halves * rows // len(lent)
+        blocks += [master[row : row + count] for row in range(0, rows, count)]
+    for step, ref in enumerate(lent):
+        target = lax.rem(where[0] + step, len(lent))
+        chosen = blocks[0]
+        for k in range(1, len(lent)):
+            chosen = jnp.where(target == k, blocks[k], chosen)
+        ref[...] = chosen
+
+
+def average_kernel(where, average, *refs):
+    *lent, out = refs
+    shards_all = len(lent)
+    width = lent[0].shape[1]
+    for source in range(shards_all):
+        step = lax.rem(where[0] + shards_all - source, shards_all)
+        chosen = lent[0][...]
+        for k in range(1, shards_all):
+            chosen = jnp.where(step == k, lent[k][...], chosen)
+        columns = slice(source * width, (source + 1) * width)
+        kept = average_keep * average[0, 0, :, columns]
+        out[0, 0, :, columns] = kept + (1.0 - average_keep) * chosen
+
+
+def weights_kernel(where, column, other, weights):
+    peers, halves, rows, width = column.shape
+    lines = weights.shape[1] // peers
+    core = where[1]
+
+    def place(ref, pair, half, start):
+        pieces = ref[pl.ds(2 * pair, 2), half].astype(jnp.float32)
+        pieces = pieces.reshape(2 * rows, width).astype(weights.dtype)
+        start = pl.multiple_of(start, 2 * rows)
+        weights[half, pl.ds(start, 2 * rows), :] = pieces
+
+    def step(pair, carry):
+        for half in range(halves):
+            place(column, pair, half, (2 * pair + core) * 2 * rows)
+            place(other, pair, half, (2 * pair + 1 - core) * 2 * rows)
+        return carry
+
+    lax.fori_loop(0, peers // 2, step, 0, unroll=8)
+
+
 def shards(features, cotangents, moment_one, moment_two, master, average):
     f32, bf16 = jnp.float32, jnp.bfloat16
     col_width = cotangents.shape[3]
@@ -82,11 +152,14 @@
     tokens = features[0]
     count, dim_model = tokens.shape
     part = count // 2
+    first, second = tokens[:part], tokens[part:]
     up, down = round_trip(nt, 1), round_trip(nt, nt - 1)
-    low = lax.ppermute(tokens, "tensor", up)
-    high = lax.ppermute(tokens, "tensor", down)
-    far_first = lax.ppermute(low[:part], "tensor", up)
-    far_second = lax.ppermute(high[part:], "tensor", down)
+    low_first = lax.ppermute(first, "tensor", up)
+    high_second = lax.ppermute(second, "tensor", down)
+    low_second = lax.ppermute(second, "tensor", up)
+    high_first = lax.ppermute(first, "tensor", down)
+    far_first = lax.ppermute(low_first, "tensor", up)
+    far_second = lax.ppermute(high_second, "tensor", down)
     outgrad = cotangents[0].reshape(cotangents.shape[1], 2 * col_width)
 
     width = 2 * col_width
@@ -97,13 +170,13 @@
     total = pl.pallas_call(
         near_kernel,
         out_shape=jax.ShapeDtypeStruct((dim_model, width), f32),
-        in_specs=[scalars] + [local] * 4,
+        in_specs=[scalars] + [local] * 6,
         out_specs=local,
         compiler_params=params,
         cost_estimate=pl.CostEstimate(
             flops=6 * count * dim_model * width, bytes_accessed=6 * 2**20, transcendentals=0
         ),
-    )(where, tokens, low, high, outgrad)
+    )(where, tokens, low_first, low_second, high_first, high_second, outgrad)
     keep, give = pl.pallas_call(
         far_kernel,
         out_shape=(
@@ -121,47 +194,45 @@
     got = lax.ppermute(give, "core", SWAP)
     half = (keep + got.astype(f32)).astype(bf16).reshape(peers, rows, width)
     terms = lax.all_to_all(half, XYR, split_axis=0, concat_axis=0, tiled=True)
-    grad_piece = jnp.sum(terms.astype(f32), axis=0).reshape(rows, 2, col_width)
-    gradient = jnp.transpose(grad_piece, (1, 0, 2))
+    grad_lines = jnp.sum(terms.astype(f32), axis=0)
+    gradient = grad_lines.reshape(rows, 2, col_width)
+
+    squares = jnp.sum(gradient * gradient, axis=(0, 1))
+    for names in (("x", "core", "replica"), ("y", "tensor")):
+        spread = jnp.broadcast_to(squares, (lax.axis_size(names), 1, col_width))
+        spread = lax.all_to_all(spread, names, 0, 0, tiled=True)
+        squares = jnp.sum(spread, axis=(0, 1))
 
     held_rows = 2 * rows // nt
-    by_rows = lambda block: block.reshape(nt, held_rows, col_width)
-    flat = by_rows(gradient)
-    squares = jnp.broadcast_to(jnp.sum(flat * flat, axis=(0, 1)), flat.shape)
-    mixed = [flat, by_rows(moment_one), by_rows(moment_two), by_rows(master), squares]
-    mixed = lax.all_to_all(jnp.concatenate(mixed, axis=1), "tensor", 0, 0, tiled=True)
-    row_grad, row_one, row_two, row_held, squares = jnp.split(mixed, 5, axis=1)
-    squares = jnp.sum(squares[:, 0], axis=0)
-    others = ("x", "y", "core", "replica")
-    spread = jnp.broadcast_to(squares, (lax.axis_size(others), col_width))
-    squares = jnp.sum(lax.all_to_all(spread, others, 0, 0, tiled=True))
-    count_all = 2.0 * dim_model * dim_model
-    clip_factor = 1.0 / jnp.sqrt(squares / count_all + 1e-06)
-
-    fix_one = 1.0 - beta_one**STEP
-    fix_two = 1.0 - beta_two**STEP
-
-    def update(grad, one, two, held):
-        scaled = clip_factor * grad
-        new_one = beta_one * one + (1.0 - beta_one) * scaled
-        new_two = beta_two * two + (1.0 - beta_two) * (scaled * scaled)
-        direction = new_one / fix_one / (jnp.sqrt(new_two / fix_two) + adam_eps)
-        return new_one, new_two, held - learn_rate * (direction + decay_rate * held)
-
-    new_first, new_second, new_master = update(gradient, moment_one, moment_two, master)
-
-    mine = new_master.astype(bf16)
-    spread = jnp.broadcast_to(mine[None], (peers,) + mine.shape)
+    piece = jax.ShapeDtypeStruct(moment_one.shape, f32)
+    line = jax.ShapeDtypeStruct((held_rows, col_width), f32)
+    new_first, new_second, new_master, spread, *lent = pl.pallas_call(
+        own_kernel,
+        out_shape=(piece, piece, piece)
+        + (jax.ShapeDtypeStruct((peers,) + moment_one.shape, bf16),)
+        + (line,) * nt,
+        in_specs=[scalars] + [local] * 5,
+        out_specs=(local,) * (4 + nt),
+    )(where, grad_lines, spread, moment_one, moment_two, master)
+
     column = lax.all_to_all(spread, XYR, split_axis=0, concat_axis=0, tiled=True)
+    for step in range(1, nt):
+        lent[step] = lax.ppermute(lent[step], "tensor", round_trip(nt, step))
+    column, lent = lax.optimization_barrier((column, lent))
+    new_average = pl.pallas_call(
+        average_kernel,
+        out_shape=jax.ShapeDtypeStruct(average.shape, f32),
+        in_specs=[scalars] + [local] * (1 + nt),
+        out_specs=local,
+    )(where, average, *lent)
     other = lax.ppermute(column, "core", SWAP)
-    even = jnp.where(core == 0, column, other)
-    odd = jnp.where(core == 0, other, column)
-    both = jnp.stack([even, odd]).reshape(2, nx * ny, nr, 2, rows, col_width)
-    weights = jnp.transpose(both, (3, 1, 0, 2, 4, 5)).reshape(2, dim_model, col_width)
-
-    row_master = update(row_grad, row_one, row_two, row_held)[2]
-    row_master = jnp.transpose(row_master, (1, 0, 2)).reshape(average.shape)
-    new_average = average_keep * average + (1.0 - average_keep) * row_master
+    weights = pl.pallas_call(
+        weights_kernel,
+        out_shape=jax.ShapeDtypeStruct((2, dim_model, col_width), bf16),
+        in_specs=[scalars, local, local],
+        out_specs=local,
+        compiler_params=params,
+    )(where, column, other)
     return (weights, new_first, new_second, new_master, new_average)
 
 

time: 169 us -> 161 us (0.953)
  starting transfers between devices: 62.4 us -> 52.8 us
  Pallas kernels: 3.65 us -> 8.52 us
  other arithmetic: 3.53 us -> 0.43 us
    ppermute x4 -> x9, waiting for transfers between devices: 23.2 us -> 37 us  [the longest x1 12.9 us: shards(): far_second = lax.ppermute(high_second, 'tensor', down)]
    all_to_all x1, waiting for transfers between devices: 15.9 us -> 2.15 us  [shards(): lax.all_to_all(spread, XYR, split_axis=0, concat_axis=0, tiled=True)]
    all_to_all x1, starting transfers between devices: 17 us -> 4.63 us  [shards(): lax.all_to_all(spread, XYR, split_axis=0, concat_axis=0, tiled=True)]
    pallas_call x0 -> x3, Pallas kernels: none -> 4.84 us  [the longest x1 1.8 us: shards(): pl.pallas_call(own_kernel, out_shape=(piece, piece, piece) + (jax.ShapeDt...]
    ppermute x4 -> x9, starting transfers between devices: 36.5 us -> 39.2 us  [the longest x1 11.5 us: shards(): high_second = lax.ppermute(second, 'tensor', down)]
  transfers between devices with their start and end apart: 7 -> 12, of which waited for: 6 -> 8; matrix products, arithmetic and copies ran while one was open for 2% -> 1% of each run, Pallas kernels for 1% -> 2%
where the time goes in v5:
time: 161 us; the launch traced here: 160 us
  blocking collectives  53.8 us (33%)
  starting transfers between devices  52.8 us (33%)
  waiting for transfers between devices  40.8 us (25%)
  Pallas kernels  8.52 us (5%)
  local copies, waits for them, and re-layouts  3.06 us (2%)
    all_to_all x2, blocking collectives, shards(): spread = lax.all_to_all(spread, names, 0, 0, tiled=True)  27.7 us
    all_to_all x1, blocking collectives, shards(): terms = lax.all_to_all(half, XYR, split_axis=0, concat_axis=0, tiled=True)  26.1 us
    ppermute x1, waiting for transfers between devices, shards(): far_second = lax.ppermute(high_second, 'tensor', down)  12.9 us
    ppermute x1, starting transfers between devices, shards(): high_second = lax.ppermute(second, 'tensor', down)  11.5 us
    ppermute x3, starting transfers between devices, shards(): lent[step] = lax.ppermute(lent[step], 'tensor', round_trip(nt, step))  10.1 us
    ppermute x1, waiting for transfers between devices, shards(): high_second = lax.ppermute(second, 'tensor', down)  7.53 us
    ppermute x1, waiting for transfers between devices, shards(): high_first = lax.ppermute(first, 'tensor', down)  7.52 us
    ppermute x1, waiting for transfers between devices, shards(): far_first = lax.ppermute(low_first, 'tensor', up)  6.39 us
  transfers between devices with their start and end apart: 12, of which 8 were waited for; matrix products, arithmetic and copies ran while one was open for 1% of the time, Pallas kernels for 2%

profile of v5, /device:TPU:1, one launch (start us, length us, event | category | flops | bytes accessed | tf_op | source)
XLA Modules:
  0.0 160.2 jit_solution(11344623236386764582)
XLA Ops:
  0.6 1.2 slice_bitcast_fusion
  1.8 11.5 %collective-permute-start.3 = (bf16[192,1024]{1,0:T(8,128)(2,1)S(1)}, bf16[192,1024]{1,0:T(8,128)(2,1)S(1)}, u32[]{:S(2)}, u32[]{:S(2)}) collective-permute-start(bf16[192,1024]{1,0:T(8,128)(2,1)S(1)} %get-tuple-element.35), channel_id=1, source_target_pairs={{0,6},{2,0},{4,2},{6,4},{1,7},{3,1},{5,3},{7,5},{8,14},{10,8},{12,... | collective-permute-start | bytes 1179656 | tf_op jit(solution)/shard_map/ppermute | solution.py:158
  13.3 1.9 %collective-permute-start = (bf16[192,1024]{1,0:T(8,128)(2,1)S(1)}, bf16[192,1024]{1,0:T(8,128)(2,1)S(1)}, u32[]{:S(2)}, u32[]{:S(2)}) collective-permute-start(bf16[192,1024]{1,0:T(8,128)(2,1)S(1)} %get-tuple-element.36), channel_id=1, source_target_pairs={{0,2},{2,4},{4,6},{6,0},{1,3},{3,5},{5,7},{7,1},{8,10},{10,12},{12... | collective-permute-start | bytes 1179656 | tf_op jit(solution)/shard_map/ppermute | solution.py:157
  15.2 2.2 %collective-permute-start.1 = (bf16[192,1024]{1,0:T(8,128)(2,1)S(1)}, bf16[192,1024]{1,0:T(8,128)(2,1)S(1)}, u32[]{:S(2)}, u32[]{:S(2)}) collective-permute-start(bf16[192,1024]{1,0:T(8,128)(2,1)S(1)} %get-tuple-element.35), channel_id=1, source_target_pairs={{0,2},{2,4},{4,6},{6,0},{1,3},{3,5},{5,7},{7,1},{8,10},{10,12},{12... | collective-permute-start | bytes 1179656 | tf_op jit(solution)/shard_map/ppermute | solution.py:159
  17.4 5.2 %collective-permute-start.2 = (bf16[192,1024]{1,0:T(8,128)(2,1)S(1)}, bf16[192,1024]{1,0:T(8,128)(2,1)S(1)}, u32[]{:S(2)}, u32[]{:S(2)}) collective-permute-start(bf16[192,1024]{1,0:T(8,128)(2,1)S(1)} %get-tuple-element.36), channel_id=1, source_target_pairs={{0,6},{2,0},{4,2},{6,4},{1,7},{3,1},{5,3},{7,5},{8,14},{10,8},{12,... | collective-permute-start | bytes 1179656 | tf_op jit(solution)/shard_map/ppermute | solution.py:160
  22.6 7.5 %collective-permute-done.3.high_second = bf16[192,1024]{1,0:T(8,128)(2,1)S(1)} collective-permute-done((bf16[192,1024]{1,0:T(8,128)(2,1)S(1)}, bf16[192,1024]{1,0:T(8,128)(2,1)S(1)}, u32[]{:S(2)}, u32[]{:S(2)}) %collective-permute-start.3) | collective-permute-done | bytes 393248 | tf_op jit(solution)/shard_map/ppermute | solution.py:158
  30.2 6.3 %collective-permute-start.5 = (bf16[192,1024]{1,0:T(8,128)(2,1)S(1)}, bf16[192,1024]{1,0:T(8,128)(2,1)S(1)}, u32[]{:S(2)}, u32[]{:S(2)}) collective-permute-start(bf16[192,1024]{1,0:T(8,128)(2,1)S(1)} %collective-permute-done.3.high_second), channel_id=1, source_target_pairs={{0,6},{2,0},{4,2},{6,4},{1,7},{3,1},{5,3},{7,5},{8,14},{10,8},{12,... | collective-permute-start | bytes 1179656 | tf_op jit(solution)/shard_map/ppermute | solution.py:162
  36.5 0.0 collective-permute-done.low_first
  36.5 1.9 %collective-permute-start.4 = (bf16[192,1024]{1,0:T(8,128)(2,1)S(1)}, bf16[192,1024]{1,0:T(8,128)(2,1)S(1)}, u32[]{:S(2)}, u32[]{:S(2)}) collective-permute-start(bf16[192,1024]{1,0:T(8,128)(2,1)S(1)} %collective-permute-done.low_first), channel_id=1, source_target_pairs={{0,2},{2,4},{4,6},{6,0},{1,3},{3,5},{5,7},{7,1},{8,10},{10,12},{12... | collective-permute-start | bytes 1179656 | tf_op jit(solution)/shard_map/ppermute | solution.py:161
  38.5 0.0 copy-start
  38.5 1.8 %copy.13 = bf16[192,8,2,256]{3,1,2,0:T(8,128)(2,1)S(1)} copy(bf16[192,8,2,256]{3,2,1,0:T(2,128)(2,1)} %bitcast.15) | data formatting | bytes 3145728
  40.3 0.1 pad_add_fusion.where
  40.4 0.0 copy-start.1
  40.4 0.0 collective-permute-done.1.low_second
  40.4 7.5 %collective-permute-done.2.high_first = bf16[192,1024]{1,0:T(8,128)(2,1)S(1)} collective-permute-done((bf16[192,1024]{1,0:T(8,128)(2,1)S(1)}, bf16[192,1024]{1,0:T(8,128)(2,1)S(1)}, u32[]{:S(2)}, u32[]{:S(2)}) %collective-permute-start.2) | collective-permute-done | bytes 393248 | tf_op jit(solution)/shard_map/ppermute | solution.py:160
  47.9 0.0 copy-done
  47.9 2.4 %shard_map.101.total = f32[1024,512]{1,0:T(8,128)S(1)} custom-call(s32[2]{0:T(128)S(1)} %pad_add_fusion.where, bf16[384,1024]{1,0:T(8,128)(2,1)S(1)} %bitcast.13, bf16[192,1024]{1,0:T(8,128)(2,1)S(1)} %collective-permute-done.low_first, bf16[192,1024]{1,0:T(8,128)(2,1)S(1)} %collective-permute-done.1.low_second, ...), custom_call_target="tpu_custom_call" | custom-call | flops 1207959552 | bytes 6291456 | tf_op jit(solution)/shard_map/pallas_call | solution.py:170
  50.3 12.9 %collective-permute-done.5.far_second = bf16[192,1024]{1,0:T(8,128)(2,1)S(1)} collective-permute-done((bf16[192,1024]{1,0:T(8,128)(2,1)S(1)}, bf16[192,1024]{1,0:T(8,128)(2,1)S(1)}, u32[]{:S(2)}, u32[]{:S(2)}) %collective-permute-start.5) | collective-permute-done | bytes 393248 | tf_op jit(solution)/shard_map/ppermute | solution.py:162
  63.2 6.4 %collective-permute-done.4.far_first = bf16[192,1024]{1,0:T(8,128)(2,1)S(1)} collective-permute-done((bf16[192,1024]{1,0:T(8,128)(2,1)S(1)}, bf16[192,1024]{1,0:T(8,128)(2,1)S(1)}, u32[]{:S(2)}, u32[]{:S(2)}) %collective-permute-start.4) | collective-permute-done | bytes 393248 | tf_op jit(solution)/shard_map/ppermute | solution.py:161
  69.5 0.0 copy-done.1
  69.5 1.3 shard_map.102
  70.9 3.3 %collective-permute-start.6 = (bf16[32,16,512]{2,1,0:T(8,128)(2,1)S(1)}, bf16[32,16,512]{2,1,0:T(8,128)(2,1)S(1)}, u32[]{:S(2)}, u32[]{:S(2)}) collective-permute-start(bf16[32,16,512]{2,1,0:T(8,128)(2,1)S(1)} %get-tuple-element.21), channel_id=1, source_target_pairs={{0,8},{8,0},{1,9},{9,1},{2,10},{10,2},{3,11},{11,3},{4,12},{12,4},... | collective-permute-start | bytes 1572872 | tf_op jit(solution)/shard_map/ppermute | solution.py:194
  74.2 1.5 collective-permute-done.6
  75.7 0.2 add_convert_fusion
  75.9 0.0 copy-start.2
  75.9 26.1 %all_to_all.20 = bf16[64,8,512]{2,1,0:T(8,128)(2,1)S(1)} all-to-all(bf16[64,8,512]{2,1,0:T(8,128)(2,1)S(1)} %bitcast.14), channel_id=1, replica_groups=mesh['x'=4,'y'=8,'core'=2,'tensor'=4,'replica'=2] {'x','y','replica'}, dimensions={0} | all-to-all | bytes 1048576 | tf_op jit(solution)/shard_map/all_to_all | solution.py:196
  102.0 0.1 convert_reduce_fusion.lines
  102.1 0.0 copy-start.3
  102.1 12.6 %all_to_all.21 = f32[16,1,256]{2,1,0:T(1,128)S(1)} all-to-all(f32[16,1,256]{2,1,0:T(1,128)S(1)} %broadcast_in_dim.6), channel_id=1, replica_groups=mesh['x'=4,'y'=8,'core'=2,'tensor'=4,'replica'=2] {'x','core','replica'}, dimensions={0} | all-to-all | bytes 32768 | tf_op jit(solution)/shard_map/all_to_all | solution.py:203
  114.8 15.2 %all_to_all.22.sums = f32[32,1,256]{2,1,0:T(1,128)} all-to-all(f32[32,1,256]{2,1,0:T(1,128)S(1)} %broadcast_in_dim.7), channel_id=1, replica_groups=mesh['x'=4,'y'=8,'core'=2,'tensor'=4,'replica'=2] {'y','tensor'}, dimensions={0} | all-to-all | bytes 65536 | tf_op jit(solution)/shard_map/all_to_all | solution.py:203
  130.0 0.0 copy-done.3
  130.0 1.8 %shard_map.103 = (f32[2,8,256]{2,1,0:T(8,128)}, f32[2,8,256]{2,1,0:T(8,128)}, f32[2,8,256]{2,1,0:T(8,128)}, bf16[64,2,8,256]{3,2,1,0:T(8,128)(2,1)}, f32[4,256]{...) custom-call(s32[2]{0:T(128)} %copy-done.1, f32[8,512]{1,0:T(8,128)} %copy-done.3, ...), custom_call_target="tpu_custom_call" | custom-call | tf_op jit(solution)/shard_map/pallas_call | solution.py:209
  131.8 4.6 %all-to-all-start.3 = ((bf16[64,2,8,256]{3,2,1,0:T(8,128)(2,1)}), bf16[64,2,8,256]{3,2,1,0:T(8,128)(2,1)S(1)}, u32[]{:S(2)}, u32[]{:S(2)}) async-start(bf16[64,2,8,256]{3,2,1,0:T(8,128)(2,1)} %get-tuple-element.22), calls=%async_computation.3 | async-start | bytes 1048576 | tf_op jit(solution)/shard_map/all_to_all | solution.py:218
  136.4 2.6 %collective-permute-start.7 = (f32[4,256]{1,0:T(4,128)}, f32[4,256]{1,0:T(4,128)S(1)}, u32[]{:S(2)}, u32[]{:S(2)}) collective-permute-start(f32[4,256]{1,0:T(4,128)} %get-tuple-element.24), channel_id=1, source_target_pairs={{0,2},{2,4},{4,6},{6,0},{1,3},{3,5},{5,7},{7,1},{8,10},{10,12},{12... | collective-permute-start | bytes 12296 | tf_op jit(solution)/shard_map/ppermute | solution.py:220
  139.0 3.9 %collective-permute-start.8 = (f32[4,256]{1,0:T(4,128)}, f32[4,256]{1,0:T(4,128)S(1)}, u32[]{:S(2)}, u32[]{:S(2)}) collective-permute-start(f32[4,256]{1,0:T(4,128)} %get-tuple-element.25), channel_id=1, source_target_pairs={{0,4},{2,6},{4,0},{6,2},{1,5},{3,7},{5,1},{7,3},{8,12},{10,14},{12... | collective-permute-start | bytes 12296 | tf_op jit(solution)/shard_map/ppermute | solution.py:220
  142.9 3.6 %collective-permute-start.9 = (f32[4,256]{1,0:T(4,128)}, f32[4,256]{1,0:T(4,128)S(1)}, u32[]{:S(2)}, u32[]{:S(2)}) collective-permute-start(f32[4,256]{1,0:T(4,128)} %get-tuple-element.26), channel_id=1, source_target_pairs={{0,6},{2,0},{4,2},{6,4},{1,7},{3,1},{5,3},{7,5},{8,14},{10,8},{12,... | collective-permute-start | bytes 12296 | tf_op jit(solution)/shard_map/ppermute | solution.py:220
  146.5 0.0 collective-permute-done.7.refs_1_
  146.5 0.0 copy-start.4
  146.6 1.3 collective-permute-done.8.refs_2_
  147.8 0.0 copy-start.5
  147.8 1.4 collective-permute-done.9.refs_3_
  149.3 0.0 copy-start.6
  149.3 2.1 %all-to-all-done.3.column = bf16[64,2,8,256]{3,2,1,0:T(8,128)(2,1)S(1)} async-done(((bf16[64,2,8,256]{3,2,1,0:T(8,128)(2,1)}), bf16[64,2,8,256]{3,2,1,0:T(8,128)(2,1)S(1)}, u32[]{:S(2)}, u32[]{:S(2)}) %all-to-all-start.3) | async-done | bytes 524320 | tf_op jit(solution)/shard_map/all_to_all | solution.py:218
  151.4 5.6 %collective-permute-start.10 = (bf16[64,2,8,256]{3,2,1,0:T(8,128)(2,1)S(1)}, bf16[64,2,8,256]{3,2,1,0:T(8,128)(2,1)S(1)}, u32[]{:S(2)}, u32[]{:S(2)}) collective-permute-start(bf16[64,2,8,256]{3,2,1,0:T(8,128)(2,1)S(1)} %all-to-all-done.3.column), channel_id=1, source_target_pairs={{0,8},{8,0},{1,9},{9,1},{2,10},{10,2},{3,11},{11,3},{4,12},{12,4},... | collective-permute-start | bytes 1572872 | tf_op jit(solution)/shard_map/ppermute | solution.py:228
  157.0 0.0 copy-done.4
  157.1 0.0 copy-done.5
  157.1 0.0 copy-done.6
  157.1 1.4 shard_map.105
  158.5 0.0 collective-permute-done.10.other
  158.6 0.0 copy-done.2
  158.6 1.6 %shard_map.104 = bf16[2,1024,256]{2,1,0:T(8,128)(2,1)} custom-call(s32[2]{0:T(128)S(1)} %copy-done.2, bf16[64,2,8,256]{3,2,1,0:T(8,128)(2,1)S(1)} %all-to-all-done.3.column, bf16[64,2,8,256]{3,2,1,0:T(8,128)(2,1)S(1)} %collective-permute-done.10.other), custom_call_target="tpu_custom_call" | custom-call | tf_op jit(solution)/shard_map/pallas_call | solution.py:229
  (6 shorter events, 0.1 us)
Async XLA Ops:
  1.8 28.4 %collective-permute-start.3 = (bf16[192,1024]{1,0:T(8,128)(2,1)S(1)}, bf16[192,1024]{1,0:T(8,128)(2,1)S(1)}, u32[]{:S(2)}, u32[]{:S(2)}) collective-permute-start(bf16[192,1024]{1,0:T(8,128)(2,1)S(1)} %get-tuple-element.35), channel_id=1, source_target_pairs={{0,6},{2,0},{4,2},{6,4},{1,7},{3,1},{5,3},{7,5},{8,14},{10,8},{12,... | collective-permute-start | bytes 1179656 | tf_op jit(solution)/shard_map/ppermute | solution.py:158
  13.3 23.2 %collective-permute-start = (bf16[192,1024]{1,0:T(8,128)(2,1)S(1)}, bf16[192,1024]{1,0:T(8,128)(2,1)S(1)}, u32[]{:S(2)}, u32[]{:S(2)}) collective-permute-start(bf16[192,1024]{1,0:T(8,128)(2,1)S(1)} %get-tuple-element.36), channel_id=1, source_target_pairs={{0,2},{2,4},{4,6},{6,0},{1,3},{3,5},{5,7},{7,1},{8,10},{10,12},{12... | collective-permute-start | bytes 1179656 | tf_op jit(solution)/shard_map/ppermute | solution.py:157
  15.2 25.1 %collective-permute-start.1 = (bf16[192,1024]{1,0:T(8,128)(2,1)S(1)}, bf16[192,1024]{1,0:T(8,128)(2,1)S(1)}, u32[]{:S(2)}, u32[]{:S(2)}) collective-permute-start(bf16[192,1024]{1,0:T(8,128)(2,1)S(1)} %get-tuple-element.35), channel_id=1, source_target_pairs={{0,2},{2,4},{4,6},{6,0},{1,3},{3,5},{5,7},{7,1},{8,10},{10,12},{12... | collective-permute-start | bytes 1179656 | tf_op jit(solution)/shard_map/ppermute | solution.py:159
  17.4 30.5 %collective-permute-start.2 = (bf16[192,1024]{1,0:T(8,128)(2,1)S(1)}, bf16[192,1024]{1,0:T(8,128)(2,1)S(1)}, u32[]{:S(2)}, u32[]{:S(2)}) collective-permute-start(bf16[192,1024]{1,0:T(8,128)(2,1)S(1)} %get-tuple-element.36), channel_id=1, source_target_pairs={{0,6},{2,0},{4,2},{6,4},{1,7},{3,1},{5,3},{7,5},{8,14},{10,8},{12,... | collective-permute-start | bytes 1179656 | tf_op jit(solution)/shard_map/ppermute | solution.py:160
  30.2 33.0 %collective-permute-start.5 = (bf16[192,1024]{1,0:T(8,128)(2,1)S(1)}, bf16[192,1024]{1,0:T(8,128)(2,1)S(1)}, u32[]{:S(2)}, u32[]{:S(2)}) collective-permute-start(bf16[192,1024]{1,0:T(8,128)(2,1)S(1)} %collective-permute-done.3.high_second), channel_id=1, source_target_pairs={{0,6},{2,0},{4,2},{6,4},{1,7},{3,1},{5,3},{7,5},{8,14},{10,8},{12,... | collective-permute-start | bytes 1179656 | tf_op jit(solution)/shard_map/ppermute | solution.py:162
  36.5 33.0 %collective-permute-start.4 = (bf16[192,1024]{1,0:T(8,128)(2,1)S(1)}, bf16[192,1024]{1,0:T(8,128)(2,1)S(1)}, u32[]{:S(2)}, u32[]{:S(2)}) collective-permute-start(bf16[192,1024]{1,0:T(8,128)(2,1)S(1)} %collective-permute-done.low_first), channel_id=1, source_target_pairs={{0,2},{2,4},{4,6},{6,0},{1,3},{3,5},{5,7},{7,1},{8,10},{10,12},{12... | collective-permute-start | bytes 1179656 | tf_op jit(solution)/shard_map/ppermute | solution.py:161
  38.5 9.4 %copy-start = (bf16[1,384,1024]{2,1,0:T(8,128)(2,1)S(1)}, bf16[1,384,1024]{2,1,0:T(8,128)(2,1)}, u32[]{:S(2)}) copy-start(bf16[1,384,1024]{2,1,0:T(8,128)(2,1)} %param.6) | copy-start | bytes 2359300
  40.4 29.2 %copy-start.1 = (s32[2]{0:T(128)}, s32[2]{0:T(128)S(1)}, u32[]{:S(2)}) copy-start(s32[2]{0:T(128)S(1)} %pad_add_fusion.where) | copy-start | bytes 28
  70.9 4.9 %collective-permute-start.6 = (bf16[32,16,512]{2,1,0:T(8,128)(2,1)S(1)}, bf16[32,16,512]{2,1,0:T(8,128)(2,1)S(1)}, u32[]{:S(2)}, u32[]{:S(2)}) collective-permute-start(bf16[32,16,512]{2,1,0:T(8,128)(2,1)S(1)} %get-tuple-element.21), channel_id=1, source_target_pairs={{0,8},{8,0},{1,9},{9,1},{2,10},{10,2},{3,11},{11,3},{4,12},{12,4},... | collective-permute-start | bytes 1572872 | tf_op jit(solution)/shard_map/ppermute | solution.py:194
  75.9 82.7 %copy-start.2 = (s32[2]{0:T(128)S(1)}, s32[2]{0:T(128)}, u32[]{:S(2)}) copy-start(s32[2]{0:T(128)} %copy-done.1) | copy-start | bytes 28
  102.1 27.9 %copy-start.3 = (f32[8,512]{1,0:T(8,128)}, f32[8,512]{1,0:T(8,128)S(1)}, u32[]{:S(2)}) copy-start(f32[8,512]{1,0:T(8,128)S(1)} %convert_reduce_fusion.lines) | copy-start | bytes 49156
  131.8 19.7 %all-to-all-start.3 = ((bf16[64,2,8,256]{3,2,1,0:T(8,128)(2,1)}), bf16[64,2,8,256]{3,2,1,0:T(8,128)(2,1)S(1)}, u32[]{:S(2)}, u32[]{:S(2)}) async-start(bf16[64,2,8,256]{3,2,1,0:T(8,128)(2,1)} %get-tuple-element.22), calls=%async_computation.3 | async-start | bytes 1048576 | tf_op jit(solution)/shard_map/all_to_all | solution.py:218
  136.4 10.1 %collective-permute-start.7 = (f32[4,256]{1,0:T(4,128)}, f32[4,256]{1,0:T(4,128)S(1)}, u32[]{:S(2)}, u32[]{:S(2)}) collective-permute-start(f32[4,256]{1,0:T(4,128)} %get-tuple-element.24), channel_id=1, source_target_pairs={{0,2},{2,4},{4,6},{6,0},{1,3},{3,5},{5,7},{7,1},{8,10},{10,12},{12... | collective-permute-start | bytes 12296 | tf_op jit(solution)/shard_map/ppermute | solution.py:220
  139.0 8.8 %collective-permute-start.8 = (f32[4,256]{1,0:T(4,128)}, f32[4,256]{1,0:T(4,128)S(1)}, u32[]{:S(2)}, u32[]{:S(2)}) collective-permute-start(f32[4,256]{1,0:T(4,128)} %get-tuple-element.25), channel_id=1, source_target_pairs={{0,4},{2,6},{4,0},{6,2},{1,5},{3,7},{5,1},{7,3},{8,12},{10,14},{12... | collective-permute-start | bytes 12296 | tf_op jit(solution)/shard_map/ppermute | solution.py:220
  142.9 6.4 %collective-permute-start.9 = (f32[4,256]{1,0:T(4,128)}, f32[4,256]{1,0:T(4,128)S(1)}, u32[]{:S(2)}, u32[]{:S(2)}) collective-permute-start(f32[4,256]{1,0:T(4,128)} %get-tuple-element.26), channel_id=1, source_target_pairs={{0,6},{2,0},{4,2},{6,4},{1,7},{3,1},{5,3},{7,5},{8,14},{10,8},{12,... | collective-permute-start | bytes 12296 | tf_op jit(solution)/shard_map/ppermute | solution.py:220
  146.5 10.5 %copy-start.4 = (f32[4,256]{1,0:T(4,128)}, f32[4,256]{1,0:T(4,128)S(1)}, u32[]{:S(2)}) copy-start(f32[4,256]{1,0:T(4,128)S(1)} %collective-permute-done.7.refs_1_) | copy-start | bytes 12292
  147.8 9.2 %copy-start.5 = (f32[4,256]{1,0:T(4,128)}, f32[4,256]{1,0:T(4,128)S(1)}, u32[]{:S(2)}) copy-start(f32[4,256]{1,0:T(4,128)S(1)} %collective-permute-done.8.refs_2_) | copy-start | bytes 12292
  149.3 7.8 %copy-start.6 = (f32[4,256]{1,0:T(4,128)}, f32[4,256]{1,0:T(4,128)S(1)}, u32[]{:S(2)}) copy-start(f32[4,256]{1,0:T(4,128)S(1)} %collective-permute-done.9.refs_3_) | copy-start | bytes 12292
  151.4 7.1 %collective-permute-start.10 = (bf16[64,2,8,256]{3,2,1,0:T(8,128)(2,1)S(1)}, bf16[64,2,8,256]{3,2,1,0:T(8,128)(2,1)S(1)}, u32[]{:S(2)}, u32[]{:S(2)}) collective-permute-start(bf16[64,2,8,256]{3,2,1,0:T(8,128)(2,1)S(1)} %all-to-all-done.3.column), channel_id=1, source_target_pairs={{0,8},{8,0},{1,9},{9,1},{2,10},{10,2},{3,11},{11,3},{4,12},{12,4},... | collective-permute-start | bytes 1572872 | tf_op jit(solution)/shard_map/ppermute | solution.py:228

commit v6 on v5

v6 whole, which is shorter than its diff:
```python
import functools

import jax
import jax.numpy as jnp
from jax import lax
from jax.experimental import pallas as pl
from jax.experimental.pallas import tpu as pltpu
from jax.sharding import Mesh, PartitionSpec as P

STEP = 100


beta_one = 0.9
beta_two = 0.95
learn_rate = 0.05
decay_rate = 0.1
adam_eps = 1e-08
average_keep = 0.9

XYR = ("x", "y", "replica")
PLANE = ("x", "y")
SWAP = ((0, 1), (1, 0))


def round_trip(count, step):
    return [(i, (i + step) % count) for i in range(count)]


def along_tokens(block, against):
    return lax.dot_general(
        block, against, (((0,), (0,)), ((), ())), preferred_element_type=jnp.float32
    )


def near_kernel(where, own, low_first, low_second, high_first, high_second, outgrad, total):
    count, part = own.shape[0], low_first.shape[0]
    shards_all = outgrad.shape[0] // count
    tile = 256

    def against(step):
        start = lax.rem(where[0] + step, shards_all) * count
        return outgrad[pl.ds(pl.multiple_of(start, count), count), :]

    for left in range(0, own.shape[1], tile):
        cut = slice(left, left + tile)
        below, above = against(shards_all - 1), against(1)
        total[cut, :] = (
            along_tokens(own[:, cut], against(0))
            + along_tokens(low_first[:, cut], below[:part])
            + along_tokens(low_second[:, cut], below[part:])
            + along_tokens(high_first[:, cut], above[:part])
            + along_tokens(high_second[:, cut], above[part:])
        )


def far_kernel(where, total, far_first, far_second, outgrad, keep, give):
    part = far_first.shape[0]
    start = lax.rem(where[0] + 2, outgrad.shape[0] // (2 * part)) * (2 * part)
    against = outgrad[pl.ds(pl.multiple_of(start, 2 * part), 2 * part), :]
    first_core = where[1] == 0
    lines, width = keep.shape[1], keep.shape[2]
    tile = 256
    for left in range(0, total.shape[0], tile):
        cut = slice(left, left + tile)
        value = (
            total[cut, :]
            + along_tokens(far_first[:, cut], against[:part])
            + along_tokens(far_second[:, cut], against[part:])
        )
        value = value.reshape(tile // (2 * lines), 2, lines, width)
        even, odd = value[:, 0], value[:, 1]
        out = slice(left // (2 * lines), (left + tile) // (2 * lines))
        keep[out] = jnp.where(first_core, even, odd)
        give[out] = jnp.where(first_core, odd, even).astype(give.dtype)


def row_blocks(lines, count):
    width = lines.shape[1] // 2
    halves = (lines[:, :width], lines[:, width:])
    held = 2 * lines.shape[0] // count
    return [half[row : row + held] for half in halves for row in range(0, lines.shape[0], held)]


def pick(index, blocks):
    chosen = blocks[0]
    for k in range(1, len(blocks)):
        chosen = jnp.where(index == k, blocks[k], chosen)
    return chosen


def whole_lines(ref):
    return jnp.concatenate([ref[0], ref[1]], axis=1)


def state_kernel(where, one, two, held, wide, *lent):
    bf16 = jnp.bfloat16
    parts = (whole_lines(one), whole_lines(two), whole_lines(held))
    high = parts[2].astype(bf16)
    low = (parts[2] - high.astype(jnp.float32)).astype(bf16)
    for k, block in enumerate((parts[0].astype(bf16), parts[1].astype(bf16), high, low)):
        wide[:, k] = jnp.broadcast_to(block[None], (wide.shape[0],) + block.shape)
    for k, block in enumerate(parts):
        blocks = row_blocks(block, len(lent))
        for step, ref in enumerate(lent):
            ref[k] = pick(lax.rem(where[0] + step, len(lent)), blocks)


def clip_of(sums, count):
    total = jnp.sum(sums[:, sums.shape[1] - 1 :, :], axis=(0, 1), keepdims=True)[0]
    total = jnp.sum(total, axis=1, keepdims=True)
    return 1.0 / jnp.sqrt(total / count + 1e-06)


def update(clip_factor, grad, one, two, held):
    fix_one = 1.0 - beta_one**STEP
    fix_two = 1.0 - beta_two**STEP
    scaled = clip_factor * grad
    first = beta_one * one + (1.0 - beta_one) * scaled
    second = beta_two * two + (1.0 - beta_two) * (scaled * scaled)
    direction = first / fix_one / (jnp.sqrt(second / fix_two) + adam_eps)
    return first, second, held - learn_rate * (direction + decay_rate * held)


def plane_kernel(count, sums, shared, state, mine):
    f32 = jnp.float32
    clip_factor = clip_of(sums, count)

    def step(k, carry):
        parts = [state[k, i].astype(f32) for i in range(4)]
        grad = shared[k].astype(f32)
        new = update(clip_factor, grad, parts[0], parts[1], parts[2] + parts[3])[2]
        mine[k] = new.astype(mine.dtype)
        return carry

    lax.fori_loop(0, shared.shape[0], step, 0, unroll=8)


def own_kernel(count, where, sums, lines, one, two, held, average, *refs):
    *lent_state, new_one, new_two, new_held, out = refs
    shards_all = len(lent_state)
    clip_factor = clip_of(sums, count)
    width = one.shape[2]
    for half in range(2):
        grad = lines[:, half * width : (half + 1) * width]
        results = update(clip_factor, grad, one[half], two[half], held[half])
        new_one[half], new_two[half], new_held[half] = results
    for source in range(shards_all):
        step = lax.rem(where[0] + shards_all - source, shards_all)
        state = [pick(step, [ref[k] for ref in lent_state]) for k in range(3)]
        grad = sums[(where[1] * shards_all + source) * 2 + where[2]][: state[0].shape[0]]
        columns = slice(source * width, (source + 1) * width)
        kept = average_keep * average[0, 0, :, columns]
        out[0, 0, :, columns] = kept + (1.0 - average_keep) * update(clip_factor, grad, *state)[2]


def weights_kernel(where, mine, twin, other, other_twin, weights):
    f32 = jnp.float32
    rows, width = mine.shape[1], weights.shape[2]
    core, first = where[1], where[2] == 0

    def place(near, far, start):
        near, far = near.astype(f32), far.astype(f32)
        pieces = [jnp.where(first, near, far), jnp.where(first, far, near)]
        pieces = jnp.concatenate(pieces, axis=0).astype(weights.dtype)
        start = pl.multiple_of(start, 2 * rows)
        weights[0, pl.ds(start, 2 * rows), :] = pieces[:, :width]
        weights[1, pl.ds(start, 2 * rows), :] = pieces[:, width:]

    def step(k, carry):
        place(mine[k], twin[k], (2 * k + core) * 2 * rows)
        place(other[k], other_twin[k], (2 * k + 1 - core) * 2 * rows)
        return carry

    lax.fori_loop(0, mine.shape[0], step, 0, unroll=8)


def shards(features, cotangents, moment_one, moment_two, master, average):
    f32, bf16 = jnp.float32, jnp.bfloat16
    col_width = cotangents.shape[3]
    rows = moment_one.shape[1]
    nx, ny, nr = (lax.axis_size(name) for name in XYR)
    nt = lax.axis_size("tensor")
    peers = nx * ny * nr
    core = lax.axis_index("core")
    place = lax.axis_index("tensor")
    where = jnp.stack([place, core, lax.axis_index("replica")]).astype(jnp.int32)
    ring = lambda blocks: [blocks[0]] + [
        lax.ppermute(blocks[k], "tensor", round_trip(nt, k)) for k in range(1, nt)
    ]

    tokens = features[0]
    count, dim_model = tokens.shape
    part = count // 2
    first, second = tokens[:part], tokens[part:]
    up, down = round_trip(nt, 1), round_trip(nt, nt - 1)
    low_first = lax.ppermute(first, "tensor", up)
    high_second = lax.ppermute(second, "tensor", down)
    low_second = lax.ppermute(second, "tensor", up)
    high_first = lax.ppermute(first, "tensor", down)
    far_first = lax.ppermute(low_first, "tensor", up)
    far_second = lax.ppermute(high_second, "tensor", down)
    outgrad = cotangents[0].reshape(cotangents.shape[1], 2 * col_width)

    scalars = pl.BlockSpec(memory_space=pltpu.SMEM)
    local = pl.BlockSpec(memory_space=pltpu.VMEM)
    params = pltpu.CompilerParams(vmem_limit_bytes=24 * 2**20)

    width = 2 * col_width
    held_rows = 2 * rows // nt
    state, *lent_state = pl.pallas_call(
        state_kernel,
        out_shape=(jax.ShapeDtypeStruct((nx * ny, 4, rows, width), bf16),)
        + (jax.ShapeDtypeStruct((3, held_rows, col_width), f32),) * nt,
        in_specs=[scalars] + [local] * 3,
        out_specs=(local,) * (1 + nt),
    )(where, moment_one, moment_two, master)
    state = lax.all_to_all(state, PLANE, 0, 0, tiled=True)

    lines = nr * rows
    total = pl.pallas_call(
        near_kernel,
        out_shape=jax.ShapeDtypeStruct((dim_model, width), f32),
        in_specs=[scalars] + [local] * 6,
        out_specs=local,
        compiler_params=params,
        cost_estimate=pl.CostEstimate(
            flops=48 * count * dim_model * width, bytes_accessed=6 * 2**20, transcendentals=0
        ),
    )(where, tokens, low_first, low_second, high_first, high_second, outgrad)
    keep, give = pl.pallas_call(
        far_kernel,
        out_shape=(
            jax.ShapeDtypeStruct((nx * ny, lines, width), f32),
            jax.ShapeDtypeStruct((nx * ny, lines, width), bf16),
        ),
        in_specs=[scalars] + [local] * 4,
        out_specs=(local, local),
        compiler_params=params,
        cost_estimate=pl.CostEstimate(
            flops=16 * count * dim_model * width, bytes_accessed=6 * 2**20, transcendentals=0
        ),
    )(where, total, far_first, far_second, outgrad)

    got = lax.ppermute(give, "core", SWAP)
    half = (keep + got.astype(f32)).astype(bf16).reshape(peers, rows, width)
    half, state, lent_state = lax.optimization_barrier((half, state, lent_state))
    terms = lax.all_to_all(half, XYR, split_axis=0, concat_axis=0, tiled=True)
    lent_state = ring(lent_state)
    terms, lent_state = lax.optimization_barrier((terms, lent_state))
    grad_lines = jnp.sum(terms.astype(f32), axis=0)

    spread = grad_lines.astype(bf16)
    spread = jnp.broadcast_to(spread[None], (nx * ny,) + spread.shape)
    shared = lax.all_to_all(spread, PLANE, 0, 0, tiled=True)
    squares = shared.astype(f32)
    squares = jnp.sum(squares * squares, axis=(0, 1))
    squares = squares[:col_width] + squares[col_width:]
    sums = jnp.transpose(grad_lines.reshape(rows, 2, col_width), (1, 0, 2))
    sums = sums.reshape(nt, held_rows, col_width)
    sums = jnp.concatenate([sums, jnp.broadcast_to(squares, sums.shape)], axis=1)
    sums = jnp.broadcast_to(sums[None, :, None], (2, nt, nr) + sums.shape[1:])
    others = ("core", "tensor", "replica")
    sums = lax.all_to_all(
        sums.reshape((2 * nt * nr,) + sums.shape[3:]), others, 0, 0, tiled=True
    )
    count_all = 2.0 * dim_model * dim_model

    mine = pl.pallas_call(
        functools.partial(plane_kernel, count_all),
        out_shape=jax.ShapeDtypeStruct((nx * ny, rows, width), bf16),
        in_specs=[local] * 3,
        out_specs=local,
        compiler_params=params,
    )(sums, shared, state)
    twin = lax.ppermute(mine, "replica", SWAP)
    other = lax.ppermute(mine, "core", SWAP)
    piece = jax.ShapeDtypeStruct(moment_one.shape, f32)
    new_first, new_second, new_master, new_average = pl.pallas_call(
        functools.partial(own_kernel, count_all),
        out_shape=(piece, piece, piece, jax.ShapeDtypeStruct(average.shape, f32)),
        in_specs=[scalars] + [local] * (6 + nt),
        out_specs=(local,) * 4,
    )(
        where, sums, grad_lines, moment_one, moment_two, master, average, *lent_state
    )
    twin, new_average = lax.optimization_barrier((twin, new_average))
    other_twin = lax.ppermute(twin, "core", SWAP)
    weights = pl.pallas_call(
        weights_kernel,
        out_shape=jax.ShapeDtypeStruct((2, dim_model, col_width), bf16),
        in_specs=[scalars] + [local] * 4,
        out_specs=local,
        compiler_params=params,
    )(where, mine, twin, other, other_twin)
    return (weights, new_first, new_second, new_master, new_average)


def solution(mesh):
    shape = dict(zip(mesh.axis_names, mesh.devices.shape))
    nx, ny = 4, shape["dp"] // 8
    fine = Mesh(
        mesh.devices.reshape(nx, ny, 2, shape["tensor"], shape["replica"]),
        ("x", "y", "core", "tensor", "replica"),
    )
    groups = ("x", "y", "core", "replica")
    state = P(None, groups, "tensor")
    placed = (
        P(groups, "tensor", None),
        P(groups, None, None, "tensor"),
        state,
        state,
        state,
        P(groups, "tensor", None, None),
    )
    return jax.shard_map(
        shards,
        mesh=fine,
        in_specs=placed,
        out_specs=(P(None, None, "tensor"), state, state, state, P(groups, "tensor", None, None)),
        check_vma=False,
    )
```

time: 161 us -> 153 us (0.950)
  blocking collectives: 53.8 us -> 16.8 us
  starting transfers between devices: 52.8 us -> 85.4 us
  waiting for transfers between devices: 40.8 us -> 33.7 us
    all_to_all x3 -> x1, blocking collectives: 53.8 us -> 16.8 us  [shards(): lax.all_to_all(sums.reshape((2 * nt * nr,) + sums.shape[3:]), others, 0,...]
    all_to_all x1 -> x3, starting transfers between devices: 4.63 us -> 28.8 us  [the longest x1 11.6 us: shards(): terms = lax.all_to_all(half, XYR, split_axis=0, concat_axis=0, tiled=True)]
    ppermute x1, waiting for transfers between devices: 12.9 us -> 0.01 us  [shards(): far_second = lax.ppermute(high_second, 'tensor', down)]
    all_to_all x1 -> x3, waiting for transfers between devices: 2.15 us -> 11.3 us  [the longest x1 9.64 us: shards(): shared = lax.all_to_all(spread, PLANE, 0, 0, tiled=True)]
    ppermute x1, waiting for transfers between devices: 6.39 us -> 15.4 us  [shards(): far_first = lax.ppermute(low_first, 'tensor', up)]
    ppermute x4 -> x6, starting transfers between devices: 15.7 us -> 24.3 us  [the longest x3 13.5 us: shards(): lax.ppermute(blocks[k], 'tensor', round_trip(nt, k))]
    ppermute x1, waiting for transfers between devices: 7.53 us -> 0.01 us  [shards(): high_second = lax.ppermute(second, 'tensor', down)]
    ppermute x1, starting transfers between devices: 1.92 us -> 6.64 us  [shards(): low_first = lax.ppermute(first, 'tensor', up)]
  transfers between devices with their start and end apart: 12 -> 16, of which waited for: 8 -> 8; matrix products, arithmetic and copies ran while one was open for 1% -> 2% of each run, Pallas kernels for 2% -> 5%
where the time goes in v6:
time: 153 us; the launch traced here: 152 us
  starting transfers between devices  85.4 us (56%)
  waiting for transfers between devices  33.7 us (22%)
  blocking collectives  16.8 us (11%)
  Pallas kernels  9.78 us (6%)
  local copies, waits for them, and re-layouts  3.77 us (2%)
  other arithmetic  1.79 us (1%)
    all_to_all x1, blocking collectives, shards(): lax.all_to_all(sums.reshape((2 * nt * nr,) + sums.shape[3:]), others, 0,...  16.8 us
    ppermute x1, waiting for transfers between devices, shards(): far_first = lax.ppermute(low_first, 'tensor', up)  15.4 us
    ppermute x3, starting transfers between devices, shards(): lax.ppermute(blocks[k], 'tensor', round_trip(nt, k))  13.5 us
    all_to_all x1, starting transfers between devices, shards(): terms = lax.all_to_all(half, XYR, split_axis=0, concat_axis=0, tiled=True)  11.6 us
    all_to_all x1, starting transfers between devices, shards(): state = lax.all_to_all(state, PLANE, 0, 0, tiled=True)  9.67 us
    all_to_all x1, waiting for transfers between devices, shards(): shared = lax.all_to_all(spread, PLANE, 0, 0, tiled=True)  9.64 us
    all_to_all x1, starting transfers between devices, shards(): shared = lax.all_to_all(spread, PLANE, 0, 0, tiled=True)  7.61 us
    ppermute x1, starting transfers between devices, shards(): high_second = lax.ppermute(second, 'tensor', down)  6.77 us
  transfers between devices with their start and end apart: 16, of which 8 were waited for; matrix products, arithmetic and copies ran while one was open for 2% of the time, Pallas kernels for 5%

profile of v6, /device:TPU:1, one launch (start us, length us, event | category | flops | bytes accessed | tf_op | source)
XLA Modules:
  0.0 152.2 jit_solution(13647457482158045931)
XLA Ops:
  0.6 1.2 slice_bitcast_fusion
  1.8 6.6 %collective-permute-start = (bf16[192,1024]{1,0:T(8,128)(2,1)S(1)}, bf16[192,1024]{1,0:T(8,128)(2,1)S(1)}, u32[]{:S(2)}, u32[]{:S(2)}) collective-permute-start(bf16[192,1024]{1,0:T(8,128)(2,1)S(1)} %get-tuple-element.54), channel_id=1, source_target_pairs={{0,2},{2,4},{4,6},{6,0},{1,3},{3,5},{5,7},{7,1},{8,10},{10,12},{12... | collective-permute-start | bytes 1179656 | tf_op jit(solution)/shard_map/ppermute | solution.py:196
  8.4 6.8 %collective-permute-start.3 = (bf16[192,1024]{1,0:T(8,128)(2,1)S(1)}, bf16[192,1024]{1,0:T(8,128)(2,1)S(1)}, u32[]{:S(2)}, u32[]{:S(2)}) collective-permute-start(bf16[192,1024]{1,0:T(8,128)(2,1)S(1)} %get-tuple-element.53), channel_id=1, source_target_pairs={{0,6},{2,0},{4,2},{6,4},{1,7},{3,1},{5,3},{7,5},{8,14},{10,8},{12,... | collective-permute-start | bytes 1179656 | tf_op jit(solution)/shard_map/ppermute | solution.py:197
  15.2 2.2 %collective-permute-start.1 = (bf16[192,1024]{1,0:T(8,128)(2,1)S(1)}, bf16[192,1024]{1,0:T(8,128)(2,1)S(1)}, u32[]{:S(2)}, u32[]{:S(2)}) collective-permute-start(bf16[192,1024]{1,0:T(8,128)(2,1)S(1)} %get-tuple-element.53), channel_id=1, source_target_pairs={{0,2},{2,4},{4,6},{6,0},{1,3},{3,5},{5,7},{7,1},{8,10},{10,12},{12... | collective-permute-start | bytes 1179656 | tf_op jit(solution)/shard_map/ppermute | solution.py:198
  17.4 5.2 %collective-permute-start.2 = (bf16[192,1024]{1,0:T(8,128)(2,1)S(1)}, bf16[192,1024]{1,0:T(8,128)(2,1)S(1)}, u32[]{:S(2)}, u32[]{:S(2)}) collective-permute-start(bf16[192,1024]{1,0:T(8,128)(2,1)S(1)} %get-tuple-element.54), channel_id=1, source_target_pairs={{0,6},{2,0},{4,2},{6,4},{1,7},{3,1},{5,3},{7,5},{8,14},{10,8},{12,... | collective-permute-start | bytes 1179656 | tf_op jit(solution)/shard_map/ppermute | solution.py:199
  22.6 0.6 pad_add_fusion.where
  23.2 1.9 %shard_map.103 = (bf16[32,4,8,512]{3,2,1,0:T(8,128)(2,1)}, f32[3,4,256]{2,1,0:T(4,128)}, f32[3,4,256]{2,1,0:T(4,128)}, f32[3,4,256]{2,1,0:T(4,128)}, f32[3,4,256]{2,1,0:T(4,128)}) custom-call(s32[3]{0:T(128)} %pad_add_fusion.where, f32[2,8,256]{2,1,0:T(8,128)} %one.3, f32[2,8,256]{2,1,0:T(8,128)} %two.3, f32[2,8,256]{2,1,0:T(8,128)} %held.3), custom_call_target="tpu_custom_call" | custom-call | tf_op jit(solution)/shard_map/pallas_call | solution.py:210
  25.1 9.7 %all-to-all-start = ((bf16[32,4,8,512]{3,2,1,0:T(8,128)(2,1)}), bf16[32,4,8,512]{3,2,1,0:T(8,128)(2,1)S(1)}, u32[]{:S(2)}, u32[]{:S(2)}) async-start(bf16[32,4,8,512]{3,2,1,0:T(8,128)(2,1)} %get-tuple-element.31), calls=%async_computation | async-start | bytes 2097152 | tf_op jit(solution)/shard_map/all_to_all | solution.py:217
  34.8 0.0 copy-start.1
  34.8 0.0 copy-start.2
  34.8 1.8 %copy.11 = bf16[192,8,2,256]{3,1,2,0:T(8,128)(2,1)S(1)} copy(bf16[192,8,2,256]{3,2,1,0:T(2,128)(2,1)} %bitcast.19) | data formatting | bytes 3145728
  36.6 0.0 collective-permute-done.low_first
  36.6 2.2 %collective-permute-start.4 = (bf16[192,1024]{1,0:T(8,128)(2,1)S(1)}, bf16[192,1024]{1,0:T(8,128)(2,1)S(1)}, u32[]{:S(2)}, u32[]{:S(2)}) collective-permute-start(bf16[192,1024]{1,0:T(8,128)(2,1)S(1)} %collective-permute-done.low_first), channel_id=1, source_target_pairs={{0,2},{2,4},{4,6},{6,0},{1,3},{3,5},{5,7},{7,1},{8,10},{10,12},{12... | collective-permute-start | bytes 1179656 | tf_op jit(solution)/shard_map/ppermute | solution.py:200
  38.8 0.0 collective-permute-done.3.high_second
  38.8 5.2 %collective-permute-start.5 = (bf16[192,1024]{1,0:T(8,128)(2,1)S(1)}, bf16[192,1024]{1,0:T(8,128)(2,1)S(1)}, u32[]{:S(2)}, u32[]{:S(2)}) collective-permute-start(bf16[192,1024]{1,0:T(8,128)(2,1)S(1)} %collective-permute-done.3.high_second), channel_id=1, source_target_pairs={{0,6},{2,0},{4,2},{6,4},{1,7},{3,1},{5,3},{7,5},{8,14},{10,8},{12,... | collective-permute-start | bytes 1179656 | tf_op jit(solution)/shard_map/ppermute | solution.py:201
  44.1 0.0 collective-permute-done.1.low_second
  44.1 3.5 %collective-permute-done.2.high_first = bf16[192,1024]{1,0:T(8,128)(2,1)S(1)} collective-permute-done((bf16[192,1024]{1,0:T(8,128)(2,1)S(1)}, bf16[192,1024]{1,0:T(8,128)(2,1)S(1)}, u32[]{:S(2)}, u32[]{:S(2)}) %collective-permute-start.2) | collective-permute-done | bytes 393248 | tf_op jit(solution)/shard_map/ppermute | solution.py:199
  47.6 0.0 copy-done.1
  47.6 0.0 copy-done.2
  47.6 2.4 %shard_map.101.total = f32[1024,512]{1,0:T(8,128)S(1)} custom-call(s32[3]{0:T(128)S(1)} %copy-done.2, bf16[384,1024]{1,0:T(8,128)(2,1)S(1)} %bitcast.18, bf16[192,1024]{1,0:T(8,128)(2,1)S(1)} %collective-permute-done.low_first, bf16[192,1024]{1,0:T(8,128)(2,1)S(1)} %collective-permute-done.1.low_second, ...), custom_call_target="tpu_custom_call" | custom-call | flops 9663676416 | bytes 6291456 | tf_op jit(solution)/shard_map/pallas_call | solution.py:220
  50.0 15.4 %collective-permute-done.4.far_first = bf16[192,1024]{1,0:T(8,128)(2,1)S(1)} collective-permute-done((bf16[192,1024]{1,0:T(8,128)(2,1)S(1)}, bf16[192,1024]{1,0:T(8,128)(2,1)S(1)}, u32[]{:S(2)}, u32[]{:S(2)}) %collective-permute-start.4) | collective-permute-done | bytes 393248 | tf_op jit(solution)/shard_map/ppermute | solution.py:200
  65.4 0.0 collective-permute-done.5.far_second
  65.4 1.3 shard_map.102
  66.7 4.1 %collective-permute-start.6 = (bf16[32,16,512]{2,1,0:T(8,128)(2,1)S(1)}, bf16[32,16,512]{2,1,0:T(8,128)(2,1)S(1)}, u32[]{:S(2)}, u32[]{:S(2)}) collective-permute-start(bf16[32,16,512]{2,1,0:T(8,128)(2,1)S(1)} %get-tuple-element.30), channel_id=1, source_target_pairs={{0,8},{8,0},{1,9},{9,1},{2,10},{10,2},{3,11},{11,3},{4,12},{12,4},... | collective-permute-start | bytes 1572872 | tf_op jit(solution)/shard_map/ppermute | solution.py:244
  70.8 1.5 collective-permute-done.6
  72.3 0.0 copy-start.10
  72.3 0.0 copy-start.9
  72.3 0.0 copy-start.8
  72.3 1.0 add_convert_fusion
  73.3 0.0 all-to-all-done.state
  73.3 11.6 %all-to-all-start.1 = ((bf16[64,8,512]{2,1,0:T(8,128)(2,1)}), bf16[64,8,512]{2,1,0:T(8,128)(2,1)S(1)}, u32[]{:S(2)}, u32[]{:S(2)}) async-start(bf16[64,8,512]{2,1,0:T(8,128)(2,1)} %bitcast.6), calls=%async_computation.1 | async-start | bytes 1048576 | tf_op jit(solution)/shard_map/all_to_all | solution.py:247
  84.9 0.0 copy-done.10
  84.9 5.2 %collective-permute-start.7 = (f32[3,4,256]{2,1,0:T(4,128)S(1)}, f32[3,4,256]{2,1,0:T(4,128)S(1)}, u32[]{:S(2)}, u32[]{:S(2)}) collective-permute-start(f32[3,4,256]{2,1,0:T(4,128)S(1)} %copy-done.10), channel_id=1, source_target_pairs={{0,2},{2,4},{4,6},{6,0},{1,3},{3,5},{5,7},{7,1},{8,10},{10,12},{12... | collective-permute-start | bytes 36872 | tf_op jit(solution)/shard_map/ppermute | solution.py:188
  90.1 0.0 copy-done.9
  90.1 3.1 %collective-permute-start.8 = (f32[3,4,256]{2,1,0:T(4,128)S(1)}, f32[3,4,256]{2,1,0:T(4,128)S(1)}, u32[]{:S(2)}, u32[]{:S(2)}) collective-permute-start(f32[3,4,256]{2,1,0:T(4,128)S(1)} %copy-done.9), channel_id=1, source_target_pairs={{0,4},{2,6},{4,0},{6,2},{1,5},{3,7},{5,1},{7,3},{8,12},{10,14},{12... | collective-permute-start | bytes 36872 | tf_op jit(solution)/shard_map/ppermute | solution.py:188
  93.2 0.0 copy-done.8
  93.2 5.2 %collective-permute-start.9 = (f32[3,4,256]{2,1,0:T(4,128)S(1)}, f32[3,4,256]{2,1,0:T(4,128)S(1)}, u32[]{:S(2)}, u32[]{:S(2)}) collective-permute-start(f32[3,4,256]{2,1,0:T(4,128)S(1)} %copy-done.8), channel_id=1, source_target_pairs={{0,6},{2,0},{4,2},{6,4},{1,7},{3,1},{5,3},{7,5},{8,14},{10,8},{12,... | collective-permute-start | bytes 36872 | tf_op jit(solution)/shard_map/ppermute | solution.py:188
  98.4 0.0 collective-permute-done.7.refs_1_
  98.5 0.0 copy-start.5
  98.5 0.7 collective-permute-done.8.refs_2_
  99.1 0.0 copy-start.6
  99.1 0.1 collective-permute-done.9.refs_3_
  99.3 1.7 %all-to-all-done.1 = bf16[64,8,512]{2,1,0:T(8,128)(2,1)S(1)} async-done(((bf16[64,8,512]{2,1,0:T(8,128)(2,1)}), bf16[64,8,512]{2,1,0:T(8,128)(2,1)S(1)}, u32[]{:S(2)}, u32[]{:S(2)}) %all-to-all-start.1) | async-done | bytes 524320 | tf_op jit(solution)/shard_map/all_to_all | solution.py:247
  100.9 0.1 convert_reduce_fusion.lines
  101.0 0.7 broadcast_in_dim.6
  101.8 7.6 %all-to-all-start.2 = ((bf16[32,8,512]{2,1,0:T(8,128)(2,1)}), bf16[32,8,512]{2,1,0:T(8,128)(2,1)S(1)}, u32[]{:S(2)}, u32[]{:S(2)}) async-start(bf16[32,8,512]{2,1,0:T(8,128)(2,1)} %broadcast_in_dim.6), calls=%async_computation.2 | async-start | bytes 524288 | tf_op jit(solution)/shard_map/all_to_all | solution.py:254
  109.4 9.6 %all-to-all-done.2.shared = bf16[32,8,512]{2,1,0:T(8,128)(2,1)S(1)} async-done(((bf16[32,8,512]{2,1,0:T(8,128)(2,1)}), bf16[32,8,512]{2,1,0:T(8,128)(2,1)S(1)}, u32[]{:S(2)}, u32[]{:S(2)}) %all-to-all-start.2) | async-done | bytes 262176 | tf_op jit(solution)/shard_map/all_to_all | solution.py:254
  119.0 0.1 multiply_reduce_fusion
  119.2 16.8 %all_to_all.20.sums = f32[16,8,256]{2,1,0:T(8,128)S(1)} all-to-all(f32[16,8,256]{2,1,0:T(8,128)S(1)} %bitcast.20), channel_id=1, replica_groups=mesh['x'=4,'y'=8,'core'=2,'tensor'=4,'replica'=2] {'core','tensor','repl..., dimensions={0} | all-to-all | bytes 262144 | tf_op jit(solution)/shard_map/all_to_all | solution.py:263
  136.0 0.7 shard_map.104.mine
  136.7 0.0 copy-done.5
  136.7 0.0 copy-done.6
  136.7 0.0 copy-done.7
  136.7 0.0 copy-done.4
  136.7 3.4 %collective-permute-start.10 = (bf16[32,8,512]{2,1,0:T(8,128)(2,1)S(1)}, bf16[32,8,512]{2,1,0:T(8,128)(2,1)S(1)}, u32[]{:S(2)}, u32[]{:S(2)}) collective-permute-start(bf16[32,8,512]{2,1,0:T(8,128)(2,1)S(1)} %shard_map.104.mine), channel_id=1, source_target_pairs={{0,1},{1,0},{2,3},{3,2},{4,5},{5,4},{6,7},{7,6},{8,9},{9,8},{10,11... | collective-permute-start | bytes 786440 | tf_op jit(solution)/shard_map/ppermute | solution.py:275
  140.1 3.3 %collective-permute-start.11 = (bf16[32,8,512]{2,1,0:T(8,128)(2,1)S(1)}, bf16[32,8,512]{2,1,0:T(8,128)(2,1)S(1)}, u32[]{:S(2)}, u32[]{:S(2)}) collective-permute-start(bf16[32,8,512]{2,1,0:T(8,128)(2,1)S(1)} %shard_map.104.mine), channel_id=1, source_target_pairs={{0,8},{8,0},{1,9},{9,1},{2,10},{10,2},{3,11},{11,3},{4,12},{12,4},... | collective-permute-start | bytes 786440 | tf_op jit(solution)/shard_map/ppermute | solution.py:276
  143.5 0.0 copy-done
  143.5 1.8 %shard_map.105 = (f32[2,8,256]{2,1,0:T(8,128)}, f32[2,8,256]{2,1,0:T(8,128)}, f32[2,8,256]{2,1,0:T(8,128)}, f32[1,1,4,1024]{3,2,1,0:T(4,128)}) custom-call(s32[3]{0:T(128)} %pad_add_fusion.where, f32[16,8,256]{2,1,0:T(8,128)} %copy-done, f32[8,512]{1,0:T(8,128)} %copy-done.4, f32[2,8,256]{2,1,0:T(8,128)} %one.3, f32[2,8,256]{2,1,0:T(8,128)} %two.3, ...), custom_call_target="tpu_custom_call" | custom-call | tf_op jit(solution)/shard_map/pallas_call | solution.py:278
  145.3 0.0 collective-permute-done.10.twin
  145.3 4.0 %collective-permute-start.12 = (bf16[32,8,512]{2,1,0:T(8,128)(2,1)S(1)}, bf16[32,8,512]{2,1,0:T(8,128)(2,1)S(1)}, u32[]{:S(2)}, u32[]{:S(2)}) collective-permute-start(bf16[32,8,512]{2,1,0:T(8,128)(2,1)S(1)} %collective-permute-done.10.twin), channel_id=1, source_target_pairs={{0,8},{8,0},{1,9},{9,1},{2,10},{10,2},{3,11},{11,3},{4,12},{12,4},... | collective-permute-start | bytes 786440 | tf_op jit(solution)/shard_map/ppermute | solution.py:287
  149.3 0.0 collective-permute-done.11.other
  149.3 1.1 collective-permute-done.12.other_twin
  150.4 0.0 copy-done.3
  150.4 1.7 %shard_map.106 = bf16[2,1024,256]{2,1,0:T(8,128)(2,1)} custom-call(s32[3]{0:T(128)S(1)} %copy-done.3, bf16[32,8,512]{2,1,0:T(8,128)(2,1)S(1)} %shard_map.104.mine, bf16[32,8,512]{2,1,0:T(8,128)(2,1)S(1)} %collective-permute-done.10.twin, bf16[32,8,512]{2,1,0:T(8,128)(2,1)S(1)} %collective-permute-done.11.other, ...), custom_call_target="tpu_custom_call" | custom-call | tf_op jit(solution)/shard_map/pallas_call | solution.py:288
  (10 shorter events, 0.1 us)
Async XLA Ops:
  1.8 34.8 %collective-permute-start = (bf16[192,1024]{1,0:T(8,128)(2,1)S(1)}, bf16[192,1024]{1,0:T(8,128)(2,1)S(1)}, u32[]{:S(2)}, u32[]{:S(2)}) collective-permute-start(bf16[192,1024]{1,0:T(8,128)(2,1)S(1)} %get-tuple-element.54), channel_id=1, source_target_pairs={{0,2},{2,4},{4,6},{6,0},{1,3},{3,5},{5,7},{7,1},{8,10},{10,12},{12... | collective-permute-start | bytes 1179656 | tf_op jit(solution)/shard_map/ppermute | solution.py:196
  8.4 30.4 %collective-permute-start.3 = (bf16[192,1024]{1,0:T(8,128)(2,1)S(1)}, bf16[192,1024]{1,0:T(8,128)(2,1)S(1)}, u32[]{:S(2)}, u32[]{:S(2)}) collective-permute-start(bf16[192,1024]{1,0:T(8,128)(2,1)S(1)} %get-tuple-element.53), channel_id=1, source_target_pairs={{0,6},{2,0},{4,2},{6,4},{1,7},{3,1},{5,3},{7,5},{8,14},{10,8},{12,... | collective-permute-start | bytes 1179656 | tf_op jit(solution)/shard_map/ppermute | solution.py:197
  15.2 28.8 %collective-permute-start.1 = (bf16[192,1024]{1,0:T(8,128)(2,1)S(1)}, bf16[192,1024]{1,0:T(8,128)(2,1)S(1)}, u32[]{:S(2)}, u32[]{:S(2)}) collective-permute-start(bf16[192,1024]{1,0:T(8,128)(2,1)S(1)} %get-tuple-element.53), channel_id=1, source_target_pairs={{0,2},{2,4},{4,6},{6,0},{1,3},{3,5},{5,7},{7,1},{8,10},{10,12},{12... | collective-permute-start | bytes 1179656 | tf_op jit(solution)/shard_map/ppermute | solution.py:198
  17.4 30.2 %collective-permute-start.2 = (bf16[192,1024]{1,0:T(8,128)(2,1)S(1)}, bf16[192,1024]{1,0:T(8,128)(2,1)S(1)}, u32[]{:S(2)}, u32[]{:S(2)}) collective-permute-start(bf16[192,1024]{1,0:T(8,128)(2,1)S(1)} %get-tuple-element.54), channel_id=1, source_target_pairs={{0,6},{2,0},{4,2},{6,4},{1,7},{3,1},{5,3},{7,5},{8,14},{10,8},{12,... | collective-permute-start | bytes 1179656 | tf_op jit(solution)/shard_map/ppermute | solution.py:199
  25.1 48.2 %all-to-all-start = ((bf16[32,4,8,512]{3,2,1,0:T(8,128)(2,1)}), bf16[32,4,8,512]{3,2,1,0:T(8,128)(2,1)S(1)}, u32[]{:S(2)}, u32[]{:S(2)}) async-start(bf16[32,4,8,512]{3,2,1,0:T(8,128)(2,1)} %get-tuple-element.31), calls=%async_computation | async-start | bytes 2097152 | tf_op jit(solution)/shard_map/all_to_all | solution.py:217
  34.8 12.8 %copy-start.1 = (bf16[1,384,1024]{2,1,0:T(8,128)(2,1)S(1)}, bf16[1,384,1024]{2,1,0:T(8,128)(2,1)}, u32[]{:S(2)}) copy-start(bf16[1,384,1024]{2,1,0:T(8,128)(2,1)} %param.6) | copy-start | bytes 2359300
  34.8 12.8 %copy-start.2 = (s32[3]{0:T(128)S(1)}, s32[3]{0:T(128)}, u32[]{:S(2)}) copy-start(s32[3]{0:T(128)} %pad_add_fusion.where) | copy-start | bytes 40
  36.6 28.7 %collective-permute-start.4 = (bf16[192,1024]{1,0:T(8,128)(2,1)S(1)}, bf16[192,1024]{1,0:T(8,128)(2,1)S(1)}, u32[]{:S(2)}, u32[]{:S(2)}) collective-permute-start(bf16[192,1024]{1,0:T(8,128)(2,1)S(1)} %collective-permute-done.low_first), channel_id=1, source_target_pairs={{0,2},{2,4},{4,6},{6,0},{1,3},{3,5},{5,7},{7,1},{8,10},{10,12},{12... | collective-permute-start | bytes 1179656 | tf_op jit(solution)/shard_map/ppermute | solution.py:200
  38.8 26.5 %collective-permute-start.5 = (bf16[192,1024]{1,0:T(8,128)(2,1)S(1)}, bf16[192,1024]{1,0:T(8,128)(2,1)S(1)}, u32[]{:S(2)}, u32[]{:S(2)}) collective-permute-start(bf16[192,1024]{1,0:T(8,128)(2,1)S(1)} %collective-permute-done.3.high_second), channel_id=1, source_target_pairs={{0,6},{2,0},{4,2},{6,4},{1,7},{3,1},{5,3},{7,5},{8,14},{10,8},{12,... | collective-permute-start | bytes 1179656 | tf_op jit(solution)/shard_map/ppermute | solution.py:201
  66.7 5.6 %collective-permute-start.6 = (bf16[32,16,512]{2,1,0:T(8,128)(2,1)S(1)}, bf16[32,16,512]{2,1,0:T(8,128)(2,1)S(1)}, u32[]{:S(2)}, u32[]{:S(2)}) collective-permute-start(bf16[32,16,512]{2,1,0:T(8,128)(2,1)S(1)} %get-tuple-element.30), channel_id=1, source_target_pairs={{0,8},{8,0},{1,9},{9,1},{2,10},{10,2},{3,11},{11,3},{4,12},{12,4},... | collective-permute-start | bytes 1572872 | tf_op jit(solution)/shard_map/ppermute | solution.py:244
  72.3 12.6 %copy-start.10 = (f32[3,4,256]{2,1,0:T(4,128)S(1)}, f32[3,4,256]{2,1,0:T(4,128)}, u32[]{:S(2)}) copy-start(f32[3,4,256]{2,1,0:T(4,128)} %get-tuple-element.38) | copy-start | bytes 36868
  72.3 17.8 %copy-start.9 = (f32[3,4,256]{2,1,0:T(4,128)S(1)}, f32[3,4,256]{2,1,0:T(4,128)}, u32[]{:S(2)}) copy-start(f32[3,4,256]{2,1,0:T(4,128)} %get-tuple-element.39) | copy-start | bytes 36868
  72.3 20.9 %copy-start.8 = (f32[3,4,256]{2,1,0:T(4,128)S(1)}, f32[3,4,256]{2,1,0:T(4,128)}, u32[]{:S(2)}) copy-start(f32[3,4,256]{2,1,0:T(4,128)} %get-tuple-element.40) | copy-start | bytes 36868
  73.3 27.6 %all-to-all-start.1 = ((bf16[64,8,512]{2,1,0:T(8,128)(2,1)}), bf16[64,8,512]{2,1,0:T(8,128)(2,1)S(1)}, u32[]{:S(2)}, u32[]{:S(2)}) async-start(bf16[64,8,512]{2,1,0:T(8,128)(2,1)} %bitcast.6), calls=%async_computation.1 | async-start | bytes 1048576 | tf_op jit(solution)/shard_map/all_to_all | solution.py:247
  84.9 13.5 %collective-permute-start.7 = (f32[3,4,256]{2,1,0:T(4,128)S(1)}, f32[3,4,256]{2,1,0:T(4,128)S(1)}, u32[]{:S(2)}, u32[]{:S(2)}) collective-permute-start(f32[3,4,256]{2,1,0:T(4,128)S(1)} %copy-done.10), channel_id=1, source_target_pairs={{0,2},{2,4},{4,6},{6,0},{1,3},{3,5},{5,7},{7,1},{8,10},{10,12},{12... | collective-permute-start | bytes 36872 | tf_op jit(solution)/shard_map/ppermute | solution.py:188
  90.1 9.0 %collective-permute-start.8 = (f32[3,4,256]{2,1,0:T(4,128)S(1)}, f32[3,4,256]{2,1,0:T(4,128)S(1)}, u32[]{:S(2)}, u32[]{:S(2)}) collective-permute-start(f32[3,4,256]{2,1,0:T(4,128)S(1)} %copy-done.9), channel_id=1, source_target_pairs={{0,4},{2,6},{4,0},{6,2},{1,5},{3,7},{5,1},{7,3},{8,12},{10,14},{12... | collective-permute-start | bytes 36872 | tf_op jit(solution)/shard_map/ppermute | solution.py:188
  93.2 6.0 %collective-permute-start.9 = (f32[3,4,256]{2,1,0:T(4,128)S(1)}, f32[3,4,256]{2,1,0:T(4,128)S(1)}, u32[]{:S(2)}, u32[]{:S(2)}) collective-permute-start(f32[3,4,256]{2,1,0:T(4,128)S(1)} %copy-done.8), channel_id=1, source_target_pairs={{0,6},{2,0},{4,2},{6,4},{1,7},{3,1},{5,3},{7,5},{8,14},{10,8},{12,... | collective-permute-start | bytes 36872 | tf_op jit(solution)/shard_map/ppermute | solution.py:188
  98.5 38.2 %copy-start.5 = (f32[3,4,256]{2,1,0:T(4,128)}, f32[3,4,256]{2,1,0:T(4,128)S(1)}, u32[]{:S(2)}) copy-start(f32[3,4,256]{2,1,0:T(4,128)S(1)} %collective-permute-done.7.refs_1_) | copy-start | bytes 36868
  99.1 37.6 %copy-start.6 = (f32[3,4,256]{2,1,0:T(4,128)}, f32[3,4,256]{2,1,0:T(4,128)S(1)}, u32[]{:S(2)}) copy-start(f32[3,4,256]{2,1,0:T(4,128)S(1)} %collective-permute-done.8.refs_2_) | copy-start | bytes 36868
  99.3 37.5 %copy-start.7 = (f32[3,4,256]{2,1,0:T(4,128)}, f32[3,4,256]{2,1,0:T(4,128)S(1)}, u32[]{:S(2)}) copy-start(f32[3,4,256]{2,1,0:T(4,128)S(1)} %collective-permute-done.9.refs_3_) | copy-start | bytes 36868
  101.0 35.7 %copy-start.4 = (f32[8,512]{1,0:T(8,128)}, f32[8,512]{1,0:T(8,128)S(1)}, u32[]{:S(2)}) copy-start(f32[8,512]{1,0:T(8,128)S(1)} %convert_reduce_fusion.lines) | copy-start | bytes 49156
  101.8 48.7 %copy-start.3 = (s32[3]{0:T(128)S(1)}, s32[3]{0:T(128)}, u32[]{:S(2)}) copy-start(s32[3]{0:T(128)} %pad_add_fusion.where) | copy-start | bytes 40
  101.8 17.3 %all-to-all-start.2 = ((bf16[32,8,512]{2,1,0:T(8,128)(2,1)}), bf16[32,8,512]{2,1,0:T(8,128)(2,1)S(1)}, u32[]{:S(2)}, u32[]{:S(2)}) async-start(bf16[32,8,512]{2,1,0:T(8,128)(2,1)} %broadcast_in_dim.6), calls=%async_computation.2 | async-start | bytes 524288 | tf_op jit(solution)/shard_map/all_to_all | solution.py:254
  136.0 7.5 %copy-start = (f32[16,8,256]{2,1,0:T(8,128)}, f32[16,8,256]{2,1,0:T(8,128)S(1)}, u32[]{:S(2)}) copy-start(f32[16,8,256]{2,1,0:T(8,128)S(1)} %all_to_all.20.sums) | copy-start | bytes 393220
  136.7 8.6 %collective-permute-start.10 = (bf16[32,8,512]{2,1,0:T(8,128)(2,1)S(1)}, bf16[32,8,512]{2,1,0:T(8,128)(2,1)S(1)}, u32[]{:S(2)}, u32[]{:S(2)}) collective-permute-start(bf16[32,8,512]{2,1,0:T(8,128)(2,1)S(1)} %shard_map.104.mine), channel_id=1, source_target_pairs={{0,1},{1,0},{2,3},{3,2},{4,5},{5,4},{6,7},{7,6},{8,9},{9,8},{10,11... | collective-permute-start | bytes 786440 | tf_op jit(solution)/shard_map/ppermute | solution.py:275
  140.1 9.2 %collective-permute-start.11 = (bf16[32,8,512]{2,1,0:T(8,128)(2,1)S(1)}, bf16[32,8,512]{2,1,0:T(8,128)(2,1)S(1)}, u32[]{:S(2)}, u32[]{:S(2)}) collective-permute-start(bf16[32,8,512]{2,1,0:T(8,128)(2,1)S(1)} %shard_map.104.mine), channel_id=1, source_target_pairs={{0,8},{8,0},{1,9},{9,1},{2,10},{10,2},{3,11},{11,3},{4,12},{12,4},... | collective-permute-start | bytes 786440 | tf_op jit(solution)/shard_map/ppermute | solution.py:276
  145.3 5.2 %collective-permute-start.12 = (bf16[32,8,512]{2,1,0:T(8,128)(2,1)S(1)}, bf16[32,8,512]{2,1,0:T(8,128)(2,1)S(1)}, u32[]{:S(2)}, u32[]{:S(2)}) collective-permute-start(bf16[32,8,512]{2,1,0:T(8,128)(2,1)S(1)} %collective-permute-done.10.twin), channel_id=1, source_target_pairs={{0,8},{8,0},{1,9},{9,1},{2,10},{10,2},{3,11},{11,3},{4,12},{12,4},... | collective-permute-start | bytes 786440 | tf_op jit(solution)/shard_map/ppermute | solution.py:287

commit v7 on v6

--- a/solution.py
+++ b/solution.py
@@ -17,8 +17,8 @@
 adam_eps = 1e-08
 average_keep = 0.9
 
-XYR = ("x", "y", "replica")
-PLANE = ("x", "y")
+PEERS = ("y", "replica", "x")
+PLANE = ("y", "x")
 SWAP = ((0, 1), (1, 0))
 
 
@@ -58,8 +58,9 @@
     start = lax.rem(where[0] + 2, outgrad.shape[0] // (2 * part)) * (2 * part)
     against = outgrad[pl.ds(pl.multiple_of(start, 2 * part), 2 * part), :]
     first_core = where[1] == 0
-    lines, width = keep.shape[1], keep.shape[2]
-    tile = 256
+    replicas, columns, rows, width = keep.shape[1:]
+    lines = replicas * rows
+    tile = total.shape[0] // columns
     for left in range(0, total.shape[0], tile):
         cut = slice(left, left + tile)
         value = (
@@ -67,11 +68,10 @@
             + along_tokens(far_first[:, cut], against[:part])
             + along_tokens(far_second[:, cut], against[part:])
         )
-        value = value.reshape(tile // (2 * lines), 2, lines, width)
+        value = value.reshape(tile // (2 * lines), 2, replicas, rows, width)
         even, odd = value[:, 0], value[:, 1]
-        out = slice(left // (2 * lines), (left + tile) // (2 * lines))
-        keep[out] = jnp.where(first_core, even, odd)
-        give[out] = jnp.where(first_core, odd, even).astype(give.dtype)
+        keep[:, :, left // tile] = jnp.where(first_core, even, odd)
+        give[:, :, left // tile] = jnp.where(first_core, odd, even).astype(give.dtype)
 
 
 def row_blocks(lines, count):
@@ -106,7 +106,8 @@
 
 
 def clip_of(sums, count):
-    total = jnp.sum(sums[:, sums.shape[1] - 1 :, :], axis=(0, 1), keepdims=True)[0]
+    parts = sums[...].astype(jnp.float32)[:, sums.shape[1] - 4 :, :]
+    total = jnp.sum(parts, axis=(0, 1), keepdims=True)[0]
     total = jnp.sum(total, axis=1, keepdims=True)
     return 1.0 / jnp.sqrt(total / count + 1e-06)
 
@@ -147,14 +148,16 @@
     for source in range(shards_all):
         step = lax.rem(where[0] + shards_all - source, shards_all)
         state = [pick(step, [ref[k] for ref in lent_state]) for k in range(3)]
-        grad = sums[(where[1] * shards_all + source) * 2 + where[2]][: state[0].shape[0]]
+        grad = sums[(source * 2 + where[2]) * 2 + where[1]].astype(jnp.float32)
+        grad = grad[: state[0].shape[0]]
         columns = slice(source * width, (source + 1) * width)
         kept = average_keep * average[0, 0, :, columns]
         out[0, 0, :, columns] = kept + (1.0 - average_keep) * update(clip_factor, grad, *state)[2]
 
 
-def weights_kernel(where, mine, twin, other, other_twin, weights):
+def weights_kernel(columns, where, mine, twin, other, other_twin, weights):
     f32 = jnp.float32
+    lines = mine.shape[0] // columns
     rows, width = mine.shape[1], weights.shape[2]
     core, first = where[1], where[2] == 0
 
@@ -166,19 +169,21 @@
         weights[0, pl.ds(start, 2 * rows), :] = pieces[:, :width]
         weights[1, pl.ds(start, 2 * rows), :] = pieces[:, width:]
 
-    def step(k, carry):
-        place(mine[k], twin[k], (2 * k + core) * 2 * rows)
-        place(other[k], other_twin[k], (2 * k + 1 - core) * 2 * rows)
+    def step(y, carry):
+        for x in range(columns):
+            k, block = y * columns + x, 2 * (x * lines + y)
+            place(mine[k], twin[k], (block + core) * 2 * rows)
+            place(other[k], other_twin[k], (block + 1 - core) * 2 * rows)
         return carry
 
-    lax.fori_loop(0, mine.shape[0], step, 0, unroll=8)
+    lax.fori_loop(0, lines, step, 0, unroll=2)
 
 
 def shards(features, cotangents, moment_one, moment_two, master, average):
     f32, bf16 = jnp.float32, jnp.bfloat16
     col_width = cotangents.shape[3]
     rows = moment_one.shape[1]
-    nx, ny, nr = (lax.axis_size(name) for name in XYR)
+    ny, nr, nx = (lax.axis_size(name) for name in PEERS)
     nt = lax.axis_size("tensor")
     peers = nx * ny * nr
     core = lax.axis_index("core")
@@ -216,7 +221,6 @@
     )(where, moment_one, moment_two, master)
     state = lax.all_to_all(state, PLANE, 0, 0, tiled=True)
 
-    lines = nr * rows
     total = pl.pallas_call(
         near_kernel,
         out_shape=jax.ShapeDtypeStruct((dim_model, width), f32),
@@ -230,8 +234,8 @@
     keep, give = pl.pallas_call(
         far_kernel,
         out_shape=(
-            jax.ShapeDtypeStruct((nx * ny, lines, width), f32),
-            jax.ShapeDtypeStruct((nx * ny, lines, width), bf16),
+            jax.ShapeDtypeStruct((ny, nr, nx, rows, width), f32),
+            jax.ShapeDtypeStruct((ny, nr, nx, rows, width), bf16),
         ),
         in_specs=[scalars] + [local] * 4,
         out_specs=(local, local),
@@ -244,7 +248,7 @@
     got = lax.ppermute(give, "core", SWAP)
     half = (keep + got.astype(f32)).astype(bf16).reshape(peers, rows, width)
     half, state, lent_state = lax.optimization_barrier((half, state, lent_state))
-    terms = lax.all_to_all(half, XYR, split_axis=0, concat_axis=0, tiled=True)
+    terms = lax.all_to_all(half, PEERS, split_axis=0, concat_axis=0, tiled=True)
     lent_state = ring(lent_state)
     terms, lent_state = lax.optimization_barrier((terms, lent_state))
     grad_lines = jnp.sum(terms.astype(f32), axis=0)
@@ -252,14 +256,19 @@
     spread = grad_lines.astype(bf16)
     spread = jnp.broadcast_to(spread[None], (nx * ny,) + spread.shape)
     shared = lax.all_to_all(spread, PLANE, 0, 0, tiled=True)
+    shared, lines_after = lax.optimization_barrier((shared, grad_lines))
     squares = shared.astype(f32)
     squares = jnp.sum(squares * squares, axis=(0, 1))
     squares = squares[:col_width] + squares[col_width:]
-    sums = jnp.transpose(grad_lines.reshape(rows, 2, col_width), (1, 0, 2))
+    high = lax.reduce_precision(squares, 8, 7)
+    middle = lax.reduce_precision(squares - high, 8, 7)
+    squares = jnp.stack([high, middle, squares - high - middle, jnp.zeros_like(squares)])
+    sums = jnp.transpose(lines_after.reshape(rows, 2, col_width), (1, 0, 2))
     sums = sums.reshape(nt, held_rows, col_width)
-    sums = jnp.concatenate([sums, jnp.broadcast_to(squares, sums.shape)], axis=1)
-    sums = jnp.broadcast_to(sums[None, :, None], (2, nt, nr) + sums.shape[1:])
-    others = ("core", "tensor", "replica")
+    squares = jnp.broadcast_to(squares[None], (nt,) + squares.shape)
+    sums = jnp.concatenate([sums, squares], axis=1).astype(bf16)
+    sums = jnp.broadcast_to(sums[:, None, None], (nt, nr, 2) + sums.shape[1:])
+    others = ("tensor", "replica", "core")
     sums = lax.all_to_all(
         sums.reshape((2 * nt * nr,) + sums.shape[3:]), others, 0, 0, tiled=True
     )
@@ -286,7 +295,7 @@
     twin, new_average = lax.optimization_barrier((twin, new_average))
     other_twin = lax.ppermute(twin, "core", SWAP)
     weights = pl.pallas_call(
-        weights_kernel,
+        functools.partial(weights_kernel, nx),
         out_shape=jax.ShapeDtypeStruct((2, dim_model, col_width), bf16),
         in_specs=[scalars] + [local] * 4,
         out_specs=local,

time: 153 us -> 154 us (level)
  waiting for transfers between devices: 33.7 us -> 37.8 us
  starting transfers between devices: 85.4 us -> 81.8 us
    ppermute x1, waiting for transfers between devices: 0.01 us -> 3.34 us  [shards(): twin = lax.ppermute(mine, 'replica', SWAP)]
  transfers between devices with their start and end apart: 16 -> 16, of which waited for: 8 -> 9; matrix products, arithmetic and copies ran while one was open for 2% -> 2% of each run, Pallas kernels for 5% -> 5%
where the time goes in v7:
time: 154 us; the launch traced here: 153 us
  starting transfers between devices  81.8 us (53%)
  waiting for transfers between devices  37.8 us (25%)
  blocking collectives  17.1 us (11%)
  Pallas kernels  9.72 us (6%)
  local copies, waits for them, and re-layouts  3.85 us (2%)
  other arithmetic  1.88 us (1%)
    all_to_all x1, blocking collectives, shards(): lax.all_to_all(sums.reshape((2 * nt * nr,) + sums.shape[3:]), others, 0,...  17.1 us
    ppermute x1, waiting for transfers between devices, shards(): far_first = lax.ppermute(low_first, 'tensor', up)  15.4 us
    ppermute x3, starting transfers between devices, shards(): lax.ppermute(blocks[k], 'tensor', round_trip(nt, k))  13.5 us
    all_to_all x1, starting transfers between devices, shards(): terms = lax.all_to_all(half, PEERS, split_axis=0, concat_axis=0, tiled=True)  11.6 us
    all_to_all x1, waiting for transfers between devices, shards(): shared = lax.all_to_all(spread, PLANE, 0, 0, tiled=True)  10.4 us
    all_to_all x1, starting transfers between devices, shards(): state = lax.all_to_all(state, PLANE, 0, 0, tiled=True)  9.67 us
    all_to_all x1, starting transfers between devices, shards(): shared = lax.all_to_all(spread, PLANE, 0, 0, tiled=True)  7.35 us
    ppermute x1, starting transfers between devices, shards(): high_second = lax.ppermute(second, 'tensor', down)  6.77 us
  transfers between devices with their start and end apart: 16, of which 9 were waited for; matrix products, arithmetic and copies ran while one was open for 2% of the time, Pallas kernels for 5%

profile of v7, /device:TPU:1, one launch (start us, length us, event | category | flops | bytes accessed | tf_op | source)
XLA Modules:
  0.0 153.1 jit_solution(4601184921967526929)
XLA Ops:
  0.6 1.2 slice_bitcast_fusion
  1.8 6.6 %collective-permute-start = (bf16[192,1024]{1,0:T(8,128)(2,1)S(1)}, bf16[192,1024]{1,0:T(8,128)(2,1)S(1)}, u32[]{:S(2)}, u32[]{:S(2)}) collective-permute-start(bf16[192,1024]{1,0:T(8,128)(2,1)S(1)} %get-tuple-element.58), channel_id=1, source_target_pairs={{0,2},{2,4},{4,6},{6,0},{1,3},{3,5},{5,7},{7,1},{8,10},{10,12},{12... | collective-permute-start | bytes 1179656 | tf_op jit(solution)/shard_map/ppermute | solution.py:201
  8.4 6.8 %collective-permute-start.3 = (bf16[192,1024]{1,0:T(8,128)(2,1)S(1)}, bf16[192,1024]{1,0:T(8,128)(2,1)S(1)}, u32[]{:S(2)}, u32[]{:S(2)}) collective-permute-start(bf16[192,1024]{1,0:T(8,128)(2,1)S(1)} %get-tuple-element.57), channel_id=1, source_target_pairs={{0,6},{2,0},{4,2},{6,4},{1,7},{3,1},{5,3},{7,5},{8,14},{10,8},{12,... | collective-permute-start | bytes 1179656 | tf_op jit(solution)/shard_map/ppermute | solution.py:202
  15.2 2.2 %collective-permute-start.1 = (bf16[192,1024]{1,0:T(8,128)(2,1)S(1)}, bf16[192,1024]{1,0:T(8,128)(2,1)S(1)}, u32[]{:S(2)}, u32[]{:S(2)}) collective-permute-start(bf16[192,1024]{1,0:T(8,128)(2,1)S(1)} %get-tuple-element.57), channel_id=1, source_target_pairs={{0,2},{2,4},{4,6},{6,0},{1,3},{3,5},{5,7},{7,1},{8,10},{10,12},{12... | collective-permute-start | bytes 1179656 | tf_op jit(solution)/shard_map/ppermute | solution.py:203
  17.4 5.2 %collective-permute-start.2 = (bf16[192,1024]{1,0:T(8,128)(2,1)S(1)}, bf16[192,1024]{1,0:T(8,128)(2,1)S(1)}, u32[]{:S(2)}, u32[]{:S(2)}) collective-permute-start(bf16[192,1024]{1,0:T(8,128)(2,1)S(1)} %get-tuple-element.58), channel_id=1, source_target_pairs={{0,6},{2,0},{4,2},{6,4},{1,7},{3,1},{5,3},{7,5},{8,14},{10,8},{12,... | collective-permute-start | bytes 1179656 | tf_op jit(solution)/shard_map/ppermute | solution.py:204
  22.6 0.6 pad_add_fusion.where
  23.3 1.9 %shard_map.103 = (bf16[32,4,8,512]{3,2,1,0:T(8,128)(2,1)}, f32[3,4,256]{2,1,0:T(4,128)}, f32[3,4,256]{2,1,0:T(4,128)}, f32[3,4,256]{2,1,0:T(4,128)}, f32[3,4,256]{2,1,0:T(4,128)}) custom-call(s32[3]{0:T(128)} %pad_add_fusion.where, f32[2,8,256]{2,1,0:T(8,128)} %one.3, f32[2,8,256]{2,1,0:T(8,128)} %two.3, f32[2,8,256]{2,1,0:T(8,128)} %held.3), custom_call_target="tpu_custom_call" | custom-call | tf_op jit(solution)/shard_map/pallas_call | solution.py:215
  25.1 9.7 %all-to-all-start = ((bf16[32,4,8,512]{3,2,1,0:T(8,128)(2,1)}), bf16[32,4,8,512]{3,2,1,0:T(8,128)(2,1)S(1)}, u32[]{:S(2)}, u32[]{:S(2)}) async-start(bf16[32,4,8,512]{3,2,1,0:T(8,128)(2,1)} %get-tuple-element.33), calls=%async_computation | async-start | bytes 2097152 | tf_op jit(solution)/shard_map/all_to_all | solution.py:222
  34.8 0.0 copy-start
  34.8 0.0 copy-start.2
  34.8 1.8 %copy.11 = bf16[192,8,2,256]{3,1,2,0:T(8,128)(2,1)S(1)} copy(bf16[192,8,2,256]{3,2,1,0:T(2,128)(2,1)} %bitcast.23) | data formatting | bytes 3145728
  36.7 0.0 collective-permute-done.low_first
  36.7 2.2 %collective-permute-start.4 = (bf16[192,1024]{1,0:T(8,128)(2,1)S(1)}, bf16[192,1024]{1,0:T(8,128)(2,1)S(1)}, u32[]{:S(2)}, u32[]{:S(2)}) collective-permute-start(bf16[192,1024]{1,0:T(8,128)(2,1)S(1)} %collective-permute-done.low_first), channel_id=1, source_target_pairs={{0,2},{2,4},{4,6},{6,0},{1,3},{3,5},{5,7},{7,1},{8,10},{10,12},{12... | collective-permute-start | bytes 1179656 | tf_op jit(solution)/shard_map/ppermute | solution.py:205
  38.8 0.0 collective-permute-done.3.high_second
  38.9 5.2 %collective-permute-start.5 = (bf16[192,1024]{1,0:T(8,128)(2,1)S(1)}, bf16[192,1024]{1,0:T(8,128)(2,1)S(1)}, u32[]{:S(2)}, u32[]{:S(2)}) collective-permute-start(bf16[192,1024]{1,0:T(8,128)(2,1)S(1)} %collective-permute-done.3.high_second), channel_id=1, source_target_pairs={{0,6},{2,0},{4,2},{6,4},{1,7},{3,1},{5,3},{7,5},{8,14},{10,8},{12,... | collective-permute-start | bytes 1179656 | tf_op jit(solution)/shard_map/ppermute | solution.py:206
  44.1 0.0 collective-permute-done.1.low_second
  44.1 3.5 %collective-permute-done.2.high_first = bf16[192,1024]{1,0:T(8,128)(2,1)S(1)} collective-permute-done((bf16[192,1024]{1,0:T(8,128)(2,1)S(1)}, bf16[192,1024]{1,0:T(8,128)(2,1)S(1)}, u32[]{:S(2)}, u32[]{:S(2)}) %collective-permute-start.2) | collective-permute-done | bytes 393248 | tf_op jit(solution)/shard_map/ppermute | solution.py:204
  47.6 0.0 copy-done
  47.6 0.0 copy-done.2
  47.6 2.4 %shard_map.101.total = f32[1024,512]{1,0:T(8,128)S(1)} custom-call(s32[3]{0:T(128)S(1)} %copy-done.2, bf16[384,1024]{1,0:T(8,128)(2,1)S(1)} %bitcast.22, bf16[192,1024]{1,0:T(8,128)(2,1)S(1)} %collective-permute-done.low_first, bf16[192,1024]{1,0:T(8,128)(2,1)S(1)} %collective-permute-done.1.low_second, ...), custom_call_target="tpu_custom_call" | custom-call | flops 9663676416 | bytes 6291456 | tf_op jit(solution)/shard_map/pallas_call | solution.py:224
  50.0 15.4 %collective-permute-done.4.far_first = bf16[192,1024]{1,0:T(8,128)(2,1)S(1)} collective-permute-done((bf16[192,1024]{1,0:T(8,128)(2,1)S(1)}, bf16[192,1024]{1,0:T(8,128)(2,1)S(1)}, u32[]{:S(2)}, u32[]{:S(2)}) %collective-permute-start.4) | collective-permute-done | bytes 393248 | tf_op jit(solution)/shard_map/ppermute | solution.py:205
  65.4 0.0 collective-permute-done.5.far_second
  65.4 1.3 shard_map.102
  66.7 4.1 %collective-permute-start.6 = (bf16[8,2,4,8,512]{4,3,2,1,0:T(8,128)(2,1)S(1)}, bf16[8,2,4,8,512]{4,3,2,1,0:T(8,128)(2,1)S(1)}, u32[]{:S(2)}, u32[]{:S(2)}) collective-permute-start(bf16[8,2,4,8,512]{4,3,2,1,0:T(8,128)(2,1)S(1)} %get-tuple-element.32), channel_id=1, source_target_pairs={{0,8},{8,0},{1,9},{9,1},{2,10},{10,2},{3,11},{11,3},{4,12},{12,4},... | collective-permute-start | bytes 1572872 | tf_op jit(solution)/shard_map/ppermute | solution.py:248
  70.8 1.5 collective-permute-done.6
  72.3 0.0 copy-start.10
  72.3 1.0 add_convert_fusion
  73.3 0.0 all-to-all-done.state
  73.3 11.6 %all-to-all-start.1 = ((bf16[64,8,512]{2,1,0:T(8,128)(2,1)}), bf16[64,8,512]{2,1,0:T(8,128)(2,1)S(1)}, u32[]{:S(2)}, u32[]{:S(2)}) async-start(bf16[64,8,512]{2,1,0:T(8,128)(2,1)} %bitcast.6), calls=%async_computation.1 | async-start | bytes 1048576 | tf_op jit(solution)/shard_map/all_to_all | solution.py:251
  84.9 0.0 copy-done.10
  84.9 5.2 %collective-permute-start.7 = (f32[3,4,256]{2,1,0:T(4,128)S(1)}, f32[3,4,256]{2,1,0:T(4,128)S(1)}, u32[]{:S(2)}, u32[]{:S(2)}) collective-permute-start(f32[3,4,256]{2,1,0:T(4,128)S(1)} %copy-done.10), channel_id=1, source_target_pairs={{0,2},{2,4},{4,6},{6,0},{1,3},{3,5},{5,7},{7,1},{8,10},{10,12},{12... | collective-permute-start | bytes 36872 | tf_op jit(solution)/shard_map/ppermute | solution.py:193
  90.1 0.0 copy-done.9
  90.1 3.1 %collective-permute-start.8 = (f32[3,4,256]{2,1,0:T(4,128)S(1)}, f32[3,4,256]{2,1,0:T(4,128)S(1)}, u32[]{:S(2)}, u32[]{:S(2)}) collective-permute-start(f32[3,4,256]{2,1,0:T(4,128)S(1)} %copy-done.9), channel_id=1, source_target_pairs={{0,4},{2,6},{4,0},{6,2},{1,5},{3,7},{5,1},{7,3},{8,12},{10,14},{12... | collective-permute-start | bytes 36872 | tf_op jit(solution)/shard_map/ppermute | solution.py:193
  93.2 0.0 copy-done.8
  93.2 5.2 %collective-permute-start.9 = (f32[3,4,256]{2,1,0:T(4,128)S(1)}, f32[3,4,256]{2,1,0:T(4,128)S(1)}, u32[]{:S(2)}, u32[]{:S(2)}) collective-permute-start(f32[3,4,256]{2,1,0:T(4,128)S(1)} %copy-done.8), channel_id=1, source_target_pairs={{0,6},{2,0},{4,2},{6,4},{1,7},{3,1},{5,3},{7,5},{8,14},{10,8},{12,... | collective-permute-start | bytes 36872 | tf_op jit(solution)/shard_map/ppermute | solution.py:193
  98.4 0.0 collective-permute-done.7.refs_1_
  98.4 0.0 copy-start.5
  98.5 0.5 collective-permute-done.8.refs_2_
  99.0 0.3 collective-permute-done.9.refs_3_
  99.2 1.8 %all-to-all-done.1 = bf16[64,8,512]{2,1,0:T(8,128)(2,1)S(1)} async-done(((bf16[64,8,512]{2,1,0:T(8,128)(2,1)}), bf16[64,8,512]{2,1,0:T(8,128)(2,1)S(1)}, u32[]{:S(2)}, u32[]{:S(2)}) %all-to-all-start.1) | async-done | bytes 524320 | tf_op jit(solution)/shard_map/all_to_all | solution.py:251
  101.0 0.1 convert_reduce_fusion.lines
  101.1 0.0 copy-start.3
  101.1 0.7 broadcast_in_dim.6
  101.8 7.3 %all-to-all-start.2 = ((bf16[32,8,512]{2,1,0:T(8,128)(2,1)}), bf16[32,8,512]{2,1,0:T(8,128)(2,1)S(1)}, u32[]{:S(2)}, u32[]{:S(2)}) async-start(bf16[32,8,512]{2,1,0:T(8,128)(2,1)} %broadcast_in_dim.6), calls=%async_computation.2 | async-start | bytes 524288 | tf_op jit(solution)/shard_map/all_to_all | solution.py:258
  109.2 0.1 pad.5.clone
  109.3 10.4 %all-to-all-done.2.shared = bf16[32,8,512]{2,1,0:T(8,128)(2,1)S(1)} async-done(((bf16[32,8,512]{2,1,0:T(8,128)(2,1)}), bf16[32,8,512]{2,1,0:T(8,128)(2,1)S(1)}, u32[]{:S(2)}, u32[]{:S(2)}) %all-to-all-start.2) | async-done | bytes 262176 | tf_op jit(solution)/shard_map/all_to_all | solution.py:258
  119.7 0.1 multiply_reduce_fusion
  119.8 0.1 maximum_convert_fusion
  119.9 17.1 %all_to_all.20.sums = bf16[16,8,256]{2,1,0:T(8,128)(2,1)S(1)} all-to-all(bf16[16,8,256]{2,1,0:T(8,128)(2,1)S(1)} %bitcast.24), channel_id=1, replica_groups=mesh['x'=4,'y'=8,'core'=2,'tensor'=4,'replica'=2] {'tensor','replica','c..., dimensions={0} | all-to-all | bytes 131072 | tf_op jit(solution)/shard_map/all_to_all | solution.py:272
  137.0 0.7 shard_map.104.mine
  137.7 0.0 copy-done.5
  137.7 0.0 copy-done.6
  137.7 0.0 copy-done.7
  137.7 2.1 %collective-permute-start.10 = (bf16[32,8,512]{2,1,0:T(8,128)(2,1)S(1)}, bf16[32,8,512]{2,1,0:T(8,128)(2,1)S(1)}, u32[]{:S(2)}, u32[]{:S(2)}) collective-permute-start(bf16[32,8,512]{2,1,0:T(8,128)(2,1)S(1)} %shard_map.104.mine), channel_id=1, source_target_pairs={{0,1},{1,0},{2,3},{3,2},{4,5},{5,4},{6,7},{7,6},{8,9},{9,8},{10,11... | collective-permute-start | bytes 786440 | tf_op jit(solution)/shard_map/ppermute | solution.py:284
  139.8 2.5 %collective-permute-start.11 = (bf16[32,8,512]{2,1,0:T(8,128)(2,1)S(1)}, bf16[32,8,512]{2,1,0:T(8,128)(2,1)S(1)}, u32[]{:S(2)}, u32[]{:S(2)}) collective-permute-start(bf16[32,8,512]{2,1,0:T(8,128)(2,1)S(1)} %shard_map.104.mine), channel_id=1, source_target_pairs={{0,8},{8,0},{1,9},{9,1},{2,10},{10,2},{3,11},{11,3},{4,12},{12,4},... | collective-permute-start | bytes 786440 | tf_op jit(solution)/shard_map/ppermute | solution.py:285
  142.3 0.0 copy-done.4
  142.3 0.0 copy-done.1
  142.3 1.7 %shard_map.105 = (f32[2,8,256]{2,1,0:T(8,128)}, f32[2,8,256]{2,1,0:T(8,128)}, f32[2,8,256]{2,1,0:T(8,128)}, f32[1,1,4,1024]{3,2,1,0:T(4,128)}) custom-call(s32[3]{0:T(128)} %pad_add_fusion.where, bf16[16,8,256]{2,1,0:T(8,128)(2,1)} %copy-done.1, f32[8,512]{1,0:T(8,128)} %copy-done.4, f32[2,8,256]{2,1,0:T(8,128)} %one.3, f32[2,8,256]{2,1,0:T(8,128)} %two.3, ...), custom_call_target="tpu_custom_call" | custom-call | tf_op jit(solution)/shard_map/pallas_call | solution.py:287
  144.0 3.3 %collective-permute-done.10.twin = bf16[32,8,512]{2,1,0:T(8,128)(2,1)S(1)} collective-permute-done((bf16[32,8,512]{2,1,0:T(8,128)(2,1)S(1)}, bf16[32,8,512]{2,1,0:T(8,128)(2,1)S(1)}, u32[]{:S(2)}, u32[]{:S(2)}) %collective-permute-start.10) | collective-permute-done | bytes 262176 | tf_op jit(solution)/shard_map/ppermute | solution.py:284
  147.3 2.9 %collective-permute-start.12 = (bf16[32,8,512]{2,1,0:T(8,128)(2,1)S(1)}, bf16[32,8,512]{2,1,0:T(8,128)(2,1)S(1)}, u32[]{:S(2)}, u32[]{:S(2)}) collective-permute-start(bf16[32,8,512]{2,1,0:T(8,128)(2,1)S(1)} %collective-permute-done.10.twin), channel_id=1, source_target_pairs={{0,8},{8,0},{1,9},{9,1},{2,10},{10,2},{3,11},{11,3},{4,12},{12,4},... | collective-permute-start | bytes 786440 | tf_op jit(solution)/shard_map/ppermute | solution.py:296
  150.2 0.0 collective-permute-done.11.other
  150.2 1.1 collective-permute-done.12.other_twin
  151.4 0.0 copy-done.3
  151.4 1.7 %shard_map.106 = bf16[2,1024,256]{2,1,0:T(8,128)(2,1)} custom-call(s32[3]{0:T(128)S(1)} %copy-done.3, bf16[32,8,512]{2,1,0:T(8,128)(2,1)S(1)} %shard_map.104.mine, bf16[32,8,512]{2,1,0:T(8,128)(2,1)S(1)} %collective-permute-done.10.twin, bf16[32,8,512]{2,1,0:T(8,128)(2,1)S(1)} %collective-permute-done.11.other, ...), custom_call_target="tpu_custom_call" | custom-call | tf_op jit(solution)/shard_map/pallas_call | solution.py:297
  (13 shorter events, 0.1 us)
Async XLA Ops:
  1.8 34.9 %collective-permute-start = (bf16[192,1024]{1,0:T(8,128)(2,1)S(1)}, bf16[192,1024]{1,0:T(8,128)(2,1)S(1)}, u32[]{:S(2)}, u32[]{:S(2)}) collective-permute-start(bf16[192,1024]{1,0:T(8,128)(2,1)S(1)} %get-tuple-element.58), channel_id=1, source_target_pairs={{0,2},{2,4},{4,6},{6,0},{1,3},{3,5},{5,7},{7,1},{8,10},{10,12},{12... | collective-permute-start | bytes 1179656 | tf_op jit(solution)/shard_map/ppermute | solution.py:201
  8.4 30.4 %collective-permute-start.3 = (bf16[192,1024]{1,0:T(8,128)(2,1)S(1)}, bf16[192,1024]{1,0:T(8,128)(2,1)S(1)}, u32[]{:S(2)}, u32[]{:S(2)}) collective-permute-start(bf16[192,1024]{1,0:T(8,128)(2,1)S(1)} %get-tuple-element.57), channel_id=1, source_target_pairs={{0,6},{2,0},{4,2},{6,4},{1,7},{3,1},{5,3},{7,5},{8,14},{10,8},{12,... | collective-permute-start | bytes 1179656 | tf_op jit(solution)/shard_map/ppermute | solution.py:202
  15.2 28.9 %collective-permute-start.1 = (bf16[192,1024]{1,0:T(8,128)(2,1)S(1)}, bf16[192,1024]{1,0:T(8,128)(2,1)S(1)}, u32[]{:S(2)}, u32[]{:S(2)}) collective-permute-start(bf16[192,1024]{1,0:T(8,128)(2,1)S(1)} %get-tuple-element.57), channel_id=1, source_target_pairs={{0,2},{2,4},{4,6},{6,0},{1,3},{3,5},{5,7},{7,1},{8,10},{10,12},{12... | collective-permute-start | bytes 1179656 | tf_op jit(solution)/shard_map/ppermute | solution.py:203
  17.4 30.2 %collective-permute-start.2 = (bf16[192,1024]{1,0:T(8,128)(2,1)S(1)}, bf16[192,1024]{1,0:T(8,128)(2,1)S(1)}, u32[]{:S(2)}, u32[]{:S(2)}) collective-permute-start(bf16[192,1024]{1,0:T(8,128)(2,1)S(1)} %get-tuple-element.58), channel_id=1, source_target_pairs={{0,6},{2,0},{4,2},{6,4},{1,7},{3,1},{5,3},{7,5},{8,14},{10,8},{12,... | collective-permute-start | bytes 1179656 | tf_op jit(solution)/shard_map/ppermute | solution.py:204
  25.1 48.2 %all-to-all-start = ((bf16[32,4,8,512]{3,2,1,0:T(8,128)(2,1)}), bf16[32,4,8,512]{3,2,1,0:T(8,128)(2,1)S(1)}, u32[]{:S(2)}, u32[]{:S(2)}) async-start(bf16[32,4,8,512]{3,2,1,0:T(8,128)(2,1)} %get-tuple-element.33), calls=%async_computation | async-start | bytes 2097152 | tf_op jit(solution)/shard_map/all_to_all | solution.py:222
  34.8 12.8 %copy-start = (bf16[1,384,1024]{2,1,0:T(8,128)(2,1)S(1)}, bf16[1,384,1024]{2,1,0:T(8,128)(2,1)}, u32[]{:S(2)}) copy-start(bf16[1,384,1024]{2,1,0:T(8,128)(2,1)} %param.6) | copy-start | bytes 2359300
  34.8 12.8 %copy-start.2 = (s32[3]{0:T(128)S(1)}, s32[3]{0:T(128)}, u32[]{:S(2)}) copy-start(s32[3]{0:T(128)} %pad_add_fusion.where) | copy-start | bytes 40
  36.7 28.7 %collective-permute-start.4 = (bf16[192,1024]{1,0:T(8,128)(2,1)S(1)}, bf16[192,1024]{1,0:T(8,128)(2,1)S(1)}, u32[]{:S(2)}, u32[]{:S(2)}) collective-permute-start(bf16[192,1024]{1,0:T(8,128)(2,1)S(1)} %collective-permute-done.low_first), channel_id=1, source_target_pairs={{0,2},{2,4},{4,6},{6,0},{1,3},{3,5},{5,7},{7,1},{8,10},{10,12},{12... | collective-permute-start | bytes 1179656 | tf_op jit(solution)/shard_map/ppermute | solution.py:205
  38.9 26.5 %collective-permute-start.5 = (bf16[192,1024]{1,0:T(8,128)(2,1)S(1)}, bf16[192,1024]{1,0:T(8,128)(2,1)S(1)}, u32[]{:S(2)}, u32[]{:S(2)}) collective-permute-start(bf16[192,1024]{1,0:T(8,128)(2,1)S(1)} %collective-permute-done.3.high_second), channel_id=1, source_target_pairs={{0,6},{2,0},{4,2},{6,4},{1,7},{3,1},{5,3},{7,5},{8,14},{10,8},{12,... | collective-permute-start | bytes 1179656 | tf_op jit(solution)/shard_map/ppermute | solution.py:206
  66.7 5.6 %collective-permute-start.6 = (bf16[8,2,4,8,512]{4,3,2,1,0:T(8,128)(2,1)S(1)}, bf16[8,2,4,8,512]{4,3,2,1,0:T(8,128)(2,1)S(1)}, u32[]{:S(2)}, u32[]{:S(2)}) collective-permute-start(bf16[8,2,4,8,512]{4,3,2,1,0:T(8,128)(2,1)S(1)} %get-tuple-element.32), channel_id=1, source_target_pairs={{0,8},{8,0},{1,9},{9,1},{2,10},{10,2},{3,11},{11,3},{4,12},{12,4},... | collective-permute-start | bytes 1572872 | tf_op jit(solution)/shard_map/ppermute | solution.py:248
  72.3 12.6 %copy-start.10 = (f32[3,4,256]{2,1,0:T(4,128)S(1)}, f32[3,4,256]{2,1,0:T(4,128)}, u32[]{:S(2)}) copy-start(f32[3,4,256]{2,1,0:T(4,128)} %get-tuple-element.40) | copy-start | bytes 36868
  72.3 17.8 %copy-start.9 = (f32[3,4,256]{2,1,0:T(4,128)S(1)}, f32[3,4,256]{2,1,0:T(4,128)}, u32[]{:S(2)}) copy-start(f32[3,4,256]{2,1,0:T(4,128)} %get-tuple-element.41) | copy-start | bytes 36868
  72.3 20.9 %copy-start.8 = (f32[3,4,256]{2,1,0:T(4,128)S(1)}, f32[3,4,256]{2,1,0:T(4,128)}, u32[]{:S(2)}) copy-start(f32[3,4,256]{2,1,0:T(4,128)} %get-tuple-element.42) | copy-start | bytes 36868
  73.3 27.7 %all-to-all-start.1 = ((bf16[64,8,512]{2,1,0:T(8,128)(2,1)}), bf16[64,8,512]{2,1,0:T(8,128)(2,1)S(1)}, u32[]{:S(2)}, u32[]{:S(2)}) async-start(bf16[64,8,512]{2,1,0:T(8,128)(2,1)} %bitcast.6), calls=%async_computation.1 | async-start | bytes 1048576 | tf_op jit(solution)/shard_map/all_to_all | solution.py:251
  84.9 13.5 %collective-permute-start.7 = (f32[3,4,256]{2,1,0:T(4,128)S(1)}, f32[3,4,256]{2,1,0:T(4,128)S(1)}, u32[]{:S(2)}, u32[]{:S(2)}) collective-permute-start(f32[3,4,256]{2,1,0:T(4,128)S(1)} %copy-done.10), channel_id=1, source_target_pairs={{0,2},{2,4},{4,6},{6,0},{1,3},{3,5},{5,7},{7,1},{8,10},{10,12},{12... | collective-permute-start | bytes 36872 | tf_op jit(solution)/shard_map/ppermute | solution.py:193
  90.1 8.9 %collective-permute-start.8 = (f32[3,4,256]{2,1,0:T(4,128)S(1)}, f32[3,4,256]{2,1,0:T(4,128)S(1)}, u32[]{:S(2)}, u32[]{:S(2)}) collective-permute-start(f32[3,4,256]{2,1,0:T(4,128)S(1)} %copy-done.9), channel_id=1, source_target_pairs={{0,4},{2,6},{4,0},{6,2},{1,5},{3,7},{5,1},{7,3},{8,12},{10,14},{12... | collective-permute-start | bytes 36872 | tf_op jit(solution)/shard_map/ppermute | solution.py:193
  93.2 6.0 %collective-permute-start.9 = (f32[3,4,256]{2,1,0:T(4,128)S(1)}, f32[3,4,256]{2,1,0:T(4,128)S(1)}, u32[]{:S(2)}, u32[]{:S(2)}) collective-permute-start(f32[3,4,256]{2,1,0:T(4,128)S(1)} %copy-done.8), channel_id=1, source_target_pairs={{0,6},{2,0},{4,2},{6,4},{1,7},{3,1},{5,3},{7,5},{8,14},{10,8},{12,... | collective-permute-start | bytes 36872 | tf_op jit(solution)/shard_map/ppermute | solution.py:193
  98.4 39.2 %copy-start.5 = (f32[3,4,256]{2,1,0:T(4,128)}, f32[3,4,256]{2,1,0:T(4,128)S(1)}, u32[]{:S(2)}) copy-start(f32[3,4,256]{2,1,0:T(4,128)S(1)} %collective-permute-done.7.refs_1_) | copy-start | bytes 36868
  99.0 38.7 %copy-start.6 = (f32[3,4,256]{2,1,0:T(4,128)}, f32[3,4,256]{2,1,0:T(4,128)S(1)}, u32[]{:S(2)}) copy-start(f32[3,4,256]{2,1,0:T(4,128)S(1)} %collective-permute-done.8.refs_2_) | copy-start | bytes 36868
  99.2 38.5 %copy-start.7 = (f32[3,4,256]{2,1,0:T(4,128)}, f32[3,4,256]{2,1,0:T(4,128)S(1)}, u32[]{:S(2)}) copy-start(f32[3,4,256]{2,1,0:T(4,128)S(1)} %collective-permute-done.9.refs_3_) | copy-start | bytes 36868
  101.1 41.2 %copy-start.4 = (f32[8,512]{1,0:T(8,128)}, f32[8,512]{1,0:T(8,128)S(1)}, u32[]{:S(2)}) copy-start(f32[8,512]{1,0:T(8,128)S(1)} %convert_reduce_fusion.lines) | copy-start | bytes 49156
  101.1 50.2 %copy-start.3 = (s32[3]{0:T(128)S(1)}, s32[3]{0:T(128)}, u32[]{:S(2)}) copy-start(s32[3]{0:T(128)} %pad_add_fusion.where) | copy-start | bytes 40
  101.8 17.8 %all-to-all-start.2 = ((bf16[32,8,512]{2,1,0:T(8,128)(2,1)}), bf16[32,8,512]{2,1,0:T(8,128)(2,1)S(1)}, u32[]{:S(2)}, u32[]{:S(2)}) async-start(bf16[32,8,512]{2,1,0:T(8,128)(2,1)} %broadcast_in_dim.6), calls=%async_computation.2 | async-start | bytes 524288 | tf_op jit(solution)/shard_map/all_to_all | solution.py:258
  137.0 5.3 %copy-start.1 = (bf16[16,8,256]{2,1,0:T(8,128)(2,1)}, bf16[16,8,256]{2,1,0:T(8,128)(2,1)S(1)}, u32[]{:S(2)}) copy-start(bf16[16,8,256]{2,1,0:T(8,128)(2,1)S(1)} %all_to_all.20.sums) | copy-start | bytes 196612
  137.7 9.6 %collective-permute-start.10 = (bf16[32,8,512]{2,1,0:T(8,128)(2,1)S(1)}, bf16[32,8,512]{2,1,0:T(8,128)(2,1)S(1)}, u32[]{:S(2)}, u32[]{:S(2)}) collective-permute-start(bf16[32,8,512]{2,1,0:T(8,128)(2,1)S(1)} %shard_map.104.mine), channel_id=1, source_target_pairs={{0,1},{1,0},{2,3},{3,2},{4,5},{5,4},{6,7},{7,6},{8,9},{9,8},{10,11... | collective-permute-start | bytes 786440 | tf_op jit(solution)/shard_map/ppermute | solution.py:284
  139.8 10.4 %collective-permute-start.11 = (bf16[32,8,512]{2,1,0:T(8,128)(2,1)S(1)}, bf16[32,8,512]{2,1,0:T(8,128)(2,1)S(1)}, u32[]{:S(2)}, u32[]{:S(2)}) collective-permute-start(bf16[32,8,512]{2,1,0:T(8,128)(2,1)S(1)} %shard_map.104.mine), channel_id=1, source_target_pairs={{0,8},{8,0},{1,9},{9,1},{2,10},{10,2},{3,11},{11,3},{4,12},{12,4},... | collective-permute-start | bytes 786440 | tf_op jit(solution)/shard_map/ppermute | solution.py:285
  147.3 4.0 %collective-permute-start.12 = (bf16[32,8,512]{2,1,0:T(8,128)(2,1)S(1)}, bf16[32,8,512]{2,1,0:T(8,128)(2,1)S(1)}, u32[]{:S(2)}, u32[]{:S(2)}) collective-permute-start(bf16[32,8,512]{2,1,0:T(8,128)(2,1)S(1)} %collective-permute-done.10.twin), channel_id=1, source_target_pairs={{0,8},{8,0},{1,9},{9,1},{2,10},{10,2},{3,11},{11,3},{4,12},{12,4},... | collective-permute-start | bytes 786440 | tf_op jit(solution)/shard_map/ppermute | solution.py:296

commit v8 on v7

--- a/solution.py
+++ b/solution.py
@@ -189,9 +189,6 @@
     core = lax.axis_index("core")
     place = lax.axis_index("tensor")
     where = jnp.stack([place, core, lax.axis_index("replica")]).astype(jnp.int32)
-    ring = lambda blocks: [blocks[0]] + [
-        lax.ppermute(blocks[k], "tensor", round_trip(nt, k)) for k in range(1, nt)
-    ]
 
     tokens = features[0]
     count, dim_model = tokens.shape
@@ -249,14 +246,16 @@
     half = (keep + got.astype(f32)).astype(bf16).reshape(peers, rows, width)
     half, state, lent_state = lax.optimization_barrier((half, state, lent_state))
     terms = lax.all_to_all(half, PEERS, split_axis=0, concat_axis=0, tiled=True)
-    lent_state = ring(lent_state)
+    for step in range(1, nt - 1):
+        lent_state[step] = lax.ppermute(lent_state[step], "tensor", round_trip(nt, step))
     terms, lent_state = lax.optimization_barrier((terms, lent_state))
     grad_lines = jnp.sum(terms.astype(f32), axis=0)
 
     spread = grad_lines.astype(bf16)
     spread = jnp.broadcast_to(spread[None], (nx * ny,) + spread.shape)
     shared = lax.all_to_all(spread, PLANE, 0, 0, tiled=True)
-    shared, lines_after = lax.optimization_barrier((shared, grad_lines))
+    lent_state[-1] = lax.ppermute(lent_state[-1], "tensor", round_trip(nt, nt - 1))
+    shared, lines_after, lent_state = lax.optimization_barrier((shared, grad_lines, lent_state))
     squares = shared.astype(f32)
     squares = jnp.sum(squares * squares, axis=(0, 1))
     squares = squares[:col_width] + squares[col_width:]

time: 154 us -> 153 us (level)
  starting transfers between devices: 81.8 us -> 79.8 us
  waiting for transfers between devices: 37.8 us -> 39.4 us
    ppermute x3, waiting for transfers between devices: 0.79 us -> 7.61 us  [the longest x2 5.75 us: shards(): lax.ppermute(lent_state[step], 'tensor', round_trip(nt, step))]
    all_to_all x1, waiting for transfers between devices: 10.4 us -> 4.85 us  [shards(): shared = lax.all_to_all(spread, PLANE, 0, 0, tiled=True)]
    ppermute x3, starting transfers between devices: 13.5 us -> 11.9 us  [the longest x2 8.29 us: shards(): lax.ppermute(lent_state[step], 'tensor', round_trip(nt, step))]
where the time goes in v8:
time: 153 us; the launch traced here: 152 us
  starting transfers between devices  79.8 us (52%)
  waiting for transfers between devices  39.4 us (26%)
  blocking collectives  16.3 us (11%)
  Pallas kernels  9.72 us (6%)
  local copies, waits for them, and re-layouts  3.85 us (3%)
  other arithmetic  1.86 us (1%)
    all_to_all x1, blocking collectives, shards(): lax.all_to_all(sums.reshape((2 * nt * nr,) + sums.shape[3:]), others, 0,...  16.3 us
    ppermute x1, waiting for transfers between devices, shards(): far_first = lax.ppermute(low_first, 'tensor', up)  15.4 us
    all_to_all x1, starting transfers between devices, shards(): terms = lax.all_to_all(half, PEERS, split_axis=0, concat_axis=0, tiled=True)  11.7 us
    all_to_all x1, starting transfers between devices, shards(): state = lax.all_to_all(state, PLANE, 0, 0, tiled=True)  9.67 us
    ppermute x2, starting transfers between devices, shards(): lax.ppermute(lent_state[step], 'tensor', round_trip(nt, step))  8.29 us
    all_to_all x1, starting transfers between devices, shards(): shared = lax.all_to_all(spread, PLANE, 0, 0, tiled=True)  6.87 us
    ppermute x1, starting transfers between devices, shards(): high_second = lax.ppermute(second, 'tensor', down)  6.77 us
    ppermute x1, starting transfers between devices, shards(): low_first = lax.ppermute(first, 'tensor', up)  6.64 us
  transfers between devices with their start and end apart: 16, of which 9 were waited for; matrix products, arithmetic and copies ran while one was open for 2% of the time, Pallas kernels for 5%

profile of v8, /device:TPU:1, one launch (start us, length us, event | category | flops | bytes accessed | tf_op | source)
XLA Modules:
  0.0 151.9 jit_solution(3330972715479433195)
XLA Ops:
  0.6 1.2 slice_bitcast_fusion
  1.8 6.6 %collective-permute-start = (bf16[192,1024]{1,0:T(8,128)(2,1)S(1)}, bf16[192,1024]{1,0:T(8,128)(2,1)S(1)}, u32[]{:S(2)}, u32[]{:S(2)}) collective-permute-start(bf16[192,1024]{1,0:T(8,128)(2,1)S(1)} %get-tuple-element.66), channel_id=1, source_target_pairs={{0,2},{2,4},{4,6},{6,0},{1,3},{3,5},{5,7},{7,1},{8,10},{10,12},{12... | collective-permute-start | bytes 1179656 | tf_op jit(solution)/shard_map/ppermute | solution.py:198
  8.4 6.8 %collective-permute-start.3 = (bf16[192,1024]{1,0:T(8,128)(2,1)S(1)}, bf16[192,1024]{1,0:T(8,128)(2,1)S(1)}, u32[]{:S(2)}, u32[]{:S(2)}) collective-permute-start(bf16[192,1024]{1,0:T(8,128)(2,1)S(1)} %get-tuple-element.65), channel_id=1, source_target_pairs={{0,6},{2,0},{4,2},{6,4},{1,7},{3,1},{5,3},{7,5},{8,14},{10,8},{12,... | collective-permute-start | bytes 1179656 | tf_op jit(solution)/shard_map/ppermute | solution.py:199
  15.2 2.2 %collective-permute-start.1 = (bf16[192,1024]{1,0:T(8,128)(2,1)S(1)}, bf16[192,1024]{1,0:T(8,128)(2,1)S(1)}, u32[]{:S(2)}, u32[]{:S(2)}) collective-permute-start(bf16[192,1024]{1,0:T(8,128)(2,1)S(1)} %get-tuple-element.65), channel_id=1, source_target_pairs={{0,2},{2,4},{4,6},{6,0},{1,3},{3,5},{5,7},{7,1},{8,10},{10,12},{12... | collective-permute-start | bytes 1179656 | tf_op jit(solution)/shard_map/ppermute | solution.py:200
  17.4 5.2 %collective-permute-start.2 = (bf16[192,1024]{1,0:T(8,128)(2,1)S(1)}, bf16[192,1024]{1,0:T(8,128)(2,1)S(1)}, u32[]{:S(2)}, u32[]{:S(2)}) collective-permute-start(bf16[192,1024]{1,0:T(8,128)(2,1)S(1)} %get-tuple-element.66), channel_id=1, source_target_pairs={{0,6},{2,0},{4,2},{6,4},{1,7},{3,1},{5,3},{7,5},{8,14},{10,8},{12,... | collective-permute-start | bytes 1179656 | tf_op jit(solution)/shard_map/ppermute | solution.py:201
  22.6 0.6 pad_add_fusion.where
  23.2 1.9 %shard_map.103 = (bf16[32,4,8,512]{3,2,1,0:T(8,128)(2,1)}, f32[3,4,256]{2,1,0:T(4,128)}, f32[3,4,256]{2,1,0:T(4,128)}, f32[3,4,256]{2,1,0:T(4,128)}, f32[3,4,256]{2,1,0:T(4,128)}) custom-call(s32[3]{0:T(128)} %pad_add_fusion.where, f32[2,8,256]{2,1,0:T(8,128)} %one.3, f32[2,8,256]{2,1,0:T(8,128)} %two.3, f32[2,8,256]{2,1,0:T(8,128)} %held.3), custom_call_target="tpu_custom_call" | custom-call | tf_op jit(solution)/shard_map/pallas_call | solution.py:212
  25.1 9.7 %all-to-all-start = ((bf16[32,4,8,512]{3,2,1,0:T(8,128)(2,1)}), bf16[32,4,8,512]{3,2,1,0:T(8,128)(2,1)S(1)}, u32[]{:S(2)}, u32[]{:S(2)}) async-start(bf16[32,4,8,512]{3,2,1,0:T(8,128)(2,1)} %get-tuple-element.37), calls=%async_computation | async-start | bytes 2097152 | tf_op jit(solution)/shard_map/all_to_all | solution.py:219
  34.8 0.0 copy-start
  34.8 0.0 copy-start.2
  34.8 1.8 %copy.11 = bf16[192,8,2,256]{3,1,2,0:T(8,128)(2,1)S(1)} copy(bf16[192,8,2,256]{3,2,1,0:T(2,128)(2,1)} %bitcast.23) | data formatting | bytes 3145728
  36.6 0.0 collective-permute-done.low_first
  36.6 2.2 %collective-permute-start.4 = (bf16[192,1024]{1,0:T(8,128)(2,1)S(1)}, bf16[192,1024]{1,0:T(8,128)(2,1)S(1)}, u32[]{:S(2)}, u32[]{:S(2)}) collective-permute-start(bf16[192,1024]{1,0:T(8,128)(2,1)S(1)} %collective-permute-done.low_first), channel_id=1, source_target_pairs={{0,2},{2,4},{4,6},{6,0},{1,3},{3,5},{5,7},{7,1},{8,10},{10,12},{12... | collective-permute-start | bytes 1179656 | tf_op jit(solution)/shard_map/ppermute | solution.py:202
  38.8 0.0 collective-permute-done.3.high_second
  38.8 5.2 %collective-permute-start.5 = (bf16[192,1024]{1,0:T(8,128)(2,1)S(1)}, bf16[192,1024]{1,0:T(8,128)(2,1)S(1)}, u32[]{:S(2)}, u32[]{:S(2)}) collective-permute-start(bf16[192,1024]{1,0:T(8,128)(2,1)S(1)} %collective-permute-done.3.high_second), channel_id=1, source_target_pairs={{0,6},{2,0},{4,2},{6,4},{1,7},{3,1},{5,3},{7,5},{8,14},{10,8},{12,... | collective-permute-start | bytes 1179656 | tf_op jit(solution)/shard_map/ppermute | solution.py:203
  44.1 0.0 collective-permute-done.1.low_second
  44.1 3.5 %collective-permute-done.2.high_first = bf16[192,1024]{1,0:T(8,128)(2,1)S(1)} collective-permute-done((bf16[192,1024]{1,0:T(8,128)(2,1)S(1)}, bf16[192,1024]{1,0:T(8,128)(2,1)S(1)}, u32[]{:S(2)}, u32[]{:S(2)}) %collective-permute-start.2) | collective-permute-done | bytes 393248 | tf_op jit(solution)/shard_map/ppermute | solution.py:201
  47.6 0.0 copy-done
  47.6 0.0 copy-done.2
  47.6 2.4 %shard_map.101.total = f32[1024,512]{1,0:T(8,128)S(1)} custom-call(s32[3]{0:T(128)S(1)} %copy-done.2, bf16[384,1024]{1,0:T(8,128)(2,1)S(1)} %bitcast.22, bf16[192,1024]{1,0:T(8,128)(2,1)S(1)} %collective-permute-done.low_first, bf16[192,1024]{1,0:T(8,128)(2,1)S(1)} %collective-permute-done.1.low_second, ...), custom_call_target="tpu_custom_call" | custom-call | flops 9663676416 | bytes 6291456 | tf_op jit(solution)/shard_map/pallas_call | solution.py:221
  50.0 15.4 %collective-permute-done.4.far_first = bf16[192,1024]{1,0:T(8,128)(2,1)S(1)} collective-permute-done((bf16[192,1024]{1,0:T(8,128)(2,1)S(1)}, bf16[192,1024]{1,0:T(8,128)(2,1)S(1)}, u32[]{:S(2)}, u32[]{:S(2)}) %collective-permute-start.4) | collective-permute-done | bytes 393248 | tf_op jit(solution)/shard_map/ppermute | solution.py:202
  65.4 0.0 collective-permute-done.5.far_second
  65.4 1.3 shard_map.102
  66.7 4.1 %collective-permute-start.6 = (bf16[8,2,4,8,512]{4,3,2,1,0:T(8,128)(2,1)S(1)}, bf16[8,2,4,8,512]{4,3,2,1,0:T(8,128)(2,1)S(1)}, u32[]{:S(2)}, u32[]{:S(2)}) collective-permute-start(bf16[8,2,4,8,512]{4,3,2,1,0:T(8,128)(2,1)S(1)} %get-tuple-element.36), channel_id=1, source_target_pairs={{0,8},{8,0},{1,9},{9,1},{2,10},{10,2},{3,11},{11,3},{4,12},{12,4},... | collective-permute-start | bytes 1572872 | tf_op jit(solution)/shard_map/ppermute | solution.py:245
  70.8 1.5 collective-permute-done.6
  72.3 0.0 copy-start.10
  72.3 1.0 add_convert_fusion
  73.3 0.0 all-to-all-done.state
  73.3 11.7 %all-to-all-start.1 = ((bf16[64,8,512]{2,1,0:T(8,128)(2,1)}), bf16[64,8,512]{2,1,0:T(8,128)(2,1)S(1)}, u32[]{:S(2)}, u32[]{:S(2)}) async-start(bf16[64,8,512]{2,1,0:T(8,128)(2,1)} %bitcast.6), calls=%async_computation.1 | async-start | bytes 1048576 | tf_op jit(solution)/shard_map/all_to_all | solution.py:248
  85.0 0.0 copy-done.10
  85.0 5.2 %collective-permute-start.7 = (f32[3,4,256]{2,1,0:T(4,128)S(1)}, f32[3,4,256]{2,1,0:T(4,128)S(1)}, u32[]{:S(2)}, u32[]{:S(2)}) collective-permute-start(f32[3,4,256]{2,1,0:T(4,128)S(1)} %copy-done.10), channel_id=1, source_target_pairs={{0,2},{2,4},{4,6},{6,0},{1,3},{3,5},{5,7},{7,1},{8,10},{10,12},{12... | collective-permute-start | bytes 36872 | tf_op jit(solution)/shard_map/ppermute | solution.py:250
  90.2 0.0 copy-done.9
  90.2 3.1 %collective-permute-start.8 = (f32[3,4,256]{2,1,0:T(4,128)S(1)}, f32[3,4,256]{2,1,0:T(4,128)S(1)}, u32[]{:S(2)}, u32[]{:S(2)}) collective-permute-start(f32[3,4,256]{2,1,0:T(4,128)S(1)} %copy-done.9), channel_id=1, source_target_pairs={{0,4},{2,6},{4,0},{6,2},{1,5},{3,7},{5,1},{7,3},{8,12},{10,14},{12... | collective-permute-start | bytes 36872 | tf_op jit(solution)/shard_map/ppermute | solution.py:250
  93.3 0.0 collective-permute-done.7.refs_1_
  93.4 0.0 copy-start.5
  93.4 5.7 %collective-permute-done.8.refs_2_ = f32[3,4,256]{2,1,0:T(4,128)S(1)} collective-permute-done((f32[3,4,256]{2,1,0:T(4,128)S(1)}, f32[3,4,256]{2,1,0:T(4,128)S(1)}, u32[]{:S(2)}, u32[]{:S(2)}) %collective-permute-start.8) | collective-permute-done | bytes 12320 | tf_op jit(solution)/shard_map/ppermute | solution.py:250
  99.1 2.0 %all-to-all-done.1 = bf16[64,8,512]{2,1,0:T(8,128)(2,1)S(1)} async-done(((bf16[64,8,512]{2,1,0:T(8,128)(2,1)}), bf16[64,8,512]{2,1,0:T(8,128)(2,1)S(1)}, u32[]{:S(2)}, u32[]{:S(2)}) %all-to-all-start.1) | async-done | bytes 524320 | tf_op jit(solution)/shard_map/all_to_all | solution.py:248
  101.1 0.1 convert_reduce_fusion.lines
  101.2 0.0 copy-start.3
  101.3 0.7 broadcast_in_dim.6
  102.0 6.9 %all-to-all-start.2 = ((bf16[32,8,512]{2,1,0:T(8,128)(2,1)}), bf16[32,8,512]{2,1,0:T(8,128)(2,1)S(1)}, u32[]{:S(2)}, u32[]{:S(2)}) async-start(bf16[32,8,512]{2,1,0:T(8,128)(2,1)} %broadcast_in_dim.6), calls=%async_computation.2 | async-start | bytes 524288 | tf_op jit(solution)/shard_map/all_to_all | solution.py:256
  108.9 0.0 copy-done.8
  108.9 3.6 %collective-permute-start.9 = (f32[3,4,256]{2,1,0:T(4,128)S(1)}, f32[3,4,256]{2,1,0:T(4,128)S(1)}, u32[]{:S(2)}, u32[]{:S(2)}) collective-permute-start(f32[3,4,256]{2,1,0:T(4,128)S(1)} %copy-done.8), channel_id=1, source_target_pairs={{0,6},{2,0},{4,2},{6,4},{1,7},{3,1},{5,3},{7,5},{8,14},{10,8},{12,... | collective-permute-start | bytes 36872 | tf_op jit(solution)/shard_map/ppermute | solution.py:257
  112.5 0.1 pad.5.clone
  112.5 1.9 %collective-permute-done.9.refs_3_ = f32[3,4,256]{2,1,0:T(4,128)S(1)} collective-permute-done((f32[3,4,256]{2,1,0:T(4,128)S(1)}, f32[3,4,256]{2,1,0:T(4,128)S(1)}, u32[]{:S(2)}, u32[]{:S(2)}) %collective-permute-start.9) | collective-permute-done | bytes 12320 | tf_op jit(solution)/shard_map/ppermute | solution.py:257
  114.4 4.9 %all-to-all-done.2.shared = bf16[32,8,512]{2,1,0:T(8,128)(2,1)S(1)} async-done(((bf16[32,8,512]{2,1,0:T(8,128)(2,1)}), bf16[32,8,512]{2,1,0:T(8,128)(2,1)S(1)}, u32[]{:S(2)}, u32[]{:S(2)}) %all-to-all-start.2) | async-done | bytes 262176 | tf_op jit(solution)/shard_map/all_to_all | solution.py:256
  119.3 0.1 multiply_reduce_fusion
  119.4 0.1 maximum_convert_fusion
  119.5 16.3 %all_to_all.20.sums = bf16[16,8,256]{2,1,0:T(8,128)(2,1)S(1)} all-to-all(bf16[16,8,256]{2,1,0:T(8,128)(2,1)S(1)} %bitcast.24), channel_id=1, replica_groups=mesh['x'=4,'y'=8,'core'=2,'tensor'=4,'replica'=2] {'tensor','replica','c..., dimensions={0} | all-to-all | bytes 131072 | tf_op jit(solution)/shard_map/all_to_all | solution.py:271
  135.8 0.7 shard_map.104.mine
  136.5 0.0 copy-done.5
  136.5 0.0 copy-done.6
  136.5 2.1 %collective-permute-start.10 = (bf16[32,8,512]{2,1,0:T(8,128)(2,1)S(1)}, bf16[32,8,512]{2,1,0:T(8,128)(2,1)S(1)}, u32[]{:S(2)}, u32[]{:S(2)}) collective-permute-start(bf16[32,8,512]{2,1,0:T(8,128)(2,1)S(1)} %shard_map.104.mine), channel_id=1, source_target_pairs={{0,1},{1,0},{2,3},{3,2},{4,5},{5,4},{6,7},{7,6},{8,9},{9,8},{10,11... | collective-permute-start | bytes 786440 | tf_op jit(solution)/shard_map/ppermute | solution.py:283
  138.6 2.5 %collective-permute-start.11 = (bf16[32,8,512]{2,1,0:T(8,128)(2,1)S(1)}, bf16[32,8,512]{2,1,0:T(8,128)(2,1)S(1)}, u32[]{:S(2)}, u32[]{:S(2)}) collective-permute-start(bf16[32,8,512]{2,1,0:T(8,128)(2,1)S(1)} %shard_map.104.mine), channel_id=1, source_target_pairs={{0,8},{8,0},{1,9},{9,1},{2,10},{10,2},{3,11},{11,3},{4,12},{12,4},... | collective-permute-start | bytes 786440 | tf_op jit(solution)/shard_map/ppermute | solution.py:284
  141.1 0.0 copy-done.4
  141.1 0.0 copy-done.7
  141.1 0.0 copy-done.1
  141.1 1.7 %shard_map.105 = (f32[2,8,256]{2,1,0:T(8,128)}, f32[2,8,256]{2,1,0:T(8,128)}, f32[2,8,256]{2,1,0:T(8,128)}, f32[1,1,4,1024]{3,2,1,0:T(4,128)}) custom-call(s32[3]{0:T(128)} %pad_add_fusion.where, bf16[16,8,256]{2,1,0:T(8,128)(2,1)} %copy-done.1, f32[8,512]{1,0:T(8,128)} %copy-done.4, f32[2,8,256]{2,1,0:T(8,128)} %one.3, f32[2,8,256]{2,1,0:T(8,128)} %two.3, ...), custom_call_target="tpu_custom_call" | custom-call | tf_op jit(solution)/shard_map/pallas_call | solution.py:286
  142.8 3.3 %collective-permute-done.10.twin = bf16[32,8,512]{2,1,0:T(8,128)(2,1)S(1)} collective-permute-done((bf16[32,8,512]{2,1,0:T(8,128)(2,1)S(1)}, bf16[32,8,512]{2,1,0:T(8,128)(2,1)S(1)}, u32[]{:S(2)}, u32[]{:S(2)}) %collective-permute-start.10) | collective-permute-done | bytes 262176 | tf_op jit(solution)/shard_map/ppermute | solution.py:283
  146.1 2.9 %collective-permute-start.12 = (bf16[32,8,512]{2,1,0:T(8,128)(2,1)S(1)}, bf16[32,8,512]{2,1,0:T(8,128)(2,1)S(1)}, u32[]{:S(2)}, u32[]{:S(2)}) collective-permute-start(bf16[32,8,512]{2,1,0:T(8,128)(2,1)S(1)} %collective-permute-done.10.twin), channel_id=1, source_target_pairs={{0,8},{8,0},{1,9},{9,1},{2,10},{10,2},{3,11},{11,3},{4,12},{12,4},... | collective-permute-start | bytes 786440 | tf_op jit(solution)/shard_map/ppermute | solution.py:295
  149.0 0.0 collective-permute-done.11.other
  149.0 1.1 collective-permute-done.12.other_twin
  150.1 0.0 copy-done.3
  150.1 1.7 %shard_map.106 = bf16[2,1024,256]{2,1,0:T(8,128)(2,1)} custom-call(s32[3]{0:T(128)S(1)} %copy-done.3, bf16[32,8,512]{2,1,0:T(8,128)(2,1)S(1)} %shard_map.104.mine, bf16[32,8,512]{2,1,0:T(8,128)(2,1)S(1)} %collective-permute-done.10.twin, bf16[32,8,512]{2,1,0:T(8,128)(2,1)S(1)} %collective-permute-done.11.other, ...), custom_call_target="tpu_custom_call" | custom-call | tf_op jit(solution)/shard_map/pallas_call | solution.py:296
  (13 shorter events, 0.1 us)
Async XLA Ops:
  1.8 34.8 %collective-permute-start = (bf16[192,1024]{1,0:T(8,128)(2,1)S(1)}, bf16[192,1024]{1,0:T(8,128)(2,1)S(1)}, u32[]{:S(2)}, u32[]{:S(2)}) collective-permute-start(bf16[192,1024]{1,0:T(8,128)(2,1)S(1)} %get-tuple-element.66), channel_id=1, source_target_pairs={{0,2},{2,4},{4,6},{6,0},{1,3},{3,5},{5,7},{7,1},{8,10},{10,12},{12... | collective-permute-start | bytes 1179656 | tf_op jit(solution)/shard_map/ppermute | solution.py:198
  8.4 30.4 %collective-permute-start.3 = (bf16[192,1024]{1,0:T(8,128)(2,1)S(1)}, bf16[192,1024]{1,0:T(8,128)(2,1)S(1)}, u32[]{:S(2)}, u32[]{:S(2)}) collective-permute-start(bf16[192,1024]{1,0:T(8,128)(2,1)S(1)} %get-tuple-element.65), channel_id=1, source_target_pairs={{0,6},{2,0},{4,2},{6,4},{1,7},{3,1},{5,3},{7,5},{8,14},{10,8},{12,... | collective-permute-start | bytes 1179656 | tf_op jit(solution)/shard_map/ppermute | solution.py:199
  15.2 28.8 %collective-permute-start.1 = (bf16[192,1024]{1,0:T(8,128)(2,1)S(1)}, bf16[192,1024]{1,0:T(8,128)(2,1)S(1)}, u32[]{:S(2)}, u32[]{:S(2)}) collective-permute-start(bf16[192,1024]{1,0:T(8,128)(2,1)S(1)} %get-tuple-element.65), channel_id=1, source_target_pairs={{0,2},{2,4},{4,6},{6,0},{1,3},{3,5},{5,7},{7,1},{8,10},{10,12},{12... | collective-permute-start | bytes 1179656 | tf_op jit(solution)/shard_map/ppermute | solution.py:200
  17.4 30.2 %collective-permute-start.2 = (bf16[192,1024]{1,0:T(8,128)(2,1)S(1)}, bf16[192,1024]{1,0:T(8,128)(2,1)S(1)}, u32[]{:S(2)}, u32[]{:S(2)}) collective-permute-start(bf16[192,1024]{1,0:T(8,128)(2,1)S(1)} %get-tuple-element.66), channel_id=1, source_target_pairs={{0,6},{2,0},{4,2},{6,4},{1,7},{3,1},{5,3},{7,5},{8,14},{10,8},{12,... | collective-permute-start | bytes 1179656 | tf_op jit(solution)/shard_map/ppermute | solution.py:201
  25.1 48.2 %all-to-all-start = ((bf16[32,4,8,512]{3,2,1,0:T(8,128)(2,1)}), bf16[32,4,8,512]{3,2,1,0:T(8,128)(2,1)S(1)}, u32[]{:S(2)}, u32[]{:S(2)}) async-start(bf16[32,4,8,512]{3,2,1,0:T(8,128)(2,1)} %get-tuple-element.37), calls=%async_computation | async-start | bytes 2097152 | tf_op jit(solution)/shard_map/all_to_all | solution.py:219
  34.8 12.8 %copy-start = (bf16[1,384,1024]{2,1,0:T(8,128)(2,1)S(1)}, bf16[1,384,1024]{2,1,0:T(8,128)(2,1)}, u32[]{:S(2)}) copy-start(bf16[1,384,1024]{2,1,0:T(8,128)(2,1)} %param.6) | copy-start | bytes 2359300
  34.8 12.8 %copy-start.2 = (s32[3]{0:T(128)S(1)}, s32[3]{0:T(128)}, u32[]{:S(2)}) copy-start(s32[3]{0:T(128)} %pad_add_fusion.where) | copy-start | bytes 40
  36.6 28.7 %collective-permute-start.4 = (bf16[192,1024]{1,0:T(8,128)(2,1)S(1)}, bf16[192,1024]{1,0:T(8,128)(2,1)S(1)}, u32[]{:S(2)}, u32[]{:S(2)}) collective-permute-start(bf16[192,1024]{1,0:T(8,128)(2,1)S(1)} %collective-permute-done.low_first), channel_id=1, source_target_pairs={{0,2},{2,4},{4,6},{6,0},{1,3},{3,5},{5,7},{7,1},{8,10},{10,12},{12... | collective-permute-start | bytes 1179656 | tf_op jit(solution)/shard_map/ppermute | solution.py:202
  38.8 26.5 %collective-permute-start.5 = (bf16[192,1024]{1,0:T(8,128)(2,1)S(1)}, bf16[192,1024]{1,0:T(8,128)(2,1)S(1)}, u32[]{:S(2)}, u32[]{:S(2)}) collective-permute-start(bf16[192,1024]{1,0:T(8,128)(2,1)S(1)} %collective-permute-done.3.high_second), channel_id=1, source_target_pairs={{0,6},{2,0},{4,2},{6,4},{1,7},{3,1},{5,3},{7,5},{8,14},{10,8},{12,... | collective-permute-start | bytes 1179656 | tf_op jit(solution)/shard_map/ppermute | solution.py:203
  66.7 5.6 %collective-permute-start.6 = (bf16[8,2,4,8,512]{4,3,2,1,0:T(8,128)(2,1)S(1)}, bf16[8,2,4,8,512]{4,3,2,1,0:T(8,128)(2,1)S(1)}, u32[]{:S(2)}, u32[]{:S(2)}) collective-permute-start(bf16[8,2,4,8,512]{4,3,2,1,0:T(8,128)(2,1)S(1)} %get-tuple-element.36), channel_id=1, source_target_pairs={{0,8},{8,0},{1,9},{9,1},{2,10},{10,2},{3,11},{11,3},{4,12},{12,4},... | collective-permute-start | bytes 1572872 | tf_op jit(solution)/shard_map/ppermute | solution.py:245
  72.3 12.7 %copy-start.10 = (f32[3,4,256]{2,1,0:T(4,128)S(1)}, f32[3,4,256]{2,1,0:T(4,128)}, u32[]{:S(2)}) copy-start(f32[3,4,256]{2,1,0:T(4,128)} %get-tuple-element.44) | copy-start | bytes 36868
  72.3 17.9 %copy-start.9 = (f32[3,4,256]{2,1,0:T(4,128)S(1)}, f32[3,4,256]{2,1,0:T(4,128)}, u32[]{:S(2)}) copy-start(f32[3,4,256]{2,1,0:T(4,128)} %get-tuple-element.45) | copy-start | bytes 36868
  73.3 35.6 %copy-start.8 = (f32[3,4,256]{2,1,0:T(4,128)S(1)}, f32[3,4,256]{2,1,0:T(4,128)}, u32[]{:S(2)}) copy-start(f32[3,4,256]{2,1,0:T(4,128)} %get-tuple-element.51) | copy-start | bytes 36868
  73.3 27.8 %all-to-all-start.1 = ((bf16[64,8,512]{2,1,0:T(8,128)(2,1)}), bf16[64,8,512]{2,1,0:T(8,128)(2,1)S(1)}, u32[]{:S(2)}, u32[]{:S(2)}) async-start(bf16[64,8,512]{2,1,0:T(8,128)(2,1)} %bitcast.6), calls=%async_computation.1 | async-start | bytes 1048576 | tf_op jit(solution)/shard_map/all_to_all | solution.py:248
  85.0 8.3 %collective-permute-start.7 = (f32[3,4,256]{2,1,0:T(4,128)S(1)}, f32[3,4,256]{2,1,0:T(4,128)S(1)}, u32[]{:S(2)}, u32[]{:S(2)}) collective-permute-start(f32[3,4,256]{2,1,0:T(4,128)S(1)} %copy-done.10), channel_id=1, source_target_pairs={{0,2},{2,4},{4,6},{6,0},{1,3},{3,5},{5,7},{7,1},{8,10},{10,12},{12... | collective-permute-start | bytes 36872 | tf_op jit(solution)/shard_map/ppermute | solution.py:250
  90.2 8.9 %collective-permute-start.8 = (f32[3,4,256]{2,1,0:T(4,128)S(1)}, f32[3,4,256]{2,1,0:T(4,128)S(1)}, u32[]{:S(2)}, u32[]{:S(2)}) collective-permute-start(f32[3,4,256]{2,1,0:T(4,128)S(1)} %copy-done.9), channel_id=1, source_target_pairs={{0,4},{2,6},{4,0},{6,2},{1,5},{3,7},{5,1},{7,3},{8,12},{10,14},{12... | collective-permute-start | bytes 36872 | tf_op jit(solution)/shard_map/ppermute | solution.py:250
  93.4 43.1 %copy-start.5 = (f32[3,4,256]{2,1,0:T(4,128)}, f32[3,4,256]{2,1,0:T(4,128)S(1)}, u32[]{:S(2)}) copy-start(f32[3,4,256]{2,1,0:T(4,128)S(1)} %collective-permute-done.7.refs_1_) | copy-start | bytes 36868
  99.1 37.4 %copy-start.6 = (f32[3,4,256]{2,1,0:T(4,128)}, f32[3,4,256]{2,1,0:T(4,128)S(1)}, u32[]{:S(2)}) copy-start(f32[3,4,256]{2,1,0:T(4,128)S(1)} %collective-permute-done.8.refs_2_) | copy-start | bytes 36868
  101.2 39.8 %copy-start.4 = (f32[8,512]{1,0:T(8,128)}, f32[8,512]{1,0:T(8,128)S(1)}, u32[]{:S(2)}) copy-start(f32[8,512]{1,0:T(8,128)S(1)} %convert_reduce_fusion.lines) | copy-start | bytes 49156
  101.2 48.9 %copy-start.3 = (s32[3]{0:T(128)S(1)}, s32[3]{0:T(128)}, u32[]{:S(2)}) copy-start(s32[3]{0:T(128)} %pad_add_fusion.where) | copy-start | bytes 40
  102.0 17.3 %all-to-all-start.2 = ((bf16[32,8,512]{2,1,0:T(8,128)(2,1)}), bf16[32,8,512]{2,1,0:T(8,128)(2,1)S(1)}, u32[]{:S(2)}, u32[]{:S(2)}) async-start(bf16[32,8,512]{2,1,0:T(8,128)(2,1)} %broadcast_in_dim.6), calls=%async_computation.2 | async-start | bytes 524288 | tf_op jit(solution)/shard_map/all_to_all | solution.py:256
  108.9 5.5 %collective-permute-start.9 = (f32[3,4,256]{2,1,0:T(4,128)S(1)}, f32[3,4,256]{2,1,0:T(4,128)S(1)}, u32[]{:S(2)}, u32[]{:S(2)}) collective-permute-start(f32[3,4,256]{2,1,0:T(4,128)S(1)} %copy-done.8), channel_id=1, source_target_pairs={{0,6},{2,0},{4,2},{6,4},{1,7},{3,1},{5,3},{7,5},{8,14},{10,8},{12,... | collective-permute-start | bytes 36872 | tf_op jit(solution)/shard_map/ppermute | solution.py:257
  114.4 26.7 %copy-start.7 = (f32[3,4,256]{2,1,0:T(4,128)}, f32[3,4,256]{2,1,0:T(4,128)S(1)}, u32[]{:S(2)}) copy-start(f32[3,4,256]{2,1,0:T(4,128)S(1)} %collective-permute-done.9.refs_3_) | copy-start | bytes 36868
  135.8 5.3 %copy-start.1 = (bf16[16,8,256]{2,1,0:T(8,128)(2,1)}, bf16[16,8,256]{2,1,0:T(8,128)(2,1)S(1)}, u32[]{:S(2)}) copy-start(bf16[16,8,256]{2,1,0:T(8,128)(2,1)S(1)} %all_to_all.20.sums) | copy-start | bytes 196612
  136.5 9.6 %collective-permute-start.10 = (bf16[32,8,512]{2,1,0:T(8,128)(2,1)S(1)}, bf16[32,8,512]{2,1,0:T(8,128)(2,1)S(1)}, u32[]{:S(2)}, u32[]{:S(2)}) collective-permute-start(bf16[32,8,512]{2,1,0:T(8,128)(2,1)S(1)} %shard_map.104.mine), channel_id=1, source_target_pairs={{0,1},{1,0},{2,3},{3,2},{4,5},{5,4},{6,7},{7,6},{8,9},{9,8},{10,11... | collective-permute-start | bytes 786440 | tf_op jit(solution)/shard_map/ppermute | solution.py:283
  138.6 10.4 %collective-permute-start.11 = (bf16[32,8,512]{2,1,0:T(8,128)(2,1)S(1)}, bf16[32,8,512]{2,1,0:T(8,128)(2,1)S(1)}, u32[]{:S(2)}, u32[]{:S(2)}) collective-permute-start(bf16[32,8,512]{2,1,0:T(8,128)(2,1)S(1)} %shard_map.104.mine), channel_id=1, source_target_pairs={{0,8},{8,0},{1,9},{9,1},{2,10},{10,2},{3,11},{11,3},{4,12},{12,4},... | collective-permute-start | bytes 786440 | tf_op jit(solution)/shard_map/ppermute | solution.py:284
  146.1 4.0 %collective-permute-start.12 = (bf16[32,8,512]{2,1,0:T(8,128)(2,1)S(1)}, bf16[32,8,512]{2,1,0:T(8,128)(2,1)S(1)}, u32[]{:S(2)}, u32[]{:S(2)}) collective-permute-start(bf16[32,8,512]{2,1,0:T(8,128)(2,1)S(1)} %collective-permute-done.10.twin), channel_id=1, source_target_pairs={{0,8},{8,0},{1,9},{9,1},{2,10},{10,2},{3,11},{11,3},{4,12},{12,4},... | collective-permute-start | bytes 786440 | tf_op jit(solution)/shard_map/ppermute | solution.py:295

commit v9 on v6

--- a/solution.py
+++ b/solution.py
@@ -106,7 +106,8 @@
 
 
 def clip_of(sums, count):
-    total = jnp.sum(sums[:, sums.shape[1] - 1 :, :], axis=(0, 1), keepdims=True)[0]
+    parts = sums[...].astype(jnp.float32)[:, sums.shape[1] - 4 :, :]
+    total = jnp.sum(parts, axis=(0, 1), keepdims=True)[0]
     total = jnp.sum(total, axis=1, keepdims=True)
     return 1.0 / jnp.sqrt(total / count + 1e-06)
 
@@ -147,7 +148,8 @@
     for source in range(shards_all):
         step = lax.rem(where[0] + shards_all - source, shards_all)
         state = [pick(step, [ref[k] for ref in lent_state]) for k in range(3)]
-        grad = sums[(where[1] * shards_all + source) * 2 + where[2]][: state[0].shape[0]]
+        grad = sums[(where[1] * shards_all + source) * 2 + where[2]].astype(jnp.float32)
+        grad = grad[: state[0].shape[0]]
         columns = slice(source * width, (source + 1) * width)
         kept = average_keep * average[0, 0, :, columns]
         out[0, 0, :, columns] = kept + (1.0 - average_keep) * update(clip_factor, grad, *state)[2]
@@ -184,9 +186,6 @@
     core = lax.axis_index("core")
     place = lax.axis_index("tensor")
     where = jnp.stack([place, core, lax.axis_index("replica")]).astype(jnp.int32)
-    ring = lambda blocks: [blocks[0]] + [
-        lax.ppermute(blocks[k], "tensor", round_trip(nt, k)) for k in range(1, nt)
-    ]
 
     tokens = features[0]
     count, dim_model = tokens.shape
@@ -245,19 +244,26 @@
     half = (keep + got.astype(f32)).astype(bf16).reshape(peers, rows, width)
     half, state, lent_state = lax.optimization_barrier((half, state, lent_state))
     terms = lax.all_to_all(half, XYR, split_axis=0, concat_axis=0, tiled=True)
-    lent_state = ring(lent_state)
+    for step in range(1, nt - 1):
+        lent_state[step] = lax.ppermute(lent_state[step], "tensor", round_trip(nt, step))
     terms, lent_state = lax.optimization_barrier((terms, lent_state))
     grad_lines = jnp.sum(terms.astype(f32), axis=0)
 
     spread = grad_lines.astype(bf16)
     spread = jnp.broadcast_to(spread[None], (nx * ny,) + spread.shape)
     shared = lax.all_to_all(spread, PLANE, 0, 0, tiled=True)
+    lent_state[-1] = lax.ppermute(lent_state[-1], "tensor", round_trip(nt, nt - 1))
+    shared, lines_after, lent_state = lax.optimization_barrier((shared, grad_lines, lent_state))
     squares = shared.astype(f32)
     squares = jnp.sum(squares * squares, axis=(0, 1))
     squares = squares[:col_width] + squares[col_width:]
-    sums = jnp.transpose(grad_lines.reshape(rows, 2, col_width), (1, 0, 2))
+    high = lax.reduce_precision(squares, 8, 7)
+    middle = lax.reduce_precision(squares - high, 8, 7)
+    squares = jnp.stack([high, middle, squares - high - middle, jnp.zeros_like(squares)])
+    sums = jnp.transpose(lines_after.reshape(rows, 2, col_width), (1, 0, 2))
     sums = sums.reshape(nt, held_rows, col_width)
-    sums = jnp.concatenate([sums, jnp.broadcast_to(squares, sums.shape)], axis=1)
+    squares = jnp.broadcast_to(squares[None], (nt,) + squares.shape)
+    sums = jnp.concatenate([sums, squares], axis=1).astype(bf16)
     sums = jnp.broadcast_to(sums[None, :, None], (2, nt, nr) + sums.shape[1:])
     others = ("core", "tensor", "replica")
     sums = lax.all_to_all(

time: 153 us -> 151 us (0.987)
  starting transfers between devices: 85.4 us -> 81.7 us
  waiting for transfers between devices: 33.7 us -> 37 us
  blocking collectives: 16.8 us -> 15.2 us
    ppermute x3, waiting for transfers between devices: 0.79 us -> 7.98 us  [the longest x2 5.89 us: shards(): lax.ppermute(lent_state[step], 'tensor', round_trip(nt, step))]
    all_to_all x1, waiting for transfers between devices: 9.64 us -> 4.3 us  [shards(): shared = lax.all_to_all(spread, PLANE, 0, 0, tiled=True)]
    ppermute x3, starting transfers between devices: 13.5 us -> 11.5 us  [the longest x2 8.29 us: shards(): lax.ppermute(lent_state[step], 'tensor', round_trip(nt, step))]
    all_to_all x1, blocking collectives: 16.8 us -> 15.2 us  [shards(): lax.all_to_all(sums.reshape((2 * nt * nr,) + sums.shape[3:]), others, 0,...]
  transfers between devices with their start and end apart: 16 -> 16, of which waited for: 8 -> 9; matrix products, arithmetic and copies ran while one was open for 2% -> 2% of each run, Pallas kernels for 5% -> 5%
where the time goes in v9:
time: 151 us; the launch traced here: 150 us
  starting transfers between devices  81.7 us (54%)
  waiting for transfers between devices  37 us (25%)
  blocking collectives  15.2 us (10%)
  Pallas kernels  9.72 us (6%)
  local copies, waits for them, and re-layouts  3.85 us (3%)
  other arithmetic  1.87 us (1%)
    ppermute x1, waiting for transfers between devices, shards(): far_first = lax.ppermute(low_first, 'tensor', up)  15.4 us
    all_to_all x1, blocking collectives, shards(): lax.all_to_all(sums.reshape((2 * nt * nr,) + sums.shape[3:]), others, 0,...  15.2 us
    all_to_all x1, starting transfers between devices, shards(): terms = lax.all_to_all(half, XYR, split_axis=0, concat_axis=0, tiled=True)  11.7 us
    all_to_all x1, starting transfers between devices, shards(): state = lax.all_to_all(state, PLANE, 0, 0, tiled=True)  9.67 us
    ppermute x2, starting transfers between devices, shards(): lax.ppermute(lent_state[step], 'tensor', round_trip(nt, step))  8.29 us
    all_to_all x1, starting transfers between devices, shards(): shared = lax.all_to_all(spread, PLANE, 0, 0, tiled=True)  7.21 us
    ppermute x1, starting transfers between devices, shards(): high_second = lax.ppermute(second, 'tensor', down)  6.77 us
    ppermute x1, starting transfers between devices, shards(): low_first = lax.ppermute(first, 'tensor', up)  6.64 us
  transfers between devices with their start and end apart: 16, of which 9 were waited for; matrix products, arithmetic and copies ran while one was open for 2% of the time, Pallas kernels for 5%

profile of v9, /device:TPU:1, one launch (start us, length us, event | category | flops | bytes accessed | tf_op | source)
XLA Modules:
  0.0 150.3 jit_solution(759045165789436482)
XLA Ops:
  0.6 1.2 slice_bitcast_fusion
  1.8 6.6 %collective-permute-start = (bf16[192,1024]{1,0:T(8,128)(2,1)S(1)}, bf16[192,1024]{1,0:T(8,128)(2,1)S(1)}, u32[]{:S(2)}, u32[]{:S(2)}) collective-permute-start(bf16[192,1024]{1,0:T(8,128)(2,1)S(1)} %get-tuple-element.66), channel_id=1, source_target_pairs={{0,2},{2,4},{4,6},{6,0},{1,3},{3,5},{5,7},{7,1},{8,10},{10,12},{12... | collective-permute-start | bytes 1179656 | tf_op jit(solution)/shard_map/ppermute | solution.py:195
  8.4 6.8 %collective-permute-start.3 = (bf16[192,1024]{1,0:T(8,128)(2,1)S(1)}, bf16[192,1024]{1,0:T(8,128)(2,1)S(1)}, u32[]{:S(2)}, u32[]{:S(2)}) collective-permute-start(bf16[192,1024]{1,0:T(8,128)(2,1)S(1)} %get-tuple-element.65), channel_id=1, source_target_pairs={{0,6},{2,0},{4,2},{6,4},{1,7},{3,1},{5,3},{7,5},{8,14},{10,8},{12,... | collective-permute-start | bytes 1179656 | tf_op jit(solution)/shard_map/ppermute | solution.py:196
  15.2 2.2 %collective-permute-start.1 = (bf16[192,1024]{1,0:T(8,128)(2,1)S(1)}, bf16[192,1024]{1,0:T(8,128)(2,1)S(1)}, u32[]{:S(2)}, u32[]{:S(2)}) collective-permute-start(bf16[192,1024]{1,0:T(8,128)(2,1)S(1)} %get-tuple-element.65), channel_id=1, source_target_pairs={{0,2},{2,4},{4,6},{6,0},{1,3},{3,5},{5,7},{7,1},{8,10},{10,12},{12... | collective-permute-start | bytes 1179656 | tf_op jit(solution)/shard_map/ppermute | solution.py:197
  17.4 5.2 %collective-permute-start.2 = (bf16[192,1024]{1,0:T(8,128)(2,1)S(1)}, bf16[192,1024]{1,0:T(8,128)(2,1)S(1)}, u32[]{:S(2)}, u32[]{:S(2)}) collective-permute-start(bf16[192,1024]{1,0:T(8,128)(2,1)S(1)} %get-tuple-element.66), channel_id=1, source_target_pairs={{0,6},{2,0},{4,2},{6,4},{1,7},{3,1},{5,3},{7,5},{8,14},{10,8},{12,... | collective-permute-start | bytes 1179656 | tf_op jit(solution)/shard_map/ppermute | solution.py:198
  22.6 0.6 pad_add_fusion.where
  23.2 1.9 %shard_map.103 = (bf16[32,4,8,512]{3,2,1,0:T(8,128)(2,1)}, f32[3,4,256]{2,1,0:T(4,128)}, f32[3,4,256]{2,1,0:T(4,128)}, f32[3,4,256]{2,1,0:T(4,128)}, f32[3,4,256]{2,1,0:T(4,128)}) custom-call(s32[3]{0:T(128)} %pad_add_fusion.where, f32[2,8,256]{2,1,0:T(8,128)} %one.3, f32[2,8,256]{2,1,0:T(8,128)} %two.3, f32[2,8,256]{2,1,0:T(8,128)} %held.3), custom_call_target="tpu_custom_call" | custom-call | tf_op jit(solution)/shard_map/pallas_call | solution.py:209
  25.1 9.7 %all-to-all-start = ((bf16[32,4,8,512]{3,2,1,0:T(8,128)(2,1)}), bf16[32,4,8,512]{3,2,1,0:T(8,128)(2,1)S(1)}, u32[]{:S(2)}, u32[]{:S(2)}) async-start(bf16[32,4,8,512]{3,2,1,0:T(8,128)(2,1)} %get-tuple-element.37), calls=%async_computation | async-start | bytes 2097152 | tf_op jit(solution)/shard_map/all_to_all | solution.py:216
  34.8 0.0 copy-start
  34.8 0.0 copy-start.2
  34.8 1.8 %copy.11 = bf16[192,8,2,256]{3,1,2,0:T(8,128)(2,1)S(1)} copy(bf16[192,8,2,256]{3,2,1,0:T(2,128)(2,1)} %bitcast.23) | data formatting | bytes 3145728
  36.6 0.0 collective-permute-done.low_first
  36.6 2.2 %collective-permute-start.4 = (bf16[192,1024]{1,0:T(8,128)(2,1)S(1)}, bf16[192,1024]{1,0:T(8,128)(2,1)S(1)}, u32[]{:S(2)}, u32[]{:S(2)}) collective-permute-start(bf16[192,1024]{1,0:T(8,128)(2,1)S(1)} %collective-permute-done.low_first), channel_id=1, source_target_pairs={{0,2},{2,4},{4,6},{6,0},{1,3},{3,5},{5,7},{7,1},{8,10},{10,12},{12... | collective-permute-start | bytes 1179656 | tf_op jit(solution)/shard_map/ppermute | solution.py:199
  38.8 0.0 collective-permute-done.3.high_second
  38.8 5.2 %collective-permute-start.5 = (bf16[192,1024]{1,0:T(8,128)(2,1)S(1)}, bf16[192,1024]{1,0:T(8,128)(2,1)S(1)}, u32[]{:S(2)}, u32[]{:S(2)}) collective-permute-start(bf16[192,1024]{1,0:T(8,128)(2,1)S(1)} %collective-permute-done.3.high_second), channel_id=1, source_target_pairs={{0,6},{2,0},{4,2},{6,4},{1,7},{3,1},{5,3},{7,5},{8,14},{10,8},{12,... | collective-permute-start | bytes 1179656 | tf_op jit(solution)/shard_map/ppermute | solution.py:200
  44.1 0.0 collective-permute-done.1.low_second
  44.1 3.5 %collective-permute-done.2.high_first = bf16[192,1024]{1,0:T(8,128)(2,1)S(1)} collective-permute-done((bf16[192,1024]{1,0:T(8,128)(2,1)S(1)}, bf16[192,1024]{1,0:T(8,128)(2,1)S(1)}, u32[]{:S(2)}, u32[]{:S(2)}) %collective-permute-start.2) | collective-permute-done | bytes 393248 | tf_op jit(solution)/shard_map/ppermute | solution.py:198
  47.6 0.0 copy-done
  47.6 0.0 copy-done.2
  47.6 2.4 %shard_map.101.total = f32[1024,512]{1,0:T(8,128)S(1)} custom-call(s32[3]{0:T(128)S(1)} %copy-done.2, bf16[384,1024]{1,0:T(8,128)(2,1)S(1)} %bitcast.22, bf16[192,1024]{1,0:T(8,128)(2,1)S(1)} %collective-permute-done.low_first, bf16[192,1024]{1,0:T(8,128)(2,1)S(1)} %collective-permute-done.1.low_second, ...), custom_call_target="tpu_custom_call" | custom-call | flops 9663676416 | bytes 6291456 | tf_op jit(solution)/shard_map/pallas_call | solution.py:219
  50.0 15.4 %collective-permute-done.4.far_first = bf16[192,1024]{1,0:T(8,128)(2,1)S(1)} collective-permute-done((bf16[192,1024]{1,0:T(8,128)(2,1)S(1)}, bf16[192,1024]{1,0:T(8,128)(2,1)S(1)}, u32[]{:S(2)}, u32[]{:S(2)}) %collective-permute-start.4) | collective-permute-done | bytes 393248 | tf_op jit(solution)/shard_map/ppermute | solution.py:199
  65.4 0.0 collective-permute-done.5.far_second
  65.4 1.3 shard_map.102
  66.7 4.1 %collective-permute-start.6 = (bf16[32,16,512]{2,1,0:T(8,128)(2,1)S(1)}, bf16[32,16,512]{2,1,0:T(8,128)(2,1)S(1)}, u32[]{:S(2)}, u32[]{:S(2)}) collective-permute-start(bf16[32,16,512]{2,1,0:T(8,128)(2,1)S(1)} %get-tuple-element.36), channel_id=1, source_target_pairs={{0,8},{8,0},{1,9},{9,1},{2,10},{10,2},{3,11},{11,3},{4,12},{12,4},... | collective-permute-start | bytes 1572872 | tf_op jit(solution)/shard_map/ppermute | solution.py:243
  70.8 1.5 %collective-permute-done.6 = bf16[32,16,512]{2,1,0:T(8,128)(2,1)S(1)} collective-permute-done((bf16[32,16,512]{2,1,0:T(8,128)(2,1)S(1)}, bf16[32,16,512]{2,1,0:T(8,128)(2,1)S(1)}, u32[]{:S(2)}, u32[]{:S(2)}) %collective-permute-start.6) | collective-permute-done | bytes 524320 | tf_op jit(solution)/shard_map/ppermute | solution.py:243
  72.3 0.0 copy-start.10
  72.3 1.0 add_convert_fusion
  73.3 0.0 all-to-all-done.state
  73.3 11.7 %all-to-all-start.1 = ((bf16[64,8,512]{2,1,0:T(8,128)(2,1)}), bf16[64,8,512]{2,1,0:T(8,128)(2,1)S(1)}, u32[]{:S(2)}, u32[]{:S(2)}) async-start(bf16[64,8,512]{2,1,0:T(8,128)(2,1)} %bitcast.6), calls=%async_computation.1 | async-start | bytes 1048576 | tf_op jit(solution)/shard_map/all_to_all | solution.py:246
  85.0 0.0 copy-done.10
  85.0 5.2 %collective-permute-start.7 = (f32[3,4,256]{2,1,0:T(4,128)S(1)}, f32[3,4,256]{2,1,0:T(4,128)S(1)}, u32[]{:S(2)}, u32[]{:S(2)}) collective-permute-start(f32[3,4,256]{2,1,0:T(4,128)S(1)} %copy-done.10), channel_id=1, source_target_pairs={{0,2},{2,4},{4,6},{6,0},{1,3},{3,5},{5,7},{7,1},{8,10},{10,12},{12... | collective-permute-start | bytes 36872 | tf_op jit(solution)/shard_map/ppermute | solution.py:248
  90.2 0.0 copy-done.9
  90.2 3.1 %collective-permute-start.8 = (f32[3,4,256]{2,1,0:T(4,128)S(1)}, f32[3,4,256]{2,1,0:T(4,128)S(1)}, u32[]{:S(2)}, u32[]{:S(2)}) collective-permute-start(f32[3,4,256]{2,1,0:T(4,128)S(1)} %copy-done.9), channel_id=1, source_target_pairs={{0,4},{2,6},{4,0},{6,2},{1,5},{3,7},{5,1},{7,3},{8,12},{10,14},{12... | collective-permute-start | bytes 36872 | tf_op jit(solution)/shard_map/ppermute | solution.py:248
  93.4 0.0 collective-permute-done.7.refs_1_
  93.4 0.0 copy-start.5
  93.4 5.9 %collective-permute-done.8.refs_2_ = f32[3,4,256]{2,1,0:T(4,128)S(1)} collective-permute-done((f32[3,4,256]{2,1,0:T(4,128)S(1)}, f32[3,4,256]{2,1,0:T(4,128)S(1)}, u32[]{:S(2)}, u32[]{:S(2)}) %collective-permute-start.8) | collective-permute-done | bytes 12320 | tf_op jit(solution)/shard_map/ppermute | solution.py:248
  99.3 1.7 %all-to-all-done.1 = bf16[64,8,512]{2,1,0:T(8,128)(2,1)S(1)} async-done(((bf16[64,8,512]{2,1,0:T(8,128)(2,1)}), bf16[64,8,512]{2,1,0:T(8,128)(2,1)S(1)}, u32[]{:S(2)}, u32[]{:S(2)}) %all-to-all-start.1) | async-done | bytes 524320 | tf_op jit(solution)/shard_map/all_to_all | solution.py:246
  101.0 0.1 convert_reduce_fusion.lines
  101.1 0.0 copy-start.3
  101.1 0.7 broadcast_in_dim.6
  101.8 7.2 %all-to-all-start.2 = ((bf16[32,8,512]{2,1,0:T(8,128)(2,1)}), bf16[32,8,512]{2,1,0:T(8,128)(2,1)S(1)}, u32[]{:S(2)}, u32[]{:S(2)}) async-start(bf16[32,8,512]{2,1,0:T(8,128)(2,1)} %broadcast_in_dim.6), calls=%async_computation.2 | async-start | bytes 524288 | tf_op jit(solution)/shard_map/all_to_all | solution.py:254
  109.1 0.0 copy-done.8
  109.1 3.2 %collective-permute-start.9 = (f32[3,4,256]{2,1,0:T(4,128)S(1)}, f32[3,4,256]{2,1,0:T(4,128)S(1)}, u32[]{:S(2)}, u32[]{:S(2)}) collective-permute-start(f32[3,4,256]{2,1,0:T(4,128)S(1)} %copy-done.8), channel_id=1, source_target_pairs={{0,6},{2,0},{4,2},{6,4},{1,7},{3,1},{5,3},{7,5},{8,14},{10,8},{12,... | collective-permute-start | bytes 36872 | tf_op jit(solution)/shard_map/ppermute | solution.py:255
  112.2 0.1 pad.5.clone
  112.3 2.1 %collective-permute-done.9.refs_3_ = f32[3,4,256]{2,1,0:T(4,128)S(1)} collective-permute-done((f32[3,4,256]{2,1,0:T(4,128)S(1)}, f32[3,4,256]{2,1,0:T(4,128)S(1)}, u32[]{:S(2)}, u32[]{:S(2)}) %collective-permute-start.9) | collective-permute-done | bytes 12320 | tf_op jit(solution)/shard_map/ppermute | solution.py:255
  114.4 4.3 %all-to-all-done.2.shared = bf16[32,8,512]{2,1,0:T(8,128)(2,1)S(1)} async-done(((bf16[32,8,512]{2,1,0:T(8,128)(2,1)}), bf16[32,8,512]{2,1,0:T(8,128)(2,1)S(1)}, u32[]{:S(2)}, u32[]{:S(2)}) %all-to-all-start.2) | async-done | bytes 262176 | tf_op jit(solution)/shard_map/all_to_all | solution.py:254
  118.7 0.1 multiply_reduce_fusion
  118.8 0.1 maximum_convert_fusion
  118.9 15.2 %all_to_all.20.sums = bf16[16,8,256]{2,1,0:T(8,128)(2,1)S(1)} all-to-all(bf16[16,8,256]{2,1,0:T(8,128)(2,1)S(1)} %bitcast.24), channel_id=1, replica_groups=mesh['x'=4,'y'=8,'core'=2,'tensor'=4,'replica'=2] {'core','tensor','repl..., dimensions={0} | all-to-all | bytes 131072 | tf_op jit(solution)/shard_map/all_to_all | solution.py:269
  134.2 0.7 shard_map.104.mine
  134.9 0.0 copy-done.5
  134.9 0.0 copy-done.6
  134.9 2.8 %collective-permute-start.10 = (bf16[32,8,512]{2,1,0:T(8,128)(2,1)S(1)}, bf16[32,8,512]{2,1,0:T(8,128)(2,1)S(1)}, u32[]{:S(2)}, u32[]{:S(2)}) collective-permute-start(bf16[32,8,512]{2,1,0:T(8,128)(2,1)S(1)} %shard_map.104.mine), channel_id=1, source_target_pairs={{0,1},{1,0},{2,3},{3,2},{4,5},{5,4},{6,7},{7,6},{8,9},{9,8},{10,11... | collective-permute-start | bytes 786440 | tf_op jit(solution)/shard_map/ppermute | solution.py:281
  137.7 2.9 %collective-permute-start.11 = (bf16[32,8,512]{2,1,0:T(8,128)(2,1)S(1)}, bf16[32,8,512]{2,1,0:T(8,128)(2,1)S(1)}, u32[]{:S(2)}, u32[]{:S(2)}) collective-permute-start(bf16[32,8,512]{2,1,0:T(8,128)(2,1)S(1)} %shard_map.104.mine), channel_id=1, source_target_pairs={{0,8},{8,0},{1,9},{9,1},{2,10},{10,2},{3,11},{11,3},{4,12},{12,4},... | collective-permute-start | bytes 786440 | tf_op jit(solution)/shard_map/ppermute | solution.py:282
  140.6 0.0 copy-done.4
  140.6 0.0 copy-done.7
  140.6 0.0 copy-done.1
  140.6 1.7 %shard_map.105 = (f32[2,8,256]{2,1,0:T(8,128)}, f32[2,8,256]{2,1,0:T(8,128)}, f32[2,8,256]{2,1,0:T(8,128)}, f32[1,1,4,1024]{3,2,1,0:T(4,128)}) custom-call(s32[3]{0:T(128)} %pad_add_fusion.where, bf16[16,8,256]{2,1,0:T(8,128)(2,1)} %copy-done.1, f32[8,512]{1,0:T(8,128)} %copy-done.4, f32[2,8,256]{2,1,0:T(8,128)} %one.3, f32[2,8,256]{2,1,0:T(8,128)} %two.3, ...), custom_call_target="tpu_custom_call" | custom-call | tf_op jit(solution)/shard_map/pallas_call | solution.py:284
  142.3 1.4 collective-permute-done.10.twin
  143.7 3.7 %collective-permute-start.12 = (bf16[32,8,512]{2,1,0:T(8,128)(2,1)S(1)}, bf16[32,8,512]{2,1,0:T(8,128)(2,1)S(1)}, u32[]{:S(2)}, u32[]{:S(2)}) collective-permute-start(bf16[32,8,512]{2,1,0:T(8,128)(2,1)S(1)} %collective-permute-done.10.twin), channel_id=1, source_target_pairs={{0,8},{8,0},{1,9},{9,1},{2,10},{10,2},{3,11},{11,3},{4,12},{12,4},... | collective-permute-start | bytes 786440 | tf_op jit(solution)/shard_map/ppermute | solution.py:293
  147.4 0.0 collective-permute-done.11.other
  147.4 1.1 collective-permute-done.12.other_twin
  148.6 0.0 copy-done.3
  148.6 1.7 %shard_map.106 = bf16[2,1024,256]{2,1,0:T(8,128)(2,1)} custom-call(s32[3]{0:T(128)S(1)} %copy-done.3, bf16[32,8,512]{2,1,0:T(8,128)(2,1)S(1)} %shard_map.104.mine, bf16[32,8,512]{2,1,0:T(8,128)(2,1)S(1)} %collective-permute-done.10.twin, bf16[32,8,512]{2,1,0:T(8,128)(2,1)S(1)} %collective-permute-done.11.other, ...), custom_call_target="tpu_custom_call" | custom-call | tf_op jit(solution)/shard_map/pallas_call | solution.py:294
  (13 shorter events, 0.1 us)
Async XLA Ops:
  1.8 34.8 %collective-permute-start = (bf16[192,1024]{1,0:T(8,128)(2,1)S(1)}, bf16[192,1024]{1,0:T(8,128)(2,1)S(1)}, u32[]{:S(2)}, u32[]{:S(2)}) collective-permute-start(bf16[192,1024]{1,0:T(8,128)(2,1)S(1)} %get-tuple-element.66), channel_id=1, source_target_pairs={{0,2},{2,4},{4,6},{6,0},{1,3},{3,5},{5,7},{7,1},{8,10},{10,12},{12... | collective-permute-start | bytes 1179656 | tf_op jit(solution)/shard_map/ppermute | solution.py:195
  8.4 30.4 %collective-permute-start.3 = (bf16[192,1024]{1,0:T(8,128)(2,1)S(1)}, bf16[192,1024]{1,0:T(8,128)(2,1)S(1)}, u32[]{:S(2)}, u32[]{:S(2)}) collective-permute-start(bf16[192,1024]{1,0:T(8,128)(2,1)S(1)} %get-tuple-element.65), channel_id=1, source_target_pairs={{0,6},{2,0},{4,2},{6,4},{1,7},{3,1},{5,3},{7,5},{8,14},{10,8},{12,... | collective-permute-start | bytes 1179656 | tf_op jit(solution)/shard_map/ppermute | solution.py:196
  15.2 28.8 %collective-permute-start.1 = (bf16[192,1024]{1,0:T(8,128)(2,1)S(1)}, bf16[192,1024]{1,0:T(8,128)(2,1)S(1)}, u32[]{:S(2)}, u32[]{:S(2)}) collective-permute-start(bf16[192,1024]{1,0:T(8,128)(2,1)S(1)} %get-tuple-element.65), channel_id=1, source_target_pairs={{0,2},{2,4},{4,6},{6,0},{1,3},{3,5},{5,7},{7,1},{8,10},{10,12},{12... | collective-permute-start | bytes 1179656 | tf_op jit(solution)/shard_map/ppermute | solution.py:197
  17.4 30.2 %collective-permute-start.2 = (bf16[192,1024]{1,0:T(8,128)(2,1)S(1)}, bf16[192,1024]{1,0:T(8,128)(2,1)S(1)}, u32[]{:S(2)}, u32[]{:S(2)}) collective-permute-start(bf16[192,1024]{1,0:T(8,128)(2,1)S(1)} %get-tuple-element.66), channel_id=1, source_target_pairs={{0,6},{2,0},{4,2},{6,4},{1,7},{3,1},{5,3},{7,5},{8,14},{10,8},{12,... | collective-permute-start | bytes 1179656 | tf_op jit(solution)/shard_map/ppermute | solution.py:198
  25.1 48.2 %all-to-all-start = ((bf16[32,4,8,512]{3,2,1,0:T(8,128)(2,1)}), bf16[32,4,8,512]{3,2,1,0:T(8,128)(2,1)S(1)}, u32[]{:S(2)}, u32[]{:S(2)}) async-start(bf16[32,4,8,512]{3,2,1,0:T(8,128)(2,1)} %get-tuple-element.37), calls=%async_computation | async-start | bytes 2097152 | tf_op jit(solution)/shard_map/all_to_all | solution.py:216
  34.8 12.8 %copy-start = (bf16[1,384,1024]{2,1,0:T(8,128)(2,1)S(1)}, bf16[1,384,1024]{2,1,0:T(8,128)(2,1)}, u32[]{:S(2)}) copy-start(bf16[1,384,1024]{2,1,0:T(8,128)(2,1)} %param.6) | copy-start | bytes 2359300
  34.8 12.8 %copy-start.2 = (s32[3]{0:T(128)S(1)}, s32[3]{0:T(128)}, u32[]{:S(2)}) copy-start(s32[3]{0:T(128)} %pad_add_fusion.where) | copy-start | bytes 40
  36.6 28.7 %collective-permute-start.4 = (bf16[192,1024]{1,0:T(8,128)(2,1)S(1)}, bf16[192,1024]{1,0:T(8,128)(2,1)S(1)}, u32[]{:S(2)}, u32[]{:S(2)}) collective-permute-start(bf16[192,1024]{1,0:T(8,128)(2,1)S(1)} %collective-permute-done.low_first), channel_id=1, source_target_pairs={{0,2},{2,4},{4,6},{6,0},{1,3},{3,5},{5,7},{7,1},{8,10},{10,12},{12... | collective-permute-start | bytes 1179656 | tf_op jit(solution)/shard_map/ppermute | solution.py:199
  38.8 26.5 %collective-permute-start.5 = (bf16[192,1024]{1,0:T(8,128)(2,1)S(1)}, bf16[192,1024]{1,0:T(8,128)(2,1)S(1)}, u32[]{:S(2)}, u32[]{:S(2)}) collective-permute-start(bf16[192,1024]{1,0:T(8,128)(2,1)S(1)} %collective-permute-done.3.high_second), channel_id=1, source_target_pairs={{0,6},{2,0},{4,2},{6,4},{1,7},{3,1},{5,3},{7,5},{8,14},{10,8},{12,... | collective-permute-start | bytes 1179656 | tf_op jit(solution)/shard_map/ppermute | solution.py:200
  66.7 5.6 %collective-permute-start.6 = (bf16[32,16,512]{2,1,0:T(8,128)(2,1)S(1)}, bf16[32,16,512]{2,1,0:T(8,128)(2,1)S(1)}, u32[]{:S(2)}, u32[]{:S(2)}) collective-permute-start(bf16[32,16,512]{2,1,0:T(8,128)(2,1)S(1)} %get-tuple-element.36), channel_id=1, source_target_pairs={{0,8},{8,0},{1,9},{9,1},{2,10},{10,2},{3,11},{11,3},{4,12},{12,4},... | collective-permute-start | bytes 1572872 | tf_op jit(solution)/shard_map/ppermute | solution.py:243
  72.3 12.7 %copy-start.10 = (f32[3,4,256]{2,1,0:T(4,128)S(1)}, f32[3,4,256]{2,1,0:T(4,128)}, u32[]{:S(2)}) copy-start(f32[3,4,256]{2,1,0:T(4,128)} %get-tuple-element.44) | copy-start | bytes 36868
  72.3 17.9 %copy-start.9 = (f32[3,4,256]{2,1,0:T(4,128)S(1)}, f32[3,4,256]{2,1,0:T(4,128)}, u32[]{:S(2)}) copy-start(f32[3,4,256]{2,1,0:T(4,128)} %get-tuple-element.45) | copy-start | bytes 36868
  73.3 35.7 %copy-start.8 = (f32[3,4,256]{2,1,0:T(4,128)S(1)}, f32[3,4,256]{2,1,0:T(4,128)}, u32[]{:S(2)}) copy-start(f32[3,4,256]{2,1,0:T(4,128)} %get-tuple-element.51) | copy-start | bytes 36868
  73.3 27.7 %all-to-all-start.1 = ((bf16[64,8,512]{2,1,0:T(8,128)(2,1)}), bf16[64,8,512]{2,1,0:T(8,128)(2,1)S(1)}, u32[]{:S(2)}, u32[]{:S(2)}) async-start(bf16[64,8,512]{2,1,0:T(8,128)(2,1)} %bitcast.6), calls=%async_computation.1 | async-start | bytes 1048576 | tf_op jit(solution)/shard_map/all_to_all | solution.py:246
  85.0 8.3 %collective-permute-start.7 = (f32[3,4,256]{2,1,0:T(4,128)S(1)}, f32[3,4,256]{2,1,0:T(4,128)S(1)}, u32[]{:S(2)}, u32[]{:S(2)}) collective-permute-start(f32[3,4,256]{2,1,0:T(4,128)S(1)} %copy-done.10), channel_id=1, source_target_pairs={{0,2},{2,4},{4,6},{6,0},{1,3},{3,5},{5,7},{7,1},{8,10},{10,12},{12... | collective-permute-start | bytes 36872 | tf_op jit(solution)/shard_map/ppermute | solution.py:248
  90.2 9.0 %collective-permute-start.8 = (f32[3,4,256]{2,1,0:T(4,128)S(1)}, f32[3,4,256]{2,1,0:T(4,128)S(1)}, u32[]{:S(2)}, u32[]{:S(2)}) collective-permute-start(f32[3,4,256]{2,1,0:T(4,128)S(1)} %copy-done.9), channel_id=1, source_target_pairs={{0,4},{2,6},{4,0},{6,2},{1,5},{3,7},{5,1},{7,3},{8,12},{10,14},{12... | collective-permute-start | bytes 36872 | tf_op jit(solution)/shard_map/ppermute | solution.py:248
  93.4 41.5 %copy-start.5 = (f32[3,4,256]{2,1,0:T(4,128)}, f32[3,4,256]{2,1,0:T(4,128)S(1)}, u32[]{:S(2)}) copy-start(f32[3,4,256]{2,1,0:T(4,128)S(1)} %collective-permute-done.7.refs_1_) | copy-start | bytes 36868
  99.3 35.6 %copy-start.6 = (f32[3,4,256]{2,1,0:T(4,128)}, f32[3,4,256]{2,1,0:T(4,128)S(1)}, u32[]{:S(2)}) copy-start(f32[3,4,256]{2,1,0:T(4,128)S(1)} %collective-permute-done.8.refs_2_) | copy-start | bytes 36868
  101.1 39.5 %copy-start.4 = (f32[8,512]{1,0:T(8,128)}, f32[8,512]{1,0:T(8,128)S(1)}, u32[]{:S(2)}) copy-start(f32[8,512]{1,0:T(8,128)S(1)} %convert_reduce_fusion.lines) | copy-start | bytes 49156
  101.1 47.5 %copy-start.3 = (s32[3]{0:T(128)S(1)}, s32[3]{0:T(128)}, u32[]{:S(2)}) copy-start(s32[3]{0:T(128)} %pad_add_fusion.where) | copy-start | bytes 40
  101.8 16.9 %all-to-all-start.2 = ((bf16[32,8,512]{2,1,0:T(8,128)(2,1)}), bf16[32,8,512]{2,1,0:T(8,128)(2,1)S(1)}, u32[]{:S(2)}, u32[]{:S(2)}) async-start(bf16[32,8,512]{2,1,0:T(8,128)(2,1)} %broadcast_in_dim.6), calls=%async_computation.2 | async-start | bytes 524288 | tf_op jit(solution)/shard_map/all_to_all | solution.py:254
  109.1 5.3 %collective-permute-start.9 = (f32[3,4,256]{2,1,0:T(4,128)S(1)}, f32[3,4,256]{2,1,0:T(4,128)S(1)}, u32[]{:S(2)}, u32[]{:S(2)}) collective-permute-start(f32[3,4,256]{2,1,0:T(4,128)S(1)} %copy-done.8), channel_id=1, source_target_pairs={{0,6},{2,0},{4,2},{6,4},{1,7},{3,1},{5,3},{7,5},{8,14},{10,8},{12,... | collective-permute-start | bytes 36872 | tf_op jit(solution)/shard_map/ppermute | solution.py:255
  114.4 26.2 %copy-start.7 = (f32[3,4,256]{2,1,0:T(4,128)}, f32[3,4,256]{2,1,0:T(4,128)S(1)}, u32[]{:S(2)}) copy-start(f32[3,4,256]{2,1,0:T(4,128)S(1)} %collective-permute-done.9.refs_3_) | copy-start | bytes 36868
  134.2 6.4 %copy-start.1 = (bf16[16,8,256]{2,1,0:T(8,128)(2,1)}, bf16[16,8,256]{2,1,0:T(8,128)(2,1)S(1)}, u32[]{:S(2)}) copy-start(bf16[16,8,256]{2,1,0:T(8,128)(2,1)S(1)} %all_to_all.20.sums) | copy-start | bytes 196612
  134.9 8.8 %collective-permute-start.10 = (bf16[32,8,512]{2,1,0:T(8,128)(2,1)S(1)}, bf16[32,8,512]{2,1,0:T(8,128)(2,1)S(1)}, u32[]{:S(2)}, u32[]{:S(2)}) collective-permute-start(bf16[32,8,512]{2,1,0:T(8,128)(2,1)S(1)} %shard_map.104.mine), channel_id=1, source_target_pairs={{0,1},{1,0},{2,3},{3,2},{4,5},{5,4},{6,7},{7,6},{8,9},{9,8},{10,11... | collective-permute-start | bytes 786440 | tf_op jit(solution)/shard_map/ppermute | solution.py:281
  137.7 9.8 %collective-permute-start.11 = (bf16[32,8,512]{2,1,0:T(8,128)(2,1)S(1)}, bf16[32,8,512]{2,1,0:T(8,128)(2,1)S(1)}, u32[]{:S(2)}, u32[]{:S(2)}) collective-permute-start(bf16[32,8,512]{2,1,0:T(8,128)(2,1)S(1)} %shard_map.104.mine), channel_id=1, source_target_pairs={{0,8},{8,0},{1,9},{9,1},{2,10},{10,2},{3,11},{11,3},{4,12},{12,4},... | collective-permute-start | bytes 786440 | tf_op jit(solution)/shard_map/ppermute | solution.py:282
  143.7 4.8 %collective-permute-start.12 = (bf16[32,8,512]{2,1,0:T(8,128)(2,1)S(1)}, bf16[32,8,512]{2,1,0:T(8,128)(2,1)S(1)}, u32[]{:S(2)}, u32[]{:S(2)}) collective-permute-start(bf16[32,8,512]{2,1,0:T(8,128)(2,1)S(1)} %collective-permute-done.10.twin), channel_id=1, source_target_pairs={{0,8},{8,0},{1,9},{9,1},{2,10},{10,2},{3,11},{11,3},{4,12},{12,4},... | collective-permute-start | bytes 786440 | tf_op jit(solution)/shard_map/ppermute | solution.py:293
